TPU v7x, 32 devices: a whole 2x2x4 slice. The times are simulated.
32 devices in a mesh: seq: 4 (over x, core), exp: 8 (over z, y).
Axes of the slice: x: 2, y: 2, z: 4, core: 2. Of those that a mesh axis runs over, the one named last changes fastest.
Arguments:
- query_rows: bfloat16 [8, 768, 4096], P('exp', 'seq'), may hold values from -6 to 6
- key_rows: bfloat16 [8, 768, 512], P('exp', 'seq'), may hold values from -6 to 6
- value_matrix: bfloat16 [8, 768, 512], P('exp', 'seq'), may hold values from -6 to 6
- doc_ids: int32 [8, 768], P('exp'), may hold values from 0 to 7, as said below
- out_weight: bfloat16 [4096, 2048], P(('seq', 'exp')), may hold values from -0.375 to 0.375
- enc_weight: bfloat16 [32, 2048, 1024], P(('seq', 'exp')), may hold values from -0.125 to 0.125
- enc_bias: float32 [32, 1024], P(('seq', 'exp')), may hold values from -3 to 3
- dec_weight: bfloat16 [32, 1024, 2048], P(('seq', 'exp')), may hold values from -0.1875 to 0.1875
- dec_bias: float32 [2048], replicated, may hold values from -3 to 3
- expert_ids: int32 [8, 768], P('exp', 'seq'), may hold values from 0 to 31
- slot_ids: int32 [8, 768], P('exp', 'seq'), may hold values from -1 to 11, as said below
Outputs:
- harvested: bfloat16 [8, 768, 2048], P('exp', 'seq')
- reconstruction: bfloat16 [8, 768, 2048], P('exp', 'seq')
- error_rows: bfloat16 [8, 768, 2048], P('exp', 'seq')
- dec_grad: bfloat16 [32, 1024, 2048], P(('seq', 'exp'))
Inputs may be any that keep to these rules, and one draw needn't show every extreme that they name: `doc_ids`: each sequence's numbers start at 0, never fall, and rise by one at each of 7 document starts. `slot_ids`: among one device's tokens, those that name the same expert and are kept hold the slots 0 to n - 1 in some order, n at most 12; -1 marks a token left out. In every draw some expert holds all 12 slots on every device.
All inputs are finite; a program needn't handle non-finite values.
Results may differ from a plain program's by a relative error of at most 0.014.
Values may be sent and summed in bfloat16 or wider, within the bound.
No kernel may reach another device: no remote copies, remote signals or barrier semaphores. Data moves between devices by JAX's collectives and lax.ppermute only.
A program may use at most 128 MiB of HBM per device.

v0:
```python
import math

import jax
import jax.numpy as jnp
from jax import lax
from jax.sharding import PartitionSpec as P

HEAD_DIMENSION = 128


masked_score = -1e30


def attend_block(query_block, key_part, value_part, visible, score_scale):
    scores = (
        jnp.einsum("qhd,kd->hqk", query_block, key_part, preferred_element_type=jnp.float32)
        * score_scale
    )
    scores = jnp.where(visible[None, :, :], scores, masked_score)
    highest = jnp.max(scores, axis=2, keepdims=True)
    weights = jnp.exp(scores - highest)
    normed = (weights / jnp.sum(weights, axis=2, keepdims=True)).astype(jnp.bfloat16)
    mixed = jnp.einsum("hqk,kd->qhd", normed, value_part, preferred_element_type=jnp.float32)
    return mixed.astype(jnp.bfloat16)


def shards(
    query_rows,
    key_rows,
    value_matrix,
    doc_ids,
    out_weight,
    enc_weight,
    enc_bias,
    dec_weight,
    dec_bias,
    expert_ids,
    slot_ids,
):
    local_tokens = query_rows.shape[1]
    seq_groups = lax.axis_size("seq")
    exp_groups = lax.axis_size("exp")
    devices_all = seq_groups * exp_groups
    query_heads = query_rows.shape[2] // HEAD_DIMENSION
    kv_heads = key_rows.shape[2] // HEAD_DIMENSION
    heads_here = query_heads // seq_groups
    kv_share = seq_groups // kv_heads
    query_local = query_rows[0].reshape(local_tokens, seq_groups, heads_here * HEAD_DIMENSION)
    paired = jnp.concatenate(
        [
            key_rows[0].reshape(local_tokens, kv_heads, HEAD_DIMENSION),
            value_matrix[0].reshape(local_tokens, kv_heads, HEAD_DIMENSION),
        ],
        axis=2,
    )
    paired = jnp.repeat(paired, kv_share, axis=1)
    query_all, paired_all = (
        lax.all_to_all(query_local, "seq", split_axis=1, concat_axis=0, tiled=True),
        lax.all_to_all(paired, "seq", split_axis=1, concat_axis=0, tiled=True),
    )
    span_length = local_tokens * seq_groups
    query_all = query_all.reshape(span_length, heads_here, HEAD_DIMENSION)
    key_all = paired_all[:, 0, :HEAD_DIMENSION]
    value_all = paired_all[:, 0, HEAD_DIMENSION:]
    doc_row = doc_ids[0]
    positions = jnp.arange(span_length)
    block_rows = 512 if span_length % 512 == 0 else span_length
    score_scale = 1.0 / math.sqrt(HEAD_DIMENSION)
    pieces_out = []
    for row_start in range(0, span_length, block_rows):
        row_stop = row_start + block_rows
        visible = (positions[row_start:row_stop, None] >= positions[None, :row_stop]) & (
            doc_row[row_start:row_stop, None] == doc_row[None, :row_stop]
        )
        mixed = attend_block(
            query_all[row_start:row_stop],
            key_all[:row_stop],
            value_all[:row_stop],
            visible,
            score_scale,
        )
        pieces_out.append(mixed.reshape(block_rows, heads_here * HEAD_DIMENSION))
    attended = jnp.concatenate(pieces_out, axis=0)
    own_rows = lax.all_gather(out_weight, "exp", axis=0, tiled=True)
    projected = lax.psum_scatter(
        jnp.dot(attended, own_rows, preferred_element_type=jnp.float32).astype(jnp.bfloat16),
        "seq",
        scatter_dimension=0,
        tiled=True,
    )
    local_experts = enc_weight.shape[0]
    experts_all = local_experts * devices_all
    capacity = 2 * local_tokens // experts_all
    model_width = projected.shape[1]
    expert_here = expert_ids[0]
    slot_here = slot_ids[0]
    kept_token = slot_here >= 0
    slot_count = experts_all * capacity
    target = jnp.where(kept_token, expert_here * capacity + slot_here, slot_count)
    send_rows = (
        jnp.zeros((slot_count, model_width), jnp.bfloat16).at[target].set(projected, mode="drop")
    )
    send_live = (
        jnp.zeros((slot_count,), jnp.bfloat16)
        .at[target]
        .set(jnp.ones((local_tokens,), jnp.bfloat16), mode="drop")
    )
    arrived, arrived_live = (
        lax.all_to_all(
            send_rows.reshape(devices_all, local_experts, capacity, model_width),
            ("seq", "exp"),
            split_axis=0,
            concat_axis=2,
            tiled=True,
        ),
        lax.all_to_all(
            send_live.reshape(devices_all, local_experts, capacity),
            ("seq", "exp"),
            split_axis=0,
            concat_axis=2,
            tiled=True,
        ),
    )
    slot_total = devices_all * capacity
    slot_rows = arrived.reshape(local_experts, slot_total, model_width)
    slot_live = arrived_live.reshape(local_experts, slot_total)
    centered = (slot_rows.astype(jnp.float32) - dec_bias).astype(jnp.bfloat16)
    pre_act = (
        jnp.einsum("esd,edf->esf", centered, enc_weight, preferred_element_type=jnp.float32)
        + enc_bias[:, None, :]
    )
    latent = jnp.maximum(pre_act, 0.0).astype(jnp.bfloat16)
    rebuilt = (
        jnp.einsum("esf,efd->esd", latent, dec_weight, preferred_element_type=jnp.float32)
        + dec_bias
    ).astype(jnp.bfloat16)
    residue = (rebuilt.astype(jnp.float32) - slot_rows.astype(jnp.float32)).astype(jnp.bfloat16)
    gated = latent * slot_live[:, :, None]
    dec_grad = jnp.einsum(
        "esf,esd->efd", gated, residue, preferred_element_type=jnp.float32
    ).astype(jnp.bfloat16)
    returned = lax.all_to_all(
        rebuilt.reshape(1, local_experts, slot_total, model_width),
        ("seq", "exp"),
        split_axis=2,
        concat_axis=0,
        tiled=True,
    )
    returned = returned.reshape(slot_count, model_width)
    picked_rows = returned[jnp.minimum(target, slot_count - 1)]
    reconstruction = jnp.where(
        kept_token[:, None], picked_rows, dec_bias.astype(jnp.bfloat16)[None, :]
    )
    error_rows = (reconstruction.astype(jnp.float32) - projected.astype(jnp.float32)).astype(
        jnp.bfloat16
    )
    return (projected[None], reconstruction[None], error_rows[None], dec_grad)


def solution(mesh):
    return jax.shard_map(
        shards,
        mesh=mesh,
        in_specs=(
            P("exp", "seq", None),
            P("exp", "seq", None),
            P("exp", "seq", None),
            P("exp", None),
            P(("seq", "exp"), None),
            P(("seq", "exp"), None, None),
            P(("seq", "exp"), None),
            P(("seq", "exp"), None, None),
            P(),
            P("exp", "seq"),
            P("exp", "seq"),
        ),
        out_specs=(
            P("exp", "seq", None),
            P("exp", "seq", None),
            P("exp", "seq", None),
            P(("seq", "exp"), None, None),
        ),
        check_vma=False,
    )
```

profile of v0, /device:TPU:0, one launch (start us, length us, event | category | flops | bytes accessed | tf_op | source)
XLA Modules:
  0.0 292.0 jit_solution(16970659422148447972)
XLA Ops:
  7.2 0.0 all-gather.2.cloned.1.call-start
  7.2 0.7 all-gather.2.cloned.1.call-update
  7.9 2.9 reshape_squeeze.11
  10.8 1.6 copy.36
  12.4 0.0 copy-start.2
  12.4 0.0 copy-start.3
  12.4 4.4 %all-to-all-start.1 = ((bf16[192,4,1024]{2,0,1:T(8,128)(2,1)}), bf16[192,4,1024]{2,0,1:T(8,128)(2,1)S(1)}, u32[]{:S(2)}, u32[]{:S(2)}) async-start(bf16[192,4,1024]{2,0,1:T(8,128)(2,1)} %copy.36), calls=%async_computation.1 | async-start | bytes 3145728 | tf_op jit(solution)/shard_map/all_to_all | solution.py:58
  16.8 0.0 copy-done.2
  16.8 0.0 copy-start.5
  16.8 0.1 reshape_squeeze.9
  16.9 0.0 copy-done.3
  16.9 0.1 reshape_squeeze.10
  17.0 0.8 pad_maximum_fusion
  17.8 19.1 %all-to-all-done.1 = bf16[192,4,1024]{2,0,1:T(8,128)(2,1)S(1)} async-done(((bf16[192,4,1024]{2,0,1:T(8,128)(2,1)}), bf16[192,4,1024]{2,0,1:T(8,128)(2,1)S(1)}, u32[]{:S(2)}, u32[]{:S(2)}) %all-to-all-start.1) | async-done | bytes 1572896 | tf_op jit(solution)/shard_map/all_to_all | solution.py:58
  36.8 3.5 %all-to-all-start = ((bf16[192,4,256]{2,0,1:T(8,128)(2,1)}), bf16[192,4,256]{2,0,1:T(8,128)(2,1)S(1)}, u32[]{:S(2)}, u32[]{:S(2)}) async-start(bf16[192,4,256]{2,0,1:T(8,128)(2,1)} %pad_maximum_fusion), calls=%async_computation | async-start | bytes 786432 | tf_op jit(solution)/shard_map/all_to_all | solution.py:59
  40.3 0.0 reduce-scatter.2.cloned.1.call-start
  40.3 0.0 copy-done.5
  40.4 1.2 fusion.14
  41.6 0.4 copy.47
  42.0 5.6 %all-to-all-done = bf16[192,4,256]{2,0,1:T(8,128)(2,1)S(1)} async-done(((bf16[192,4,256]{2,0,1:T(8,128)(2,1)}), bf16[192,4,256]{2,0,1:T(8,128)(2,1)S(1)}, u32[]{:S(2)}, u32[]{:S(2)}) %all-to-all-start) | async-done | bytes 393248 | tf_op jit(solution)/shard_map/all_to_all | solution.py:59
  47.7 12.1 %fusion.36 = (f32[8,768]{1,0:T(8,128)}, f32[8,768,768]{1,2,0:T(8,128)}) fusion(pred[768,768]{0,1:T(8,128)(4,1)} %fusion.14, bf16[768,8,128]{2,1,0:T(8,128)(2,1)S(1)} %bitcast.84, bf16[768,1,256]{2,0,1:T(8,128)(2,1)S(1)} %bitcast.87), kind=kOutput, calls=%fused_computation.50 | convolution fusion | flops 1226834688 | bytes 21258240 | tf_op jit(solution)/shard_map/sub | solution.py:21
  59.8 8.5 %fusion.15 = bf16[128,8,768]{2,0,1:T(8,128)(2,1)S(1)} fusion(f32[8,768,768]{1,2,0:T(8,128)} %get-tuple-element.7, f32[8,768]{1,0:T(8,128)} %get-tuple-element.6, bf16[768,1,256]{2,0,1:T(8,128)(2,1)S(1)} %bitcast.88), kind=kOutput, calls=%fused_computation.24 | convolution fusion | flops 1218183168 | bytes 20668416 | tf_op jit(solution)/shard_map/hqk,kd->qhd/dot_general | solution.py:23
  68.3 17.3 %all-gather.2.cloned.1.call-done = bf16[1024,2048]{1,0:T(8,128)(2,1)} async-done(((bf16[128,2048]{1,0:T(8,128)(2,1)}), bf16[1024,2048]{1,0:T(8,128)(2,1)}) %all-gather.2.cloned.1.call-update) | async-done | bytes 4194320 | tf_op jit(solution)/shard_map/all_gather | solution.py:84
  85.6 7.0 %convolution_convert_fusion = bf16[768,2048]{1,0:T(8,128)(2,1)} fusion(bf16[768,1024]{0,1:T(8,128)(2,1)S(1)} %bitcast.93, bf16[1024,2048]{1,0:T(8,128)(2,1)} %all-gather.2.cloned.1.call-done), kind=kOutput, calls=%fused_computation.19 | convolution fusion | flops 3222798336 | bytes 8912896 | tf_op jit(solution)/shard_map/dot_general | solution.py:86
  92.7 0.0 copy-start.6
  92.7 0.0 copy-start.7
  92.7 0.0 reduce-scatter.2.cloned.1.call-update
  92.7 0.7 copy-done.6
  93.3 0.0 copy-done.7
  93.4 35.9 %reduce-scatter.2.cloned.1.call-done = bf16[192,2048]{1,0:T(8,128)(2,1)} async-done(((bf16[768,2048]{1,0:T(8,128)(2,1)}), bf16[192,2048]{1,0:T(8,128)(2,1)}) %reduce-scatter.2.cloned.1.call-update) | async-done | bytes 786448 | tf_op jit(solution)/shard_map/reduce_scatter | solution.py:85
  129.2 2.9 scatter_custom_fusion
  132.1 1.5 reshape.271
  133.6 4.6 %all-to-all-start.2 = ((bf16[32,1,12,2048]{3,2,1,0:T(8,128)(2,1)}), bf16[32,1,12,2048]{3,2,1,0:T(8,128)(2,1)S(1)}, u32[]{:S(2)}, u32[]{:S(2)}) async-start(bf16[32,1,12,2048]{3,2,1,0:T(8,128)(2,1)} %bitcast.82), calls=%async_computation.3 | async-start | bytes 4194304 | tf_op jit(solution)/shard_map/all_to_all | solution.py:109
  138.2 1.8 scatter_custom_fusion.1
  140.0 0.7 reshape.304
  140.7 47.6 %all-to-all-done.2 = bf16[32,1,12,2048]{3,2,1,0:T(8,128)(2,1)S(1)} async-done(((bf16[32,1,12,2048]{3,2,1,0:T(8,128)(2,1)}), bf16[32,1,12,2048]{3,2,1,0:T(8,128)(2,1)S(1)}, u32[]{:S(2)}, u32[]{:S(2)}) %all-to-all-start.2) | async-done | bytes 1572896 | tf_op jit(solution)/shard_map/all_to_all | solution.py:109
  188.3 2.5 all-to-all-start.4
  190.8 0.0 copy-done.4
  190.9 1.8 subtract_convert_fusion
  192.6 3.6 %convert_element_type.76 = bf16[384,2048]{1,0:T(8,128)(2,1)} reshape(bf16[32,1,12,2048]{3,2,1,0:T(8,128)(2,1)} %subtract_convert_fusion) | data formatting | bytes 3145728 | tf_op jit(solution)/shard_map/convert_element_type | solution.py:127
  196.3 0.0 copy-done.9
  196.3 4.6 %maximum_convert_fusion = bf16[384,1024]{1,0:T(8,128)(2,1)S(1)} fusion(bf16[384,2048]{1,0:T(8,128)(2,1)} %convert_element_type.76, bf16[1,2048,1024]{2,1,0:T(8,128)(2,1)} %param.16, f32[1024]{0:T(1024)S(1)} %bitcast.92), kind=kOutput, calls=%fused_computation.27 | convolution fusion | flops 1611792384 | bytes 6557696 | tf_op jit(solution)/shard_map/esd,edf->esf/dot_general | solution.py:129
  200.9 0.0 copy-done.8
  200.9 1.8 add_convert_fusion
  202.7 0.0 copy-start
  202.7 4.1 %copy.63 = bf16[1,1,384,2048]{3,1,0,2:T(2,128)(2,1)} copy(bf16[1,1,384,2048]{3,2,1,0:T(8,128)(2,1)S(1)} %bitcast.85) | data formatting | bytes 3145728 | tf_op jit(solution)/shard_map/reshape | solution.py:143
  206.8 0.0 copy-done
  206.8 0.5 broadcast.184
  207.3 12.6 %reduce.4 = bf16[384,2048]{1,0:T(8,128)(2,1)} reduce(bf16[384,1,1,2048]{3,2,1,0:T(2,128)(2,1)} %bitcast.80, bf16[]{:T(256)} %broadcast.184), dimensions={1,2}, to_apply=%bitcast.78.reduce_sub_computation | reduce | bytes 3145730
  219.9 4.8 %reshape.312 = bf16[32,2,12288]{2,1,0:T(2,128)(2,1)} reshape(bf16[384,2048]{1,0:T(8,128)(2,1)} %reduce.4) | data formatting | bytes 3145728
  224.8 0.0 all-to-all-done.4
  224.8 5.9 %all-to-all-start.3 = ((bf16[32,2,12288]{2,1,0:T(2,128)(2,1)}), bf16[32,2,12288]{2,1,0:T(2,128)(2,1)}, u32[]{:S(2)}, u32[]{:S(2)}) async-start(bf16[32,2,12288]{2,1,0:T(2,128)(2,1)} %reshape.312), calls=%async_computation.4 | async-start | bytes 3145728 | tf_op jit(solution)/shard_map/all_to_all | solution.py:142
  230.8 0.1 reduce.2
  230.8 0.1 mul.43
  230.9 1.8 reshape.277
  232.8 6.9 %convert_bitcast_fusion = bf16[1,1024,2048]{2,1,0:T(8,128)(2,1)} fusion(f32[384,2048]{1,0:T(8,128)} %reshape.277, bf16[384,2048]{1,0:T(8,128)(2,1)} %copy-done, bf16[384,1024]{1,0:T(8,128)(2,1)S(1)} %maximum_convert_fusion, bf16[384]{0:T(512)(128)(2,1)S(1)} %mul.43), kind=kOutput, calls=%fused_computation.17 | convolution fusion | flops 1615462400 | bytes 9700096 | tf_op jit(solution)/shard_map/esf,esd->efd/dot_general | solution.py:139
  239.6 29.9 %all-to-all-done.3 = bf16[32,2,12288]{2,1,0:T(2,128)(2,1)} async-done(((bf16[32,2,12288]{2,1,0:T(2,128)(2,1)}), bf16[32,2,12288]{2,1,0:T(2,128)(2,1)}, u32[]{:S(2)}, u32[]{:S(2)}) %all-to-all-start.3) | async-done | bytes 1572896 | tf_op jit(solution)/shard_map/all_to_all | solution.py:142
  269.5 9.5 %reshape.313 = bf16[384,1,1,2048]{3,2,1,0:T(2,128)(2,1)} reshape(bf16[32,2,12288]{2,1,0:T(2,128)(2,1)} %all-to-all-done.3) | data formatting | bytes 3145728
  279.0 2.8 copy.62
  281.8 0.0 copy-start.1
  281.8 1.1 gather_fusion
  283.0 1.0 bitcast_select_fusion.4
  284.0 0.0 copy-done.1
  284.0 1.2 fusion.25
  (12 shorter events, 0.1 us)
Async XLA Ops:
  7.2 78.5 %all-gather.2.cloned.1.call-start = ((), (), s32[]{:S(2)}) async-start(), calls=%async_computation.6 | async-start | bytes 4718592 | tf_op jit(solution)/shard_map/all_gather | solution.py:84
  12.4 4.4 %copy-start.2 = (bf16[1,192,512]{2,1,0:T(8,128)(2,1)S(1)}, bf16[1,192,512]{2,1,0:T(8,128)(2,1)}, u32[]{:S(2)}) copy-start(bf16[1,192,512]{2,1,0:T(8,128)(2,1)} %param.12) | copy-start | bytes 589828
  12.4 4.5 %copy-start.3 = (bf16[1,192,512]{2,1,0:T(8,128)(2,1)S(1)}, bf16[1,192,512]{2,1,0:T(8,128)(2,1)}, u32[]{:S(2)}) copy-start(bf16[1,192,512]{2,1,0:T(8,128)(2,1)} %param.13) | copy-start | bytes 589828
  12.4 24.4 %all-to-all-start.1 = ((bf16[192,4,1024]{2,0,1:T(8,128)(2,1)}), bf16[192,4,1024]{2,0,1:T(8,128)(2,1)S(1)}, u32[]{:S(2)}, u32[]{:S(2)}) async-start(bf16[192,4,1024]{2,0,1:T(8,128)(2,1)} %copy.36), calls=%async_computation.1 | async-start | bytes 3145728 | tf_op jit(solution)/shard_map/all_to_all | solution.py:58
  16.8 23.6 %copy-start.5 = (s32[1,768]{1,0:T(1,128)S(1)}, s32[1,768]{1,0:T(1,128)}, u32[]{:S(2)}) copy-start(s32[1,768]{1,0:T(1,128)} %param.14) | copy-start | bytes 9220
  36.8 10.8 %all-to-all-start = ((bf16[192,4,256]{2,0,1:T(8,128)(2,1)}), bf16[192,4,256]{2,0,1:T(8,128)(2,1)S(1)}, u32[]{:S(2)}, u32[]{:S(2)}) async-start(bf16[192,4,256]{2,0,1:T(8,128)(2,1)} %pad_maximum_fusion), calls=%async_computation | async-start | bytes 786432 | tf_op jit(solution)/shard_map/all_to_all | solution.py:59
  40.3 89.0 %reduce-scatter.2.cloned.1.call-start = ((), (), s32[]{:S(2)}) async-start(), calls=%async_computation.7 | async-start | bytes 3932160 | tf_op jit(solution)/shard_map/reduce_scatter | solution.py:85
  92.7 0.7 copy-start.6
  92.7 0.7 copy-start.7
  133.6 57.2 %copy-start.4 = (f32[2048]{0:T(1024)S(1)}, f32[2048]{0:T(1024)}, u32[]{:S(2)}) copy-start(f32[2048]{0:T(1024)} %param.19) | copy-start | bytes 24580
  133.6 54.7 %all-to-all-start.2 = ((bf16[32,1,12,2048]{3,2,1,0:T(8,128)(2,1)}), bf16[32,1,12,2048]{3,2,1,0:T(8,128)(2,1)S(1)}, u32[]{:S(2)}, u32[]{:S(2)}) async-start(bf16[32,1,12,2048]{3,2,1,0:T(8,128)(2,1)} %bitcast.82), calls=%async_computation.3 | async-start | bytes 4194304 | tf_op jit(solution)/shard_map/all_to_all | solution.py:109
  188.3 36.5 %all-to-all-start.4 = ((bf16[32,1,12]{2,1,0:T(2,128)(2,1)}), bf16[32,1,12]{2,1,0:T(2,128)(2,1)S(1)}, u32[]{:S(2)}, u32[]{:S(2)}) async-start(bf16[32,1,12]{2,1,0:T(2,128)(2,1)} %reshape.304), calls=%async_computation.5 | async-start | bytes 32768 | tf_op jit(solution)/shard_map/all_to_all | solution.py:116
  192.6 3.6 %copy-start.9 = (f32[1,1024]{1,0:T(1,128)S(1)}, f32[1,1024]{1,0:T(1,128)}, u32[]{:S(2)}) copy-start(f32[1,1024]{1,0:T(1,128)} %param.17) | copy-start | bytes 12292
  196.3 4.6 %copy-start.8 = (bf16[1,1024,2048]{2,1,0:T(8,128)(2,1)S(1)}, bf16[1,1024,2048]{2,1,0:T(8,128)(2,1)}, u32[]{:S(2)}) copy-start(bf16[1,1024,2048]{2,1,0:T(8,128)(2,1)} %param.18) | copy-start | bytes 12582916
  202.7 4.1 %copy-start = (bf16[384,2048]{1,0:T(8,128)(2,1)}, bf16[384,2048]{1,0:T(8,128)(2,1)S(1)}, u32[]{:S(2)}) copy-start(bf16[384,2048]{1,0:T(8,128)(2,1)S(1)} %add_convert_fusion) | copy-start | bytes 4718596
  224.8 44.7 %all-to-all-start.3 = ((bf16[32,2,12288]{2,1,0:T(2,128)(2,1)}), bf16[32,2,12288]{2,1,0:T(2,128)(2,1)}, u32[]{:S(2)}, u32[]{:S(2)}) async-start(bf16[32,2,12288]{2,1,0:T(2,128)(2,1)} %reshape.312), calls=%async_computation.4 | async-start | bytes 3145728 | tf_op jit(solution)/shard_map/all_to_all | solution.py:142
  281.8 2.2 copy-start.1
Sparse Core Ops, SparseCore 0:
  10.1 75.5 all-gather.1
  92.8 36.3 reduce-scatter.1
where the time goes:
time: 293 us; the launch traced here: 292 us
  waiting for transfers between devices  156 us (53%)
  local copies, waits for them, and re-layouts  41.1 us (14%)
  matrix products  41 us (14%)
  starting transfers between devices  21 us (7%)
  other arithmetic  18.7 us (6%)
  between operations  14.3 us (5%)
    all_to_all x1, waiting for transfers between devices, shards(): lax.all_to_all(send_rows.reshape(devices_all, local_experts, capacity, mo...  47.6 us
    reduce_scatter x1, waiting for transfers between devices, shards(): lax.psum_scatter(jnp.dot(attended, own_rows, preferred_element_type=jnp.f...  35.9 us
    all_to_all x1, waiting for transfers between devices, shards(): lax.all_to_all(rebuilt.reshape(1, local_experts, slot_total, model_width)...  29.9 us
    all_to_all x1, waiting for transfers between devices, shards(): lax.all_to_all(query_local, 'seq', split_axis=1, concat_axis=0, tiled=True)  19.1 us
    unnamed x25, local copies, waits for them, and re-layouts  18.8 us
    all_gather x1, waiting for transfers between devices, shards(): own_rows = lax.all_gather(out_weight, 'exp', axis=0, tiled=True)  17.3 us
    unnamed x2, other arithmetic  12.6 us
    sub x1, matrix products, attend_block(): weights = jnp.exp(scores - highest)  12.1 us
  transfers between devices with their start and end apart: 7, of which 6 were waited for; matrix products, arithmetic and copies ran while one was open for 25% of the time, Pallas kernels for 0%

commit v1 on v0

v1 whole, which is shorter than its diff:
```python
import functools
import math

import jax
import jax.numpy as jnp
from jax import lax
from jax.experimental import pallas as pl
from jax.experimental.pallas import tpu as pltpu
from jax.sharding import PartitionSpec as P

HEAD_DIMENSION = 128
CORES = 2
KEY_BLOCK = 128
ROW_BLOCK = 64
EMPTY = 1e30
MASKED = -1e30
CHUNKS = 2

bf16 = jnp.bfloat16
f32 = jnp.float32


def call(kernel, name, out_shape, flops, moved, **kw):
    return pl.pallas_call(
        kernel,
        name=name,
        out_shape=out_shape,
        cost_estimate=pl.CostEstimate(flops=int(flops), bytes_accessed=int(moved), transcendentals=0),
        **kw,
    )


def dot(a, b, dims=((1,), (0,))):
    return lax.dot_general(a, b, (dims, ((), ())), preferred_element_type=f32)


def attention_kernel(
    heads, parts, scal, first, q_ref, mine_ref, theirs_ref, dcol_ref, drow_ref, o_ref,
    k_scr, v_scr, s_scr, m_scr, l_scr, a_scr,
):
    group = pl.program_id(0)
    tokens = q_ref.shape[0]
    width = k_scr.shape[1]
    hd = HEAD_DIMENSION

    @pl.when(group == 0)
    def _():
        for d in range(parts):
            for which, ref in enumerate((mine_ref, theirs_ref)):
                at = pl.multiple_of(scal[2 + d * CORES + which] * tokens, tokens)
                k_scr[pl.ds(at, tokens), :] = ref[d * tokens : (d + 1) * tokens, :width]
                v_scr[pl.ds(at, tokens), :] = ref[d * tokens : (d + 1) * tokens, width:]

    base = scal[0] * tokens
    lane = pl.multiple_of(group * hd, hd)
    scale = math.log2(math.e) / math.sqrt(hd)
    rows = heads * ROW_BLOCK

    def part(i, carry):
        at = pl.multiple_of(i * ROW_BLOCK, ROW_BLOCK)
        here = pl.multiple_of(base + at, ROW_BLOCK)
        q_all = q_ref[pl.ds(at, ROW_BLOCK), :]
        q = jnp.concatenate([q_all[:, h * hd : (h + 1) * hd] for h in range(heads)], axis=0)
        lo = first[scal[0] * (tokens // ROW_BLOCK) + i]
        hi = (here + ROW_BLOCK - 1) // KEY_BLOCK + 1
        row_pos = here + lax.broadcasted_iota(jnp.int32, (ROW_BLOCK, KEY_BLOCK), 0)
        lane_pos = lax.broadcasted_iota(jnp.int32, (ROW_BLOCK, KEY_BLOCK), 1)
        row_doc = drow_ref[pl.ds(here, ROW_BLOCK), :]
        m_scr[...] = jnp.full_like(m_scr, MASKED)

        def scores(j, carry):
            col = pl.multiple_of(j * KEY_BLOCK, KEY_BLOCK)
            s = dot(q, k_scr[pl.ds(col, KEY_BLOCK), pl.ds(lane, hd)], ((1,), (1,)))
            visible = (row_pos >= lane_pos + col) & (row_doc == dcol_ref[:, pl.ds(col, KEY_BLOCK)])
            s = jnp.where(visible[None], s.reshape(heads, ROW_BLOCK, KEY_BLOCK), MASKED)
            s = s.reshape(rows, KEY_BLOCK)
            s_scr[j - lo] = s
            m_scr[...] = jnp.maximum(m_scr[...], s)
            return carry

        lax.fori_loop(lo, hi, scores, 0)
        top = jnp.max(m_scr[...], axis=1, keepdims=True)
        m_scr[...] = jnp.broadcast_to(top * scale, m_scr.shape)
        l_scr[...] = jnp.zeros_like(l_scr)
        a_scr[...] = jnp.zeros_like(a_scr)

        def weigh(j, carry):
            col = pl.multiple_of(j * KEY_BLOCK, KEY_BLOCK)
            p = jnp.exp2(s_scr[j - lo] * scale - m_scr[...])
            l_scr[...] += p
            a_scr[...] += dot(p.astype(bf16), v_scr[pl.ds(col, KEY_BLOCK), pl.ds(lane, hd)])
            return carry

        lax.fori_loop(lo, hi, weigh, 0)
        out = (a_scr[...] / jnp.sum(l_scr[...], axis=1, keepdims=True)).astype(bf16)
        for h in range(heads):
            o_ref[pl.ds(at, ROW_BLOCK), h * hd : (h + 1) * hd] = out[
                h * ROW_BLOCK : (h + 1) * ROW_BLOCK
            ]
        return carry

    lax.fori_loop(0, tokens // ROW_BLOCK, part, 0)


def attend(scal, first, q, q_at, heads, mine, theirs, doc_col, doc_row, parts, tag):
    tokens = q.shape[0]
    span = doc_col.shape[1]
    width = mine.shape[1] // 2
    groups = width // HEAD_DIMENSION
    rows = heads * ROW_BLOCK
    lanes = heads * HEAD_DIMENSION
    whole = lambda *shape: pl.BlockSpec(shape, lambda g, *_: (0,) * len(shape))
    return call(
        functools.partial(attention_kernel, heads, parts),
        "attend_" + tag,
        jax.ShapeDtypeStruct((tokens, groups * lanes), bf16),
        4 * tokens * groups * lanes * span // 2,
        4 * tokens * groups * lanes + 8 * span * width,
        grid_spec=pltpu.PrefetchScalarGridSpec(
            num_scalar_prefetch=2,
            grid=(groups,),
            in_specs=[
                pl.BlockSpec((tokens, lanes), lambda g, sc, fi: (0, sc[1] * q_at + g)),
                whole(*mine.shape),
                whole(*theirs.shape),
                whole(1, span),
                whole(span, 1),
            ],
            out_specs=pl.BlockSpec((tokens, lanes), lambda g, *_: (0, g)),
            scratch_shapes=[
                pltpu.VMEM((span, width), bf16),
                pltpu.VMEM((span, width), bf16),
                pltpu.VMEM((span // KEY_BLOCK, rows, KEY_BLOCK), f32),
                pltpu.VMEM((rows, KEY_BLOCK), f32),
                pltpu.VMEM((rows, KEY_BLOCK), f32),
                pltpu.VMEM((rows, HEAD_DIMENSION), f32),
            ],
        ),
    )(scal, first, q, mine, theirs, doc_col, doc_row)


def order_kernel(order, *refs):
    blocks, out = refs[:-1], refs[-1]
    depth = blocks[0].shape[0]
    at = lambda i: pl.multiple_of(order[i] * depth, depth)
    for i, block in enumerate(blocks[:-2]):
        out[pl.ds(at(i), depth), :] = block[...]
    last = at(len(blocks) - 2)
    out[pl.ds(pl.multiple_of(last, depth // 2), depth // 2), :] = blocks[-2][...]
    out[pl.ds(pl.multiple_of(last + depth // 2, depth // 2), depth // 2), :] = blocks[-1][...]


def in_order(order, blocks):
    depth, cols = blocks[0].shape
    rows = depth * (len(blocks) - 1)
    vmem = pl.BlockSpec(memory_space=pltpu.VMEM)
    return call(
        order_kernel,
        "in_order",
        jax.ShapeDtypeStruct((rows, cols), bf16),
        0,
        4 * rows * cols,
        in_specs=[pl.BlockSpec(memory_space=pltpu.SMEM)] + [vmem] * len(blocks),
        out_specs=vmem,
    )(order, *blocks)


def ring_gather(w, ring):
    size = len(ring)
    half = size // 2
    ahead = [(ring[i], ring[(i + 1) % size]) for i in range(size)]
    back = [(ring[i], ring[(i - 1) % size]) for i in range(size)]
    depth = w.shape[0]
    fw = bw = w
    blocks = [w]
    for step in range(1, half):
        fw = lax.ppermute(fw, "exp", ahead)
        bw = lax.ppermute(bw, "exp", back)
        blocks += [fw, bw]
    blocks.append(lax.ppermute(fw[: depth // 2], "exp", ahead))
    blocks.append(lax.ppermute(bw[depth // 2 :], "exp", back))
    return blocks


def project_kernel(depth, scal, *refs):
    rest, (w_mine, w_theirs, own_ref), sends = refs[: len(refs) // 2 - 1], refs[len(refs) // 2 - 1 : len(refs) // 2 + 2], refs[len(refs) // 2 + 2 :]
    tokens = rest[0].shape[0]
    a = pl.multiple_of(scal[0] * depth, depth)
    b = pl.multiple_of((1 - scal[0]) * depth, depth)
    x = jnp.concatenate([r[:, pl.ds(a, depth)] for r in rest], axis=0)
    y = jnp.concatenate([r[:, pl.ds(b, depth)] for r in rest], axis=0)
    out = dot(x, w_mine[...]) + dot(y, w_theirs[...])
    own_ref[...] = out[:tokens]
    for i, ref in enumerate(sends):
        ref[...] = out[(i + 1) * tokens : (i + 2) * tokens].astype(bf16)


def project(core, attended, w_mine, w_theirs):
    tokens, width = attended[0].shape
    depth, cols = w_mine.shape
    parts = len(attended)
    tile = min(512, cols)
    col = lambda n: pl.BlockSpec((n, tile), lambda i, *_: (0, i))
    full = pl.BlockSpec((tokens, width), lambda i, *_: (0, 0))
    return call(
        functools.partial(project_kernel, depth),
        "project",
        [jax.ShapeDtypeStruct((tokens, cols), f32)]
        + [jax.ShapeDtypeStruct((tokens, cols), bf16)] * (parts - 1),
        2 * parts * tokens * width * cols,
        2 * parts * tokens * width + 2 * width * cols,
        grid_spec=pltpu.PrefetchScalarGridSpec(
            num_scalar_prefetch=1,
            grid=(cols // tile,),
            in_specs=[full] * parts + [col(depth)] * 2,
            out_specs=[col(tokens)] * parts,
        ),
    )(core, *attended, w_mine, w_theirs)


class Slots:
    def __init__(self, capacity, devices):
        self.devices = devices
        self.full = capacity // 8
        rest = capacity % 8
        self.tail = 0
        if rest:
            self.tail = 1
            while self.tail < rest:
                self.tail *= 2
        self.cuts = 8 // self.tail if self.tail else 0
        self.rows = 8 * devices
        self.groups = self.full + (1 if self.tail else 0)

    def width(self, cols):
        return self.full * cols + (cols // self.cuts if self.tail else 0)


def slot_keys(slots, expert, slot):
    keys = []
    kept = slot >= 0
    for g in range(slots.full):
        ok = kept & (slot >= 8 * g) & (slot < 8 * g + 8)
        keys.append(jnp.where(ok, expert * 8 + slot - 8 * g, -1))
    if slots.tail:
        rest = slot - 8 * slots.full
        for i in range(slots.cuts):
            keys.append(jnp.where(kept & (rest >= 0), expert * 8 + i * slots.tail + rest, -1))
    return jnp.stack(keys, axis=0).astype(jnp.int32)


def one_hot(keys_ref, i, rows):
    n = keys_ref.shape[1]
    return lax.broadcasted_iota(jnp.int32, (rows, n), 0) == keys_ref[i : i + 1, :]


def pack_kernel(slots, parts, keys_ref, own_ref, *refs):
    recv, (rows_ref, out_ref) = refs[:parts], refs[-2:]
    total = own_ref[...]
    for r in recv:
        total = total + r[...].astype(f32)
    x = total.astype(bf16)
    rows_ref[...] = x
    cols = x.shape[1]

    def place(hot, part):
        hot = hot.astype(f32)
        return dot(hot.astype(bf16), part), jnp.sum(hot, axis=1, keepdims=True)

    for g in range(slots.full):
        rows, live = place(one_hot(keys_ref, g, slots.rows), x)
        out_ref[:, g * cols : (g + 1) * cols] = jnp.where(live > 0, rows, EMPTY).astype(bf16)
    if slots.tail:
        cut = cols // slots.cuts
        acc = live_all = None
        for i in range(slots.cuts):
            rows, live = place(one_hot(keys_ref, slots.full + i, slots.rows), x[:, i * cut : (i + 1) * cut])
            acc = rows if acc is None else acc + rows
            live_all = live if live_all is None else live_all + live
        out_ref[:, slots.full * cols :] = jnp.where(live_all > 0, acc, EMPTY).astype(bf16)


def pack(slots, keys, own, received, rows_out, chunk):
    tokens, cols = own.shape
    width = slots.width(cols)
    parts = len(received)
    full = lambda *shape: pl.BlockSpec(shape, lambda i: (0,) * len(shape))
    args = [keys, own, *received]
    specs = [full(*a.shape) for a in args]
    alias = {}
    if rows_out.shape != (0,):
        alias = {len(args): 0}
        args.append(rows_out)
        specs.append(pl.BlockSpec(memory_space=pl.ANY))
    model = cols * CHUNKS

    def kernel(*refs):
        keep = refs[: 2 + parts] + refs[-2:]
        pack_kernel(slots, parts, *keep)

    return call(
        kernel,
        "pack",
        [
            jax.ShapeDtypeStruct((tokens, model), bf16),
            jax.ShapeDtypeStruct((slots.rows, width), bf16),
        ],
        4 * slots.rows * tokens * cols,
        8 * tokens * cols + 2 * slots.rows * width,
        grid=(1,),
        in_specs=specs,
        out_specs=[
            pl.BlockSpec((tokens, cols), lambda i: (0, chunk)),
            full(slots.rows, width),
        ],
        input_output_aliases=alias,
    )(*args)


def spread(slots, block):
    cols = block.shape[1]
    full, cuts = slots.full, slots.cuts
    n = cols * cuts // (full * cuts + 1) if slots.tail else cols // full
    out = [block[:, g * n : (g + 1) * n].astype(f32) for g in range(full)]
    if slots.tail:
        rest = block[:, full * n :].astype(f32)
        rows = rest.shape[0]
        out.append(
            jnp.concatenate(
                [rest]
                + [pltpu.roll(rest, rows - i * slots.tail, 0) for i in range(1, cuts)],
                axis=1,
            )
        )
    return out


def tail_rows(slots, shape):
    return lax.broadcasted_iota(jnp.int32, shape, 0) % 8


def encode_kernel(slots, first, last, block_ref, bias_ref, w_ref, *refs):
    refs = list(refs)
    prev_ref = None if first else refs.pop(0)
    enc_bias_ref = refs.pop(0) if last else None
    out_ref = refs.pop(0)
    n = slots.rows
    for g, rows in enumerate(spread(slots, block_ref[...])):
        live = rows[:, :1] < EMPTY / 2
        if slots.tail and g == slots.full:
            live = live & (tail_rows(slots, (n, 1)) < slots.tail)
        x = jnp.where(live, rows - bias_ref[...], 0.0).astype(bf16)
        at = slice(g * n, (g + 1) * n)
        pre = dot(x, w_ref[0])
        if prev_ref is not None:
            pre = pre + prev_ref[at]
        if last:
            pre = jnp.maximum(pre + enc_bias_ref[...], 0.0)
            pre = jnp.where(live, pre, 0.0)
        out_ref[at] = pre.astype(out_ref.dtype)


def encode(slots, block, dec_bias, enc, chunk, prev, enc_bias):
    first, last = prev is None, enc_bias is not None
    _, model, hidden = enc.shape
    cols = model // CHUNKS
    n = slots.rows * slots.groups
    full = lambda *shape: pl.BlockSpec(shape, lambda i: (0,) * len(shape))
    args = [block, dec_bias, enc]
    specs = [
        full(*block.shape),
        pl.BlockSpec((1, cols), lambda i: (0, chunk)),
        pl.BlockSpec((1, cols, hidden), lambda i: (0, chunk, 0)),
    ]
    for extra in (prev, enc_bias):
        if extra is not None:
            args.append(extra)
            specs.append(full(*extra.shape))
    return call(
        functools.partial(encode_kernel, slots, first, last),
        "encode",
        jax.ShapeDtypeStruct((n, hidden), bf16 if last else f32),
        2 * n * cols * hidden,
        2 * cols * hidden + 2 * block.size + 4 * n * hidden,
        grid=(1,),
        in_specs=specs,
        out_specs=full(n, hidden),
    )(*args)


def decode_kernel(slots, latent_ref, w_ref, bias_ref, block_ref, out_ref, residue_ref):
    n = slots.rows
    source = spread(slots, block_ref[...])
    cols = w_ref.shape[2]
    for g in range(slots.groups):
        at = slice(g * n, (g + 1) * n)
        rebuilt = (dot(latent_ref[at], w_ref[0]) + bias_ref[...]).astype(bf16).astype(f32)
        tail = slots.tail and g == slots.full
        live = source[g][:, :1] < EMPTY / 2
        if tail:
            live = live & (tail_rows(slots, (n, 1)) < slots.tail)
        residue_ref[at] = jnp.where(live, rebuilt - source[g], 0.0).astype(bf16)
        if not tail:
            out_ref[:, g * cols : (g + 1) * cols] = rebuilt.astype(bf16)
            continue
        cut = cols // slots.cuts
        rest = rebuilt[:, :cut]
        which = tail_rows(slots, (n, 1)) // slots.tail
        for i in range(1, slots.cuts):
            moved = pltpu.roll(rebuilt[:, i * cut : (i + 1) * cut], i * slots.tail, 0)
            rest = jnp.where(which == i, moved, rest)
        out_ref[:, slots.full * cols :] = rest.astype(bf16)


def decode(slots, latent, dec, dec_bias, block, chunk):
    _, hidden, model = dec.shape
    cols = model // CHUNKS
    n = latent.shape[0]
    full = lambda *shape: pl.BlockSpec(shape, lambda i: (0,) * len(shape))
    return call(
        functools.partial(decode_kernel, slots),
        "decode",
        [
            jax.ShapeDtypeStruct(block.shape, bf16),
            jax.ShapeDtypeStruct((n, cols), bf16),
        ],
        2 * n * cols * hidden,
        2 * cols * hidden + 4 * block.size + 2 * n * hidden + 2 * n * cols,
        grid=(1,),
        in_specs=[
            full(n, hidden),
            pl.BlockSpec((1, hidden, cols), lambda i: (0, 0, chunk)),
            pl.BlockSpec((1, cols), lambda i: (0, chunk)),
            full(*block.shape),
        ],
        out_specs=[full(*block.shape), full(n, cols)],
    )(latent, dec, dec_bias, block)


def grad_kernel(latent_ref, *refs):
    residues, out_ref = refs[:-1], refs[-1]
    cols = residues[0].shape[1]
    for j, r in enumerate(residues):
        out_ref[0, :, j * cols : (j + 1) * cols] = dot(
            latent_ref[...], r[...], ((0,), (0,))
        ).astype(bf16)


def decoder_grad(latent, residues):
    n, hidden = latent.shape
    cols = residues[0].shape[1]
    model = cols * len(residues)
    tile = min(256, hidden)
    return call(
        grad_kernel,
        "decoder_grad",
        jax.ShapeDtypeStruct((1, hidden, model), bf16),
        2 * n * hidden * model,
        2 * hidden * model + 2 * n * (hidden + model),
        grid=(hidden // tile,),
        in_specs=[pl.BlockSpec((n, tile), lambda i: (0, i))]
        + [pl.BlockSpec((n, cols), lambda i: (0, 0))] * len(residues),
        out_specs=pl.BlockSpec((1, tile, model), lambda i: (0, i, 0)),
    )(latent, *residues)


def finish_kernel(slots, keys_ref, kept_ref, block_ref, bias_ref, rows_ref, *refs):
    recon_ref, error_ref = refs[-2:]
    cols = rows_ref.shape[1]
    turn = lambda i, part: dot(
        one_hot(keys_ref, i, slots.rows).astype(f32).astype(bf16), part, ((0,), (0,))
    )
    total = 0.0
    for g in range(slots.full):
        total = total + turn(g, block_ref[:, g * cols : (g + 1) * cols])
    if slots.tail:
        rest = block_ref[:, slots.full * cols :]
        total = total + jnp.concatenate(
            [turn(slots.full + i, rest) for i in range(slots.cuts)], axis=1
        )
    recon = jnp.where(kept_ref[...] > 0, total, bias_ref[...]).astype(bf16)
    recon_ref[...] = recon
    error_ref[...] = (recon.astype(f32) - rows_ref[...].astype(f32)).astype(bf16)


def finish(slots, keys, kept, block, dec_bias, rows, chunk, outs):
    tokens, model = rows.shape
    cols = model // CHUNKS
    full = lambda *shape: pl.BlockSpec(shape, lambda i: (0,) * len(shape))
    col = lambda n: pl.BlockSpec((n, cols), lambda i: (0, chunk))
    args = [keys, kept, block, dec_bias, rows]
    specs = [full(*keys.shape), full(*kept.shape), full(*block.shape), col(1), col(tokens)]
    alias = {}
    if outs:
        alias = {len(args): 0, len(args) + 1: 1}
        args += list(outs)
        specs += [pl.BlockSpec(memory_space=pl.ANY)] * 2
    return call(
        functools.partial(finish_kernel, slots),
        "finish",
        [jax.ShapeDtypeStruct((tokens, model), bf16)] * 2,
        4 * slots.rows * tokens * cols,
        6 * tokens * cols + 2 * block.size,
        grid=(1,),
        in_specs=specs,
        out_specs=[col(tokens)] * 2,
        input_output_aliases=alias,
    )(*args)


def shards(
    query_rows,
    key_rows,
    value_matrix,
    doc_ids,
    out_weight,
    enc_weight,
    enc_bias,
    dec_weight,
    dec_bias,
    expert_ids,
    slot_ids,
):
    q, k, v = query_rows[0], key_rows[0], value_matrix[0]
    tokens = q.shape[0]
    size, exp_size = lax.axis_size("seq"), lax.axis_size("exp")
    chips = size // CORES
    devices = size * exp_size
    me = lax.axis_index("seq")
    chip, core = me // CORES, me % CORES
    q_cols, kv_cols = q.shape[1] // chips, k.shape[1] // chips
    heads = q.shape[1] // k.shape[1]
    span = tokens * size
    model = out_weight.shape[1]
    cols = model // CHUNKS

    def over(d):
        return [
            (a * CORES + b, ((a + d) % chips) * CORES + b)
            for a in range(chips)
            for b in range(CORES)
        ]

    swap = [(a, a ^ 1) for a in range(size)]

    def cut(x, at, n):
        return lax.dynamic_slice(x, (0, at * n), (x.shape[0], n))

    pair = lambda at: jnp.concatenate([cut(k, at, kv_cols), cut(v, at, kv_cols)], axis=1)
    kv_parts = [pair(chip)]
    q_parts = [q]
    for d in range(1, chips):
        to = (chip + d) % chips
        kv_parts.append(lax.ppermute(pair(to), "seq", over(d)))
        q_parts.append(lax.ppermute(cut(q, to, q_cols), "seq", over(d)))
    mine = jnp.concatenate(kv_parts, axis=0)
    theirs = lax.ppermute(mine, "seq", swap)

    ring = [2 * i for i in range(exp_size // 2)] + [2 * i + 1 for i in reversed(range(exp_size // 2))]
    exp_me = lax.axis_index("exp")
    place = jnp.where(exp_me % 2 == 0, exp_me // 2, exp_size - 1 - exp_me // 2)
    offsets = [0]
    for step in range(1, exp_size // 2):
        offsets += [-step, step]
    offsets.append(exp_size // 2)
    spot = (place + jnp.array(offsets, jnp.int32)) % exp_size
    order = jnp.where(
        spot < exp_size // 2, 2 * spot, 2 * (exp_size - 1 - spot) + 1
    ).astype(jnp.int32)
    w_mine, w_theirs = [], []
    for j in range(CHUNKS):
        got = in_order(order, ring_gather(out_weight[:, j * cols : (j + 1) * cols], ring))
        w_mine.append(got)
        w_theirs.append(lax.ppermute(got, "seq", swap))

    doc_col = doc_ids
    doc_row = doc_ids.reshape(span, 1)
    starts = jnp.sum(
        (doc_ids < doc_ids[0, ::ROW_BLOCK][:, None]).astype(jnp.int32), axis=1
    ) // KEY_BLOCK
    attended = []
    for d in range(chips):
        seats = []
        for a in range(chips):
            seats += [((chip - a) % chips) * CORES + core, ((chip - a) % chips) * CORES + 1 - core]
        scal = jnp.stack([seats[d * CORES], chip if d == 0 else 0 * chip] + seats).astype(jnp.int32)
        attended.append(
            attend(
                scal,
                starts,
                q_parts[d],
                q_cols // (heads * HEAD_DIMENSION),
                heads,
                mine,
                theirs,
                doc_col,
                doc_row,
                chips,
                "own" if d == 0 else "far",
            )
        )

    capacity = 2 * tokens // devices
    slots = Slots(capacity, devices)
    keys = slot_keys(slots, expert_ids[0], slot_ids[0])
    kept = (slot_ids[0] >= 0).astype(jnp.int32).reshape(tokens, 1)
    bias_row = dec_bias[None]
    core_row = core.reshape(1).astype(jnp.int32)
    rows = jnp.zeros((0,), bf16)
    arrived, sums = [], None
    to_all = lambda block: lax.all_to_all(
        block.reshape(devices, 8, block.shape[1]), ("seq", "exp"), 0, 0, tiled=True
    ).reshape(block.shape)
    for j in range(CHUNKS):
        own, *sends = project(core_row, attended, w_mine[j], w_theirs[j])
        received = [
            lax.ppermute(part, "seq", over(chips - d)) for d, part in enumerate(sends, start=1)
        ]
        rows, packed = pack(slots, keys, own, received, rows, j)
        arrived.append(to_all(packed))

    pre = None
    for j in range(CHUNKS):
        last = j == CHUNKS - 1
        pre = encode(slots, arrived[j], bias_row, enc_weight, j, pre, enc_bias if last else None)
    latent = pre
    residues, returned = [], []
    for j in range(CHUNKS):
        rebuilt, residue = decode(slots, latent, dec_weight, bias_row, arrived[j], j)
        residues.append(residue)
        returned.append(to_all(rebuilt))
    dec_grad = decoder_grad(latent, residues)
    outs = ()
    for j in range(CHUNKS):
        outs = finish(slots, keys, kept, returned[j], bias_row, rows, j, outs)
    return (rows[None], outs[0][None], outs[1][None], dec_grad)


def solution(mesh):
    return jax.shard_map(
        shards,
        mesh=mesh,
        in_specs=(
            P("exp", "seq", None),
            P("exp", "seq", None),
            P("exp", "seq", None),
            P("exp", None),
            P(("seq", "exp"), None),
            P(("seq", "exp"), None, None),
            P(("seq", "exp"), None),
            P(("seq", "exp"), None, None),
            P(),
            P("exp", "seq"),
            P("exp", "seq"),
        ),
        out_specs=(
            P("exp", "seq", None),
            P("exp", "seq", None),
            P("exp", "seq", None),
            P(("seq", "exp"), None, None),
        ),
        check_vma=False,
    )
```

time: 293 us -> 231 us (0.79)
  Pallas kernels: 0 us -> 68.5 us
  waiting for transfers between devices: 156 us -> 107 us
  matrix products: 41 us -> 0 us
  local copies, waits for them, and re-layouts: 41.1 us -> 10.4 us
  starting transfers between devices: 21 us -> 39.8 us
  other arithmetic: 18.7 us -> 4.19 us
  between operations: 14.3 us -> 0.91 us
    pallas_call x0 -> x15, Pallas kernels: none -> 68.5 us  [the longest x2 17.1 us: attend(): call(functools.partial(attention_kernel, heads, parts), 'attend_' + tag,...]
    ppermute x0 -> x23, waiting for transfers between devices: none -> 60.4 us  [the longest x6 28.9 us: ring_gather(): bw = lax.ppermute(bw, 'exp', back)]
    all_to_all x5 -> x4, waiting for transfers between devices: 102 us -> 46.3 us  [shards(): lax.all_to_all(block.reshape(devices, 8, block.shape[1]), ('seq', 'exp'),...]
    reduce_scatter x1 -> x0, waiting for transfers between devices: 35.9 us -> none  [shards(): lax.psum_scatter(jnp.dot(attended, own_rows, preferred_element_type=jnp.f...]
    dot_general x5 -> x0, matrix products: 28.8 us -> none  [the longest x1 8.54 us: attend_block(): jnp.einsum('hqk,kd->qhd', normed, value_part, preferred_element_type=jnp....]
    ppermute x0 -> x23, starting transfers between devices: none -> 24.1 us  [the longest x6 10.9 us: ring_gather(): bw = lax.ppermute(bw, 'exp', back)]
    all_gather x1 -> x0, waiting for transfers between devices: 17.3 us -> none  [shards(): own_rows = lax.all_gather(out_weight, 'exp', axis=0, tiled=True)]
    unnamed x25 -> x58, local copies, waits for them, and re-layouts: 18.8 us -> 5.05 us
  transfers between devices with their start and end apart: 7 -> 27, of which waited for: 6 -> 17; matrix products, arithmetic and copies ran while one was open for 25% -> 4% of each run, Pallas kernels for 0% -> 23%
where the time goes in v1:
time: 231 us
  waiting for transfers between devices  107 us (46%)
  Pallas kernels  68.5 us (30%)
  starting transfers between devices  39.8 us (17%)
  local copies, waits for them, and re-layouts  10.4 us (5%)
  other arithmetic  4.19 us (2%)
    all_to_all x4, waiting for transfers between devices, shards(): lax.all_to_all(block.reshape(devices, 8, block.shape[1]), ('seq', 'exp'),...  46.3 us
    ppermute x6, waiting for transfers between devices, ring_gather(): bw = lax.ppermute(bw, 'exp', back)  28.9 us
    ppermute x2, waiting for transfers between devices, shards(): lax.ppermute(part, 'seq', over(chips - d))  23 us
    pallas_call x2, Pallas kernels, attend(): call(functools.partial(attention_kernel, heads, parts), 'attend_' + tag,...  17.1 us
    all_to_all x4, starting transfers between devices, shards(): lax.all_to_all(block.reshape(devices, 8, block.shape[1]), ('seq', 'exp'),...  15.7 us
    ppermute x6, starting transfers between devices, ring_gather(): bw = lax.ppermute(bw, 'exp', back)  10.9 us
    pallas_call x2, Pallas kernels, decode(): call(functools.partial(decode_kernel, slots), 'decode', [jax.ShapeDtypeSt...  9.81 us
    pallas_call x2, Pallas kernels, project(): call(functools.partial(project_kernel, depth), 'project', [jax.ShapeDtype...  9.54 us
  transfers between devices with their start and end apart: 27, of which 17 were waited for; matrix products, arithmetic and copies ran while one was open for 4% of the time, Pallas kernels for 23%

profile of v1, /device:TPU:0, one launch (start us, length us, event | category | flops | bytes accessed | tf_op | source)
XLA Modules:
  0.0 230.7 jit_solution(5641586679552782779)
XLA Ops:
  0.6 1.1 fusion.1
  1.7 3.0 %collective-permute-start.14 = (bf16[128,1024]{1,0:T(8,128)(2,1)S(1)}, bf16[128,1024]{1,0:T(8,128)(2,1)S(1)}, u32[]{:S(2)}, u32[]{:S(2)}) collective-permute-start(bf16[128,1024]{1,0:T(8,128)(2,1)S(1)} %get-tuple-element.36.refs_0_), channel_id=1, source_target_pairs={{0,1},{2,0},{4,2},{6,4},{7,6},{5,7},{3,5},{1,3},{8,9},{10,8},{12,1... | collective-permute-start | bytes 786440 | tf_op jit(solution)/shard_map/ppermute | solution.py:178
  4.9 6.2 %collective-permute-done.14.refs_2_ = bf16[128,1024]{1,0:T(8,128)(2,1)S(1)} collective-permute-done((bf16[128,1024]{1,0:T(8,128)(2,1)S(1)}, bf16[128,1024]{1,0:T(8,128)(2,1)S(1)}, u32[]{:S(2)}, u32[]{:S(2)}) %collective-permute-start.14) | collective-permute-done | bytes 262176 | tf_op jit(solution)/shard_map/ppermute | solution.py:178
  11.1 1.7 collective-permute-start.16
  13.2 5.4 %collective-permute-done.16.refs_4_ = bf16[128,1024]{1,0:T(8,128)(2,1)S(1)} collective-permute-done((bf16[128,1024]{1,0:T(8,128)(2,1)S(1)}, bf16[128,1024]{1,0:T(8,128)(2,1)S(1)}, u32[]{:S(2)}, u32[]{:S(2)}) %collective-permute-start.16) | collective-permute-done | bytes 262176 | tf_op jit(solution)/shard_map/ppermute | solution.py:178
  18.6 1.4 collective-permute-start.18
  20.0 0.6 collective-permute-start.17
  20.6 4.6 %collective-permute-done.18.refs_6_ = bf16[128,1024]{1,0:T(8,128)(2,1)S(1)} collective-permute-done((bf16[128,1024]{1,0:T(8,128)(2,1)S(1)}, bf16[128,1024]{1,0:T(8,128)(2,1)S(1)}, u32[]{:S(2)}, u32[]{:S(2)}) %collective-permute-start.18) | collective-permute-done | bytes 262176 | tf_op jit(solution)/shard_map/ppermute | solution.py:178
  25.2 1.6 collective-permute-start.20
  26.8 0.6 collective-permute-start.19
  27.4 1.2 compare_select_fusion.2.order
  28.6 1.7 collective-permute-done.20.refs_8_
  30.3 1.7 collective-permute-done.19.refs_7_
  32.0 3.0 %in_order.3.refs_2_ = bf16[1024,1024]{1,0:T(8,128)(2,1)} custom-call(s32[8]{0:T(128)} %compare_select_fusion.2.order, bf16[128,1024]{1,0:T(8,128)(2,1)} %copy-done.8, bf16[128,1024]{1,0:T(8,128)(2,1)} %copy-done.21, bf16[128,1024]{1,0:T(8,128)(2,1)} %copy-done.20, bf16[128,1024]{1,0:T(8,128)(2,1)} %copy-done.23, bf16[128,1024]{1,0:T(8,128)(2,1)} %copy-done.22, ...), custom_call_target="tpu_custom_call" | custom-call | bytes 4194304 | tf_op jit(solution)/shard_map/in_order/pallas_call | solution.py:157
  35.0 1.6 collective-permute-start.4
  37.0 6.7 %collective-permute-done.4.refs_2_ = bf16[128,1024]{1,0:T(8,128)(2,1)S(1)} collective-permute-done((bf16[128,1024]{1,0:T(8,128)(2,1)S(1)}, bf16[128,1024]{1,0:T(8,128)(2,1)S(1)}, u32[]{:S(2)}, u32[]{:S(2)}) %collective-permute-start.4) | collective-permute-done | bytes 262176 | tf_op jit(solution)/shard_map/ppermute | solution.py:178
  43.7 1.6 collective-permute-start.6
  45.8 1.6 collective-permute-start.2
  47.4 4.2 %collective-permute-done.6.refs_4_ = bf16[128,1024]{1,0:T(8,128)(2,1)S(1)} collective-permute-done((bf16[128,1024]{1,0:T(8,128)(2,1)S(1)}, bf16[128,1024]{1,0:T(8,128)(2,1)S(1)}, u32[]{:S(2)}, u32[]{:S(2)}) %collective-permute-start.6) | collective-permute-done | bytes 262176 | tf_op jit(solution)/shard_map/ppermute | solution.py:178
  51.6 1.6 collective-permute-start.8
  53.6 1.1 dynamic-slice_bitcast_fusion.3
  54.7 0.7 pad_maximum_fusion.1
  55.4 1.5 collective-permute-start
  56.9 1.7 collective-permute-done.8.refs_6_
  58.6 1.6 collective-permute-start.10
  60.8 2.9 %collective-permute-done.10.refs_8_ = bf16[64,1024]{1,0:T(8,128)(2,1)S(1)} collective-permute-done((bf16[64,1024]{1,0:T(8,128)(2,1)S(1)}, bf16[64,1024]{1,0:T(8,128)(2,1)S(1)}, u32[]{:S(2)}, u32[]{:S(2)}) %collective-permute-start.10) | collective-permute-done | bytes 131104 | tf_op jit(solution)/shard_map/ppermute | solution.py:181
  63.6 1.8 collective-permute-done.9.refs_7_
  65.4 3.0 %in_order.2.refs_2_ = bf16[1024,1024]{1,0:T(8,128)(2,1)} custom-call(s32[8]{0:T(128)} %compare_select_fusion.2.order, bf16[128,1024]{1,0:T(8,128)(2,1)} %copy-done.7, bf16[128,1024]{1,0:T(8,128)(2,1)} %copy-done.17, bf16[128,1024]{1,0:T(8,128)(2,1)} %copy-done.16, bf16[128,1024]{1,0:T(8,128)(2,1)} %copy-done.19, bf16[128,1024]{1,0:T(8,128)(2,1)} %copy-done.18, ...), custom_call_target="tpu_custom_call" | custom-call | bytes 4194304 | tf_op jit(solution)/shard_map/in_order/pallas_call | solution.py:157
  68.8 1.0 pad_maximum_fusion.mine_ref
  70.1 0.7 stack.39.scal
  70.8 0.6 stack.40.scal
  71.4 1.0 copy.23.drow_ref
  73.4 0.8 copy-done.6
  74.1 7.8 %attend_own.1.refs_0_ = bf16[192,2048]{1,0:T(8,128)(2,1)} custom-call(s32[6]{0:T(128)} %stack.39.scal, s32[12]{0:T(128)} %and_select_fusion.2.first, bf16[192,4096]{1,0:T(8,128)(2,1)} %bitcast.38, bf16[384,512]{1,0:T(8,128)(2,1)} %copy-done.3, bf16[384,512]{1,0:T(8,128)(2,1)} %copy-done.6, s32[1,768]{1,0:T(1,128)} %dcol_ref.3, s32[768,1]{1,0:T(8,128)} %copy.23.drow_ref), custom_call_target="tpu_custom_call" | custom-call | flops 603979776 | bytes 3145728 | tf_op jit(solution)/shard_map/attend_own/pallas_call | solution.py:113
  81.9 0.9 copy-done.9
  82.8 9.3 %attend_far.1.refs_1_ = bf16[192,2048]{1,0:T(8,128)(2,1)} custom-call(s32[6]{0:T(128)} %stack.40.scal, s32[12]{0:T(128)} %and_select_fusion.2.first, bf16[192,2048]{1,0:T(8,128)(2,1)} %copy-done.9, bf16[384,512]{1,0:T(8,128)(2,1)} %copy-done.3, bf16[384,512]{1,0:T(8,128)(2,1)} %copy-done.6, s32[1,768]{1,0:T(1,128)} %dcol_ref.3, s32[768,1]{1,0:T(8,128)} %copy.23.drow_ref), custom_call_target="tpu_custom_call" | custom-call | flops 603979776 | bytes 3145728 | tf_op jit(solution)/shard_map/attend_far/pallas_call | solution.py:113
  92.1 4.8 %project.3 = (f32[192,1024]{1,0:T(8,128)}, bf16[192,1024]{1,0:T(8,128)(2,1)}) custom-call(s32[1]{0:T(128)} %bitcast.scal, bf16[192,2048]{1,0:T(8,128)(2,1)} %attend_own.1.refs_0_, bf16[192,2048]{1,0:T(8,128)(2,1)} %attend_far.1.refs_1_, bf16[1024,1024]{1,0:T(8,128)(2,1)} %in_order.3.refs_2_, bf16[1024,1024]{1,0:T(8,128)(2,1)} %collective-permute-done.21.refs_3_), custom_call_target="tpu_custom_call" | custom-call | flops 1610612736 | bytes 5767168 | tf_op jit(solution)/shard_map/project/pallas_call | solution.py:205
  96.9 1.5 collective-permute-start.22
  98.4 0.6 pad_add_fusion.refs_0_.keys_ref
  99.0 10.0 %collective-permute-done.22.refs_2_ = bf16[192,1024]{1,0:T(8,128)(2,1)S(1)} collective-permute-done((bf16[192,1024]{1,0:T(8,128)(2,1)}, bf16[192,1024]{1,0:T(8,128)(2,1)S(1)}, u32[]{:S(2)}, u32[]{:S(2)}) %collective-permute-start.22) | collective-permute-done | bytes 393248 | tf_op jit(solution)/shard_map/ppermute | solution.py:617
  109.0 0.7 copy-done.14
  109.7 2.7 %pack.2 = (bf16[192,2048]{1,0:T(8,128)(2,1)}, bf16[256,1536]{1,0:T(8,128)(2,1)}) custom-call(s32[3,192]{1,0:T(4,128)} %pad_add_fusion.refs_0_.keys_ref, f32[192,1024]{1,0:T(8,128)} %get-tuple-element.22.refs_1_, bf16[192,1024]{1,0:T(8,128)(2,1)} %copy-done.14), custom_call_target="tpu_custom_call" | custom-call | flops 201326592 | bytes 2359296 | tf_op jit(solution)/shard_map/pack/pallas_call | solution.py:301
  112.4 4.6 %all-to-all-start.1 = ((bf16[32,8,1536]{2,1,0:T(8,128)(2,1)}), bf16[32,8,1536]{2,1,0:T(8,128)(2,1)S(1)}, u32[]{:S(2)}, u32[]{:S(2)}) async-start(bf16[32,8,1536]{2,1,0:T(8,128)(2,1)} %bitcast.41), calls=%async_computation.1 | async-start | bytes 1572864 | tf_op jit(solution)/shard_map/all_to_all | solution.py:611
  117.1 4.8 %project.2 = (f32[192,1024]{1,0:T(8,128)}, bf16[192,1024]{1,0:T(8,128)(2,1)}) custom-call(s32[1]{0:T(128)} %bitcast.scal, bf16[192,2048]{1,0:T(8,128)(2,1)} %attend_own.1.refs_0_, bf16[192,2048]{1,0:T(8,128)(2,1)} %attend_far.1.refs_1_, bf16[1024,1024]{1,0:T(8,128)(2,1)} %in_order.2.refs_2_, bf16[1024,1024]{1,0:T(8,128)(2,1)} %collective-permute-done.11.refs_3_), custom_call_target="tpu_custom_call" | custom-call | flops 1610612736 | bytes 5767168 | tf_op jit(solution)/shard_map/project/pallas_call | solution.py:205
  121.8 1.8 collective-permute-start.12
  123.6 13.0 %collective-permute-done.12.refs_2_ = bf16[192,1024]{1,0:T(8,128)(2,1)S(1)} collective-permute-done((bf16[192,1024]{1,0:T(8,128)(2,1)}, bf16[192,1024]{1,0:T(8,128)(2,1)S(1)}, u32[]{:S(2)}, u32[]{:S(2)}) %collective-permute-start.12) | collective-permute-done | bytes 393248 | tf_op jit(solution)/shard_map/ppermute | solution.py:617
  136.6 0.7 copy-done.15
  137.3 2.6 %pack.3 = (bf16[192,2048]{1,0:T(8,128)(2,1)}, bf16[256,1536]{1,0:T(8,128)(2,1)}) custom-call(s32[3,192]{1,0:T(4,128)} %pad_add_fusion.refs_0_.keys_ref, f32[192,1024]{1,0:T(8,128)} %get-tuple-element.20.refs_1_, bf16[192,1024]{1,0:T(8,128)(2,1)} %copy-done.15, bf16[192,2048]{1,0:T(8,128)(2,1)} %get-tuple-element.24.refs_3_), custom_call_target="tpu_custom_call", output_to_operand_aliasing={{0}: (3, {})} | custom-call | flops 201326592 | bytes 2359296 | tf_op jit(solution)/shard_map/pack/pallas_call | solution.py:301
  140.0 5.7 %all-to-all-start = ((bf16[32,8,1536]{2,1,0:T(8,128)(2,1)}), bf16[32,8,1536]{2,1,0:T(8,128)(2,1)S(1)}, u32[]{:S(2)}, u32[]{:S(2)}) async-start(bf16[32,8,1536]{2,1,0:T(8,128)(2,1)} %bitcast.43), calls=%async_computation | async-start | bytes 1572864 | tf_op jit(solution)/shard_map/all_to_all | solution.py:611
  145.6 4.5 %encode.2.refs_0_ = f32[512,1024]{1,0:T(8,128)} custom-call(bf16[256,1536]{1,0:T(8,128)(2,1)} %bitcast.36, f32[1,2048]{1,0:T(1,128)} %bitcast.47, bf16[1,2048,1024]{2,1,0:T(8,128)(2,1)} %w_ref.5), custom_call_target="tpu_custom_call" | custom-call | flops 1073741824 | bytes 4980736 | tf_op jit(solution)/shard_map/encode/pallas_call | solution.py:379
  150.1 17.3 %all-to-all-done = bf16[32,8,1536]{2,1,0:T(8,128)(2,1)S(1)} async-done(((bf16[32,8,1536]{2,1,0:T(8,128)(2,1)}), bf16[32,8,1536]{2,1,0:T(8,128)(2,1)S(1)}, u32[]{:S(2)}, u32[]{:S(2)}) %all-to-all-start) | async-done | bytes 786464 | tf_op jit(solution)/shard_map/all_to_all | solution.py:611
  167.5 0.9 copy-done
  168.4 4.9 %encode.3.latent_ref = bf16[512,1024]{1,0:T(8,128)(2,1)} custom-call(bf16[256,1536]{1,0:T(8,128)(2,1)} %bitcast.34, f32[1,2048]{1,0:T(1,128)} %bitcast.48, bf16[1,2048,1024]{2,1,0:T(8,128)(2,1)} %w_ref.5, f32[512,1024]{1,0:T(8,128)} %encode.2.refs_0_, f32[1,1024]{1,0:T(1,128)} %refs_1_.1), custom_call_target="tpu_custom_call" | custom-call | flops 1073741824 | bytes 4980736 | tf_op jit(solution)/shard_map/encode/pallas_call | solution.py:379
  173.3 4.9 %decode.3 = (bf16[256,1536]{1,0:T(8,128)(2,1)}, bf16[512,1024]{1,0:T(8,128)(2,1)}) custom-call(bf16[512,1024]{1,0:T(8,128)(2,1)} %encode.3.latent_ref, bf16[1,1024,2048]{2,1,0:T(8,128)(2,1)} %w_ref.7, f32[1,2048]{1,0:T(1,128)} %bitcast.49, bf16[256,1536]{1,0:T(8,128)(2,1)} %bitcast.37), custom_call_target="tpu_custom_call" | custom-call | flops 1073741824 | bytes 5767168 | tf_op jit(solution)/shard_map/decode/pallas_call | solution.py:420
  178.2 2.8 %all-to-all-start.3 = ((bf16[32,8,1536]{2,1,0:T(8,128)(2,1)}), bf16[32,8,1536]{2,1,0:T(8,128)(2,1)S(1)}, u32[]{:S(2)}, u32[]{:S(2)}) async-start(bf16[32,8,1536]{2,1,0:T(8,128)(2,1)} %bitcast.44), calls=%async_computation.3 | async-start | bytes 1572864 | tf_op jit(solution)/shard_map/all_to_all | solution.py:611
  181.0 4.9 %decode.2 = (bf16[256,1536]{1,0:T(8,128)(2,1)}, bf16[512,1024]{1,0:T(8,128)(2,1)}) custom-call(bf16[512,1024]{1,0:T(8,128)(2,1)} %encode.3.latent_ref, bf16[1,1024,2048]{2,1,0:T(8,128)(2,1)} %w_ref.7, f32[1,2048]{1,0:T(1,128)} %bitcast.50, bf16[256,1536]{1,0:T(8,128)(2,1)} %bitcast.35), custom_call_target="tpu_custom_call" | custom-call | flops 1073741824 | bytes 5767168 | tf_op jit(solution)/shard_map/decode/pallas_call | solution.py:420
  185.9 16.7 %all-to-all-done.3 = bf16[32,8,1536]{2,1,0:T(8,128)(2,1)S(1)} async-done(((bf16[32,8,1536]{2,1,0:T(8,128)(2,1)}), bf16[32,8,1536]{2,1,0:T(8,128)(2,1)S(1)}, u32[]{:S(2)}, u32[]{:S(2)}) %all-to-all-start.3) | async-done | bytes 786464 | tf_op jit(solution)/shard_map/all_to_all | solution.py:611
  202.7 2.6 %all-to-all-start.2 = ((bf16[32,8,1536]{2,1,0:T(8,128)(2,1)}), bf16[32,8,1536]{2,1,0:T(8,128)(2,1)S(1)}, u32[]{:S(2)}, u32[]{:S(2)}) async-start(bf16[32,8,1536]{2,1,0:T(8,128)(2,1)} %bitcast.42), calls=%async_computation.2 | async-start | bytes 1572864 | tf_op jit(solution)/shard_map/all_to_all | solution.py:611
  205.3 0.8 copy.26.kept_ref
  206.1 6.2 %decoder_grad.1 = bf16[1,1024,2048]{2,1,0:T(8,128)(2,1)} custom-call(bf16[512,1024]{1,0:T(8,128)(2,1)} %encode.3.latent_ref, bf16[512,1024]{1,0:T(8,128)(2,1)} %get-tuple-element.34.refs_0_, bf16[512,1024]{1,0:T(8,128)(2,1)} %get-tuple-element.35.refs_1_), custom_call_target="tpu_custom_call" | custom-call | flops 2147483648 | bytes 7340032 | tf_op jit(solution)/shard_map/decoder_grad/pallas_call | solution.py:454
  212.2 2.6 %finish.2 = (bf16[192,2048]{1,0:T(8,128)(2,1)}, bf16[192,2048]{1,0:T(8,128)(2,1)}) custom-call(s32[3,192]{1,0:T(4,128)} %pad_add_fusion.refs_0_.keys_ref, s32[192,1]{1,0:T(8,128)} %copy.26.kept_ref, bf16[256,1536]{1,0:T(8,128)(2,1)} %bitcast.39, f32[1,2048]{1,0:T(1,128)} %bitcast.51, bf16[192,2048]{1,0:T(8,128)(2,1)} %get-tuple-element.25.rows_ref), custom_call_target="tpu_custom_call" | custom-call | flops 201326592 | bytes 1966080 | tf_op jit(solution)/shard_map/finish/pallas_call | solution.py:498
  214.9 12.3 %all-to-all-done.2 = bf16[32,8,1536]{2,1,0:T(8,128)(2,1)S(1)} async-done(((bf16[32,8,1536]{2,1,0:T(8,128)(2,1)}), bf16[32,8,1536]{2,1,0:T(8,128)(2,1)S(1)}, u32[]{:S(2)}, u32[]{:S(2)}) %all-to-all-start.2) | async-done | bytes 786464 | tf_op jit(solution)/shard_map/all_to_all | solution.py:611
  227.1 0.9 copy-done.5
  228.1 2.6 %finish.3 = (bf16[192,2048]{1,0:T(8,128)(2,1)}, bf16[192,2048]{1,0:T(8,128)(2,1)}) custom-call(s32[3,192]{1,0:T(4,128)} %pad_add_fusion.refs_0_.keys_ref, s32[192,1]{1,0:T(8,128)} %copy.26.kept_ref, bf16[256,1536]{1,0:T(8,128)(2,1)} %bitcast.40, f32[1,2048]{1,0:T(1,128)} %bitcast.52, ...), custom_call_target="tpu_custom_call", output_to_operand_aliasing={{0}: (5, {}), {1}: (6, {})} | custom-call | flops 201326592 | bytes 1966080 | tf_op jit(solution)/shard_map/finish/pallas_call | solution.py:498
  (84 shorter events, 4.2 us)
Async XLA Ops:
  1.7 30.3 %copy-start.8 = (bf16[128,1024]{1,0:T(8,128)(2,1)}, bf16[128,1024]{1,0:T(8,128)(2,1)S(1)}, u32[]{:S(2)}) copy-start(bf16[128,1024]{1,0:T(8,128)(2,1)S(1)} %get-tuple-element.36.refs_0_) | copy-start | bytes 786436
  1.7 34.9 %copy-start.7 = (bf16[128,1024]{1,0:T(8,128)(2,1)}, bf16[128,1024]{1,0:T(8,128)(2,1)S(1)}, u32[]{:S(2)}) copy-start(bf16[128,1024]{1,0:T(8,128)(2,1)S(1)} %get-tuple-element.37.refs_0_) | copy-start | bytes 786436
  1.7 9.4 %collective-permute-start.14 = (bf16[128,1024]{1,0:T(8,128)(2,1)S(1)}, bf16[128,1024]{1,0:T(8,128)(2,1)S(1)}, u32[]{:S(2)}, u32[]{:S(2)}) collective-permute-start(bf16[128,1024]{1,0:T(8,128)(2,1)S(1)} %get-tuple-element.36.refs_0_), channel_id=1, source_target_pairs={{0,1},{2,0},{4,2},{6,4},{7,6},{5,7},{3,5},{1,3},{8,9},{10,8},{12,1... | collective-permute-start | bytes 786440 | tf_op jit(solution)/shard_map/ppermute | solution.py:178
  4.8 8.1 %collective-permute-start.13 = (bf16[128,1024]{1,0:T(8,128)(2,1)S(1)}, bf16[128,1024]{1,0:T(8,128)(2,1)S(1)}, u32[]{:S(2)}, u32[]{:S(2)}) collective-permute-start(bf16[128,1024]{1,0:T(8,128)(2,1)S(1)} %get-tuple-element.36.refs_0_), channel_id=1, source_target_pairs={{0,2},{2,4},{4,6},{6,7},{7,5},{5,3},{3,1},{1,0},{8,10},{10,12},{12... | collective-permute-start | bytes 786440 | tf_op jit(solution)/shard_map/ppermute | solution.py:177
  11.1 20.8 %copy-start.20 = (bf16[128,1024]{1,0:T(8,128)(2,1)}, bf16[128,1024]{1,0:T(8,128)(2,1)S(1)}, u32[]{:S(2)}) copy-start(bf16[128,1024]{1,0:T(8,128)(2,1)S(1)} %collective-permute-done.14.refs_2_) | copy-start | bytes 786436
  11.1 7.5 %collective-permute-start.16 = (bf16[128,1024]{1,0:T(8,128)(2,1)S(1)}, bf16[128,1024]{1,0:T(8,128)(2,1)S(1)}, u32[]{:S(2)}, u32[]{:S(2)}) collective-permute-start(bf16[128,1024]{1,0:T(8,128)(2,1)S(1)} %collective-permute-done.14.refs_2_), channel_id=1, source_target_pairs={{0,1},{2,0},{4,2},{6,4},{7,6},{5,7},{3,5},{1,3},{8,9},{10,8},{12,1... | collective-permute-start | bytes 786440 | tf_op jit(solution)/shard_map/ppermute | solution.py:178
  12.8 19.1 %copy-start.21 = (bf16[128,1024]{1,0:T(8,128)(2,1)}, bf16[128,1024]{1,0:T(8,128)(2,1)S(1)}, u32[]{:S(2)}) copy-start(bf16[128,1024]{1,0:T(8,128)(2,1)S(1)} %collective-permute-done.13.refs_1_) | copy-start | bytes 786436
  12.8 7.2 %collective-permute-start.15 = (bf16[128,1024]{1,0:T(8,128)(2,1)S(1)}, bf16[128,1024]{1,0:T(8,128)(2,1)S(1)}, u32[]{:S(2)}, u32[]{:S(2)}) collective-permute-start(bf16[128,1024]{1,0:T(8,128)(2,1)S(1)} %collective-permute-done.13.refs_1_), channel_id=1, source_target_pairs={{0,2},{2,4},{4,6},{6,7},{7,5},{5,3},{3,1},{1,0},{8,10},{10,12},{12... | collective-permute-start | bytes 786440 | tf_op jit(solution)/shard_map/ppermute | solution.py:177
  18.6 13.4 %copy-start.22 = (bf16[128,1024]{1,0:T(8,128)(2,1)}, bf16[128,1024]{1,0:T(8,128)(2,1)S(1)}, u32[]{:S(2)}) copy-start(bf16[128,1024]{1,0:T(8,128)(2,1)S(1)} %collective-permute-done.16.refs_4_) | copy-start | bytes 786436
  18.6 6.6 %collective-permute-start.18 = (bf16[128,1024]{1,0:T(8,128)(2,1)S(1)}, bf16[128,1024]{1,0:T(8,128)(2,1)S(1)}, u32[]{:S(2)}, u32[]{:S(2)}) collective-permute-start(bf16[128,1024]{1,0:T(8,128)(2,1)S(1)} %collective-permute-done.16.refs_4_), channel_id=1, source_target_pairs={{0,1},{2,0},{4,2},{6,4},{7,6},{5,7},{3,5},{1,3},{8,9},{10,8},{12,1... | collective-permute-start | bytes 786440 | tf_op jit(solution)/shard_map/ppermute | solution.py:178
  20.0 7.4 %copy-start.23 = (bf16[128,1024]{1,0:T(8,128)(2,1)}, bf16[128,1024]{1,0:T(8,128)(2,1)S(1)}, u32[]{:S(2)}) copy-start(bf16[128,1024]{1,0:T(8,128)(2,1)S(1)} %collective-permute-done.15.refs_3_) | copy-start | bytes 786436
  20.0 6.8 %collective-permute-start.17 = (bf16[128,1024]{1,0:T(8,128)(2,1)S(1)}, bf16[128,1024]{1,0:T(8,128)(2,1)S(1)}, u32[]{:S(2)}, u32[]{:S(2)}) collective-permute-start(bf16[128,1024]{1,0:T(8,128)(2,1)S(1)} %collective-permute-done.15.refs_3_), channel_id=1, source_target_pairs={{0,2},{2,4},{4,6},{6,7},{7,5},{5,3},{3,1},{1,0},{8,10},{10,12},{12... | collective-permute-start | bytes 786440 | tf_op jit(solution)/shard_map/ppermute | solution.py:177
  25.2 6.8 %copy-start.10 = (bf16[128,1024]{1,0:T(8,128)(2,1)}, bf16[128,1024]{1,0:T(8,128)(2,1)S(1)}, u32[]{:S(2)}) copy-start(bf16[128,1024]{1,0:T(8,128)(2,1)S(1)} %collective-permute-done.18.refs_6_) | copy-start | bytes 786436
  25.2 5.0 %collective-permute-start.20 = (bf16[64,1024]{1,0:T(8,128)(2,1)S(1)}, bf16[64,1024]{1,0:T(8,128)(2,1)S(1)}, u32[]{:S(2)}, u32[]{:S(2)}) collective-permute-start(bf16[64,1024]{1,0:T(8,128)(2,1)S(1)} %slice.31), channel_id=1, source_target_pairs={{0,1},{2,0},{4,2},{6,4},{7,6},{5,7},{3,5},{1,3},{8,9},{10,8},{12,1... | collective-permute-start | bytes 393224 | tf_op jit(solution)/shard_map/ppermute | solution.py:181
  26.8 5.2 %copy-start.11 = (bf16[128,1024]{1,0:T(8,128)(2,1)}, bf16[128,1024]{1,0:T(8,128)(2,1)S(1)}, u32[]{:S(2)}) copy-start(bf16[128,1024]{1,0:T(8,128)(2,1)S(1)} %collective-permute-done.17.refs_5_) | copy-start | bytes 786436
  26.8 5.1 %collective-permute-start.19 = (bf16[64,1024]{1,0:T(8,128)(2,1)S(1)}, bf16[64,1024]{1,0:T(8,128)(2,1)}, u32[]{:S(2)}, u32[]{:S(2)}) collective-permute-start(bf16[64,1024]{1,0:T(8,128)(2,1)S(1)} %slice.30), channel_id=1, source_target_pairs={{0,2},{2,4},{4,6},{6,7},{7,5},{5,3},{3,1},{1,0},{8,10},{10,12},{12... | collective-permute-start | bytes 393224 | tf_op jit(solution)/shard_map/ppermute | solution.py:180
  28.6 17.2 %copy-start.2 = (bf16[1,192,4096]{2,1,0:T(8,128)(2,1)S(1)}, bf16[1,192,4096]{2,1,0:T(8,128)(2,1)}, u32[]{:S(2)}) copy-start(bf16[1,192,4096]{2,1,0:T(8,128)(2,1)} %param.12) | copy-start | bytes 4718596
  30.3 1.7 copy-start.24
  35.0 57.1 %collective-permute-start.21 = (bf16[1024,1024]{1,0:T(8,128)(2,1)}, bf16[1024,1024]{1,0:T(8,128)(2,1)}, u32[]{:S(2)}, u32[]{:S(2)}) collective-permute-start(bf16[1024,1024]{1,0:T(8,128)(2,1)} %in_order.3.refs_2_), channel_id=1, source_target_pairs={{0,8},{8,0},{16,24},{24,16},{1,9},{9,1},{17,25},{25,17},{2,10},{10... | collective-permute-start | bytes 6291464 | tf_op jit(solution)/shard_map/ppermute | solution.py:574
  35.0 8.7 %collective-permute-start.4 = (bf16[128,1024]{1,0:T(8,128)(2,1)S(1)}, bf16[128,1024]{1,0:T(8,128)(2,1)S(1)}, u32[]{:S(2)}, u32[]{:S(2)}) collective-permute-start(bf16[128,1024]{1,0:T(8,128)(2,1)S(1)} %get-tuple-element.37.refs_0_), channel_id=1, source_target_pairs={{0,1},{2,0},{4,2},{6,4},{7,6},{5,7},{3,5},{1,3},{8,9},{10,8},{12,1... | collective-permute-start | bytes 786440 | tf_op jit(solution)/shard_map/ppermute | solution.py:178
  36.6 8.7 %collective-permute-start.3 = (bf16[128,1024]{1,0:T(8,128)(2,1)S(1)}, bf16[128,1024]{1,0:T(8,128)(2,1)S(1)}, u32[]{:S(2)}, u32[]{:S(2)}) collective-permute-start(bf16[128,1024]{1,0:T(8,128)(2,1)S(1)} %get-tuple-element.37.refs_0_), channel_id=1, source_target_pairs={{0,2},{2,4},{4,6},{6,7},{7,5},{5,3},{3,1},{1,0},{8,10},{10,12},{12... | collective-permute-start | bytes 786440 | tf_op jit(solution)/shard_map/ppermute | solution.py:177
  43.7 21.7 %copy-start.16 = (bf16[128,1024]{1,0:T(8,128)(2,1)}, bf16[128,1024]{1,0:T(8,128)(2,1)S(1)}, u32[]{:S(2)}) copy-start(bf16[128,1024]{1,0:T(8,128)(2,1)S(1)} %collective-permute-done.4.refs_2_) | copy-start | bytes 786436
  43.7 7.9 %collective-permute-start.6 = (bf16[128,1024]{1,0:T(8,128)(2,1)S(1)}, bf16[128,1024]{1,0:T(8,128)(2,1)S(1)}, u32[]{:S(2)}, u32[]{:S(2)}) collective-permute-start(bf16[128,1024]{1,0:T(8,128)(2,1)S(1)} %collective-permute-done.4.refs_2_), channel_id=1, source_target_pairs={{0,1},{2,0},{4,2},{6,4},{7,6},{5,7},{3,5},{1,3},{8,9},{10,8},{12,1... | collective-permute-start | bytes 786440 | tf_op jit(solution)/shard_map/ppermute | solution.py:178
  45.3 20.1 %copy-start.17 = (bf16[128,1024]{1,0:T(8,128)(2,1)}, bf16[128,1024]{1,0:T(8,128)(2,1)S(1)}, u32[]{:S(2)}) copy-start(bf16[128,1024]{1,0:T(8,128)(2,1)S(1)} %collective-permute-done.3.refs_1_) | copy-start | bytes 786436
  45.3 7.9 %collective-permute-start.5 = (bf16[128,1024]{1,0:T(8,128)(2,1)S(1)}, bf16[128,1024]{1,0:T(8,128)(2,1)S(1)}, u32[]{:S(2)}, u32[]{:S(2)}) collective-permute-start(bf16[128,1024]{1,0:T(8,128)(2,1)S(1)} %collective-permute-done.3.refs_1_), channel_id=1, source_target_pairs={{0,2},{2,4},{4,6},{6,7},{7,5},{5,3},{3,1},{1,0},{8,10},{10,12},{12... | collective-permute-start | bytes 786440 | tf_op jit(solution)/shard_map/ppermute | solution.py:177
  45.8 36.1 %collective-permute-start.2 = (bf16[192,2048]{1,0:T(8,128)(2,1)S(1)}, bf16[192,2048]{1,0:T(8,128)(2,1)S(1)}, u32[]{:S(2)}, u32[]{:S(2)}) collective-permute-start(bf16[192,2048]{1,0:T(8,128)(2,1)S(1)} %dynamic-slice_bitcast_fusion), channel_id=1, source_target_pairs={{0,16},{8,24},{16,0},{24,8},{1,17},{9,25},{17,1},{25,9},{2,18},{10... | collective-permute-start | bytes 2359304 | tf_op jit(solution)/shard_map/ppermute | solution.py:555
  51.6 13.8 %copy-start.18 = (bf16[128,1024]{1,0:T(8,128)(2,1)}, bf16[128,1024]{1,0:T(8,128)(2,1)S(1)}, u32[]{:S(2)}) copy-start(bf16[128,1024]{1,0:T(8,128)(2,1)S(1)} %collective-permute-done.6.refs_4_) | copy-start | bytes 786436
  51.6 7.0 %collective-permute-start.8 = (bf16[128,1024]{1,0:T(8,128)(2,1)S(1)}, bf16[128,1024]{1,0:T(8,128)(2,1)S(1)}, u32[]{:S(2)}, u32[]{:S(2)}) collective-permute-start(bf16[128,1024]{1,0:T(8,128)(2,1)S(1)} %collective-permute-done.6.refs_4_), channel_id=1, source_target_pairs={{0,1},{2,0},{4,2},{6,4},{7,6},{5,7},{3,5},{1,3},{8,9},{10,8},{12,1... | collective-permute-start | bytes 786440 | tf_op jit(solution)/shard_map/ppermute | solution.py:178
  53.2 12.2 %copy-start.19 = (bf16[128,1024]{1,0:T(8,128)(2,1)}, bf16[128,1024]{1,0:T(8,128)(2,1)S(1)}, u32[]{:S(2)}) copy-start(bf16[128,1024]{1,0:T(8,128)(2,1)S(1)} %collective-permute-done.5.refs_3_) | copy-start | bytes 786436
  53.2 7.1 %collective-permute-start.7 = (bf16[128,1024]{1,0:T(8,128)(2,1)S(1)}, bf16[128,1024]{1,0:T(8,128)(2,1)S(1)}, u32[]{:S(2)}, u32[]{:S(2)}) collective-permute-start(bf16[128,1024]{1,0:T(8,128)(2,1)S(1)} %collective-permute-done.5.refs_3_), channel_id=1, source_target_pairs={{0,2},{2,4},{4,6},{6,7},{7,5},{5,3},{3,1},{1,0},{8,10},{10,12},{12... | collective-permute-start | bytes 786440 | tf_op jit(solution)/shard_map/ppermute | solution.py:177
  55.4 13.4 %collective-permute-start = (bf16[192,512]{1,0:T(8,128)(2,1)}, bf16[192,512]{1,0:T(8,128)(2,1)}, u32[]{:S(2)}, u32[]{:S(2)}) collective-permute-start(bf16[192,512]{1,0:T(8,128)(2,1)} %pad_maximum_fusion.1), channel_id=1, source_target_pairs={{0,16},{8,24},{16,0},{24,8},{1,17},{9,25},{17,1},{25,9},{2,18},{10... | collective-permute-start | bytes 589832 | tf_op jit(solution)/shard_map/ppermute | solution.py:554
  58.6 6.8 %copy-start.12 = (bf16[128,1024]{1,0:T(8,128)(2,1)}, bf16[128,1024]{1,0:T(8,128)(2,1)S(1)}, u32[]{:S(2)}) copy-start(bf16[128,1024]{1,0:T(8,128)(2,1)S(1)} %collective-permute-done.8.refs_6_) | copy-start | bytes 786436
  58.6 5.0 %collective-permute-start.10 = (bf16[64,1024]{1,0:T(8,128)(2,1)S(1)}, bf16[64,1024]{1,0:T(8,128)(2,1)S(1)}, u32[]{:S(2)}, u32[]{:S(2)}) collective-permute-start(bf16[64,1024]{1,0:T(8,128)(2,1)S(1)} %slice.29), channel_id=1, source_target_pairs={{0,1},{2,0},{4,2},{6,4},{7,6},{5,7},{3,5},{1,3},{8,9},{10,8},{12,1... | collective-permute-start | bytes 393224 | tf_op jit(solution)/shard_map/ppermute | solution.py:181
  60.2 5.2 %copy-start.13 = (bf16[128,1024]{1,0:T(8,128)(2,1)}, bf16[128,1024]{1,0:T(8,128)(2,1)S(1)}, u32[]{:S(2)}) copy-start(bf16[128,1024]{1,0:T(8,128)(2,1)S(1)} %collective-permute-done.7.refs_5_) | copy-start | bytes 786436
  60.3 9.7 %copy-start.26 = (s32[1,768]{1,0:T(1,128)S(1)}, s32[1,768]{1,0:T(1,128)}, u32[]{:S(2)}) copy-start(s32[1,768]{1,0:T(1,128)} %dcol_ref.3) | copy-start | bytes 9220
  60.3 5.1 %collective-permute-start.9 = (bf16[64,1024]{1,0:T(8,128)(2,1)S(1)}, bf16[64,1024]{1,0:T(8,128)(2,1)}, u32[]{:S(2)}, u32[]{:S(2)}) collective-permute-start(bf16[64,1024]{1,0:T(8,128)(2,1)S(1)} %slice.28), channel_id=1, source_target_pairs={{0,2},{2,4},{4,6},{6,7},{7,5},{5,3},{3,1},{1,0},{8,10},{10,12},{12... | collective-permute-start | bytes 393224 | tf_op jit(solution)/shard_map/ppermute | solution.py:180
  63.6 1.8 copy-start.25
  68.4 48.6 %collective-permute-start.11 = (bf16[1024,1024]{1,0:T(8,128)(2,1)}, bf16[1024,1024]{1,0:T(8,128)(2,1)}, u32[]{:S(2)}, u32[]{:S(2)}) collective-permute-start(bf16[1024,1024]{1,0:T(8,128)(2,1)} %in_order.2.refs_2_), channel_id=1, source_target_pairs={{0,8},{8,0},{16,24},{24,16},{1,9},{9,1},{17,25},{25,17},{2,10},{10... | collective-permute-start | bytes 6291464 | tf_op jit(solution)/shard_map/ppermute | solution.py:574
  69.7 3.6 %copy-start.3 = (bf16[384,512]{1,0:T(8,128)(2,1)}, bf16[384,512]{1,0:T(8,128)(2,1)S(1)}, u32[]{:S(2)}) copy-start(bf16[384,512]{1,0:T(8,128)(2,1)S(1)} %pad_maximum_fusion.mine_ref) | copy-start | bytes 1179652
  69.7 3.6 %collective-permute-start.1 = (bf16[384,512]{1,0:T(8,128)(2,1)S(1)}, bf16[384,512]{1,0:T(8,128)(2,1)S(1)}, u32[]{:S(2)}, u32[]{:S(2)}) collective-permute-start(bf16[384,512]{1,0:T(8,128)(2,1)S(1)} %pad_maximum_fusion.mine_ref), channel_id=1, source_target_pairs={{0,8},{8,0},{16,24},{24,16},{1,9},{9,1},{17,25},{25,17},{2,10},{10... | collective-permute-start | bytes 1179656 | tf_op jit(solution)/shard_map/ppermute | solution.py:557
  73.3 0.8 copy-start.6
  81.9 0.9 copy-start.9
  92.1 6.3 %copy-start.27 = (s32[1,192]{1,0:T(1,128)S(1)}, s32[1,192]{1,0:T(1,128)}, u32[]{:S(2)}) copy-start(s32[1,192]{1,0:T(1,128)} %param.22) | copy-start | bytes 2308
  92.1 6.3 %copy-start.28 = (s32[1,192]{1,0:T(1,128)S(1)}, s32[1,192]{1,0:T(1,128)}, u32[]{:S(2)}) copy-start(s32[1,192]{1,0:T(1,128)} %param.21) | copy-start | bytes 2308
  96.9 12.1 %collective-permute-start.22 = (bf16[192,1024]{1,0:T(8,128)(2,1)}, bf16[192,1024]{1,0:T(8,128)(2,1)S(1)}, u32[]{:S(2)}, u32[]{:S(2)}) collective-permute-start(bf16[192,1024]{1,0:T(8,128)(2,1)} %get-tuple-element.23), channel_id=1, source_target_pairs={{0,16},{8,24},{16,0},{24,8},{1,17},{9,25},{17,1},{25,9},{2,18},{10... | collective-permute-start | bytes 1179656 | tf_op jit(solution)/shard_map/ppermute | solution.py:617
  109.0 0.7 copy-start.14
  112.4 27.5 %all-to-all-start.1 = ((bf16[32,8,1536]{2,1,0:T(8,128)(2,1)}), bf16[32,8,1536]{2,1,0:T(8,128)(2,1)S(1)}, u32[]{:S(2)}, u32[]{:S(2)}) async-start(bf16[32,8,1536]{2,1,0:T(8,128)(2,1)} %bitcast.41), calls=%async_computation.1 | async-start | bytes 1572864 | tf_op jit(solution)/shard_map/all_to_all | solution.py:611
  121.8 14.7 %collective-permute-start.12 = (bf16[192,1024]{1,0:T(8,128)(2,1)}, bf16[192,1024]{1,0:T(8,128)(2,1)S(1)}, u32[]{:S(2)}, u32[]{:S(2)}) collective-permute-start(bf16[192,1024]{1,0:T(8,128)(2,1)} %get-tuple-element.21), channel_id=1, source_target_pairs={{0,16},{8,24},{16,0},{24,8},{1,17},{9,25},{17,1},{25,9},{2,18},{10... | collective-permute-start | bytes 1179656 | tf_op jit(solution)/shard_map/ppermute | solution.py:617
  136.6 0.7 copy-start.15
  140.0 5.7 %copy-start.1 = (bf16[32,8,1536]{2,1,0:T(8,128)(2,1)}, bf16[32,8,1536]{2,1,0:T(8,128)(2,1)S(1)}, u32[]{:S(2)}) copy-start(bf16[32,8,1536]{2,1,0:T(8,128)(2,1)S(1)} %all-to-all-done.1) | copy-start | bytes 2359300
  140.0 27.5 %all-to-all-start = ((bf16[32,8,1536]{2,1,0:T(8,128)(2,1)}), bf16[32,8,1536]{2,1,0:T(8,128)(2,1)S(1)}, u32[]{:S(2)}, u32[]{:S(2)}) async-start(bf16[32,8,1536]{2,1,0:T(8,128)(2,1)} %bitcast.43), calls=%async_computation | async-start | bytes 1572864 | tf_op jit(solution)/shard_map/all_to_all | solution.py:611
  167.5 0.9 copy-start
  178.2 24.5 %all-to-all-start.3 = ((bf16[32,8,1536]{2,1,0:T(8,128)(2,1)}), bf16[32,8,1536]{2,1,0:T(8,128)(2,1)S(1)}, u32[]{:S(2)}, u32[]{:S(2)}) async-start(bf16[32,8,1536]{2,1,0:T(8,128)(2,1)} %bitcast.44), calls=%async_computation.3 | async-start | bytes 1572864 | tf_op jit(solution)/shard_map/all_to_all | solution.py:611
  202.6 9.6 %copy-start.4 = (bf16[32,8,1536]{2,1,0:T(8,128)(2,1)}, bf16[32,8,1536]{2,1,0:T(8,128)(2,1)S(1)}, u32[]{:S(2)}) copy-start(bf16[32,8,1536]{2,1,0:T(8,128)(2,1)S(1)} %all-to-all-done.3) | copy-start | bytes 2359300
  202.7 24.5 %all-to-all-start.2 = ((bf16[32,8,1536]{2,1,0:T(8,128)(2,1)}), bf16[32,8,1536]{2,1,0:T(8,128)(2,1)S(1)}, u32[]{:S(2)}, u32[]{:S(2)}) async-start(bf16[32,8,1536]{2,1,0:T(8,128)(2,1)} %bitcast.42), calls=%async_computation.2 | async-start | bytes 1572864 | tf_op jit(solution)/shard_map/all_to_all | solution.py:611
  227.1 0.9 copy-start.5

commit v2 on v0

v2 whole, which is shorter than its diff:
```python
import functools
import math

import jax
import jax.numpy as jnp
from jax import lax
from jax.experimental import pallas as pl
from jax.experimental.pallas import tpu as pltpu
from jax.sharding import PartitionSpec as P


HEAD_DIMENSION = 128
CORES = 2
KEY_BLOCK = 256
KEY_STEP = 128
ROW_BLOCK = 64
EMPTY = 1e30
MASKED = -1e30
CHUNKS = 2
LIMIT = 20 * 2**20
ALMOST_ALL = 61_400_000
VMEM, SMEM, ANY, HBM = pltpu.VMEM, pltpu.SMEM, pl.ANY, pltpu.HBM
TILES = 4

bf16 = jnp.bfloat16
f32 = jnp.float32


def call(kernel, out_shape, flops, moved, ins, outs, scratch=(), alias={}, limit=None):
    spec = lambda space: pl.BlockSpec(memory_space=space)
    return pl.pallas_call(
        kernel,
        out_shape=out_shape,
        in_specs=[spec(s) for s in ins],
        out_specs=jax.tree.map(spec, outs),
        scratch_shapes=list(scratch),
        input_output_aliases=alias,
        cost_estimate=pl.CostEstimate(flops=int(flops), bytes_accessed=int(moved), transcendentals=0),
        compiler_params=pltpu.CompilerParams(vmem_limit_bytes=limit or LIMIT),
    )


def dot(a, b, dims=((1,), (0,))):
    return lax.dot_general(a, b, (dims, ((), ())), preferred_element_type=f32)


def attention_kernel(
    heads, parts, group, scal, first, q_ref, mine_ref, theirs_ref, dcol_ref, drow_ref, o_ref,
    k_scr, v_scr, m_scr, l_scr, a_scr,
):
    tokens = q_ref.shape[0]
    hd = HEAD_DIMENSION
    width = mine_ref.shape[1] // 2
    span = parts * CORES * tokens
    key_at = slice(group * hd, (group + 1) * hd)
    value_at = slice(width + group * hd, width + (group + 1) * hd)
    for d in range(parts):
        for which, ref in enumerate((mine_ref, theirs_ref)):
            at = pl.multiple_of(scal[2 + d * CORES + which] * tokens, tokens)
            k_scr[pl.ds(at, tokens), :] = ref[d * tokens : (d + 1) * tokens, key_at]
            v_scr[pl.ds(at, tokens), :] = ref[d * tokens : (d + 1) * tokens, value_at]
    k_scr[span:, :] = jnp.zeros((KEY_BLOCK, hd), bf16)
    v_scr[span:, :] = jnp.zeros((KEY_BLOCK, hd), bf16)

    base = scal[0] * tokens
    scale = math.log2(math.e) / math.sqrt(hd)
    rows = heads * ROW_BLOCK
    blocks = tokens // ROW_BLOCK
    lane_pos = lax.broadcasted_iota(jnp.int32, (ROW_BLOCK, KEY_BLOCK), 1)
    row_in = lax.broadcasted_iota(jnp.int32, (ROW_BLOCK, KEY_BLOCK), 0)

    def queries(i):
        at = slice(i * ROW_BLOCK, (i + 1) * ROW_BLOCK)
        lane = [pl.multiple_of(scal[1] + (group * heads + h) * hd, hd) for h in range(heads)]
        return jnp.concatenate([q_ref[at, pl.ds(n, hd)] for n in lane], axis=0)

    def scores(i, q, col):
        col = pl.multiple_of(col, KEY_STEP)
        here = pl.multiple_of(base + i * ROW_BLOCK, ROW_BLOCK)
        s = dot(q, k_scr[pl.ds(col, KEY_BLOCK), :], ((1,), (1,))) * scale
        visible = (row_in + here >= lane_pos + col) & (
            drow_ref[pl.ds(here, ROW_BLOCK), :] == dcol_ref[:, pl.ds(col, KEY_BLOCK)]
        )
        s = jnp.where(visible[None], s.reshape(heads, ROW_BLOCK, KEY_BLOCK), MASKED)
        return s.reshape(rows, KEY_BLOCK)

    def values(col):
        return v_scr[pl.ds(pl.multiple_of(col, KEY_STEP), KEY_BLOCK), :]

    starts = [first[scal[0] * blocks + i] * KEY_STEP for i in range(blocks)]
    for i in range(blocks):
        s = scores(i, queries(i), starts[i])
        top = jnp.max(s, axis=1, keepdims=True)
        p = jnp.exp2(s - top)
        m_scr[i] = top
        l_scr[i] = jnp.sum(p, axis=1, keepdims=True)
        a_scr[i] = dot(p.astype(bf16), values(starts[i]))

    for i in range(blocks):
        trips = (base + (i + 1) * ROW_BLOCK - starts[i] + KEY_BLOCK - 1) // KEY_BLOCK

        def more(j, carry):
            col = starts[i] + j * KEY_BLOCK
            s = scores(i, queries(i), col)
            old = m_scr[i]
            top = jnp.maximum(old, jnp.max(s, axis=1, keepdims=True))
            p = jnp.exp2(s - top)
            fade = jnp.exp2(old - top)
            m_scr[i] = top
            l_scr[i] = l_scr[i] * fade + jnp.sum(p, axis=1, keepdims=True)
            a_scr[i] = a_scr[i] * fade + dot(p.astype(bf16), values(col))
            return carry

        lax.fori_loop(1, trips, more, 0)

    for i in range(blocks):
        out = (a_scr[i] * (1.0 / l_scr[i])).astype(bf16)
        for h in range(heads):
            o_ref[i * ROW_BLOCK : (i + 1) * ROW_BLOCK, h * hd : (h + 1) * hd] = out[
                h * ROW_BLOCK : (h + 1) * ROW_BLOCK
            ]


def attend(scal, first, q, heads, group, mine, theirs, doc_col, doc_row, parts):
    tokens = q.shape[0]
    span = parts * CORES * tokens
    rows = heads * ROW_BLOCK
    lanes = heads * HEAD_DIMENSION
    blocks = tokens // ROW_BLOCK
    keys = pltpu.VMEM((span + KEY_BLOCK, HEAD_DIMENSION), bf16)
    column = pltpu.VMEM((blocks, rows, 1), f32)
    return call(
        functools.partial(attention_kernel, heads, parts, group),
        jax.ShapeDtypeStruct((tokens, lanes), bf16),
        4 * tokens * lanes * span // 2,
        4 * tokens * lanes + 8 * span * HEAD_DIMENSION,
        [SMEM, SMEM] + [VMEM] * 5,
        VMEM,
        [keys, keys, column, column, pltpu.VMEM((blocks, rows, HEAD_DIMENSION), f32)],
    )(scal, first, q, mine, theirs, doc_col, doc_row)


def ring_gather(w, ring, swap, flip):
    size = len(ring)
    half = size // 2
    ahead = [(ring[i], ring[(i + 1) % size]) for i in range(size)]
    back = [(ring[i], ring[(i - 1) % size]) for i in range(size)]
    fw = bw = w
    blocks = [w]
    for step in range(1, half + 1):
        if step < half or not flip:
            fw = lax.ppermute(fw, "exp", ahead)
            blocks.append(fw)
        if step < half or flip:
            bw = lax.ppermute(bw, "exp", back)
            blocks.append(bw)
    theirs = [lax.ppermute(b, "seq", swap) for b in blocks]
    return blocks, theirs


def project_far_kernel(blocks, pieces, parts, order, *refs):
    w_refs, refs = refs[: 2 * blocks], refs[2 * blocks :]
    att, refs = refs[: parts * pieces], refs[parts * pieces :]
    w_out, sends = refs[0], refs[1:]
    for which in range(2):
        for i in range(blocks):
            ref = w_refs[which * blocks + i]
            n = ref.shape[0]
            at = pl.multiple_of(order[which * blocks + i], n)
            w_out[pl.ds(at, n), :] = ref[...]
    for d, send in enumerate(sends):
        x = jnp.concatenate([r[...] for r in att[d * pieces : (d + 1) * pieces]], axis=1)
        send[...] = dot(x, w_out[...]).astype(bf16)


def project_far(order, mine, theirs, attended):
    tokens = attended[0][0].shape[0]
    pieces = len(attended[0])
    width = sum(a.shape[1] for a in attended[0])
    cols = mine[0].shape[1]
    parts = len(attended)
    flat = [a for group in attended for a in group]
    return call(
        functools.partial(project_far_kernel, len(mine), pieces, parts),
        [jax.ShapeDtypeStruct((width, cols), bf16)]
        + [jax.ShapeDtypeStruct((tokens, cols), bf16)] * parts,
        2 * parts * tokens * width * cols,
        2 * parts * tokens * width + 4 * width * cols,
        [SMEM] + [VMEM] * (2 * len(mine) + len(flat)),
        [VMEM] * (1 + parts),
    )(order, *mine, *theirs, *flat)


def project_own_kernel(*refs):
    att, (w_ref, out_ref) = refs[:-2], refs[-2:]
    out_ref[...] = dot(jnp.concatenate([r[...] for r in att], axis=1), w_ref[...])


def project_own(attended, w):
    tokens = attended[0].shape[0]
    width, cols = w.shape
    return call(
        project_own_kernel,
        jax.ShapeDtypeStruct((tokens, cols), f32),
        2 * tokens * width * cols,
        2 * tokens * width + 2 * width * cols,
        [VMEM] * (len(attended) + 1),
        VMEM,
    )(*attended, w)


class Slots:
    def __init__(self, capacity, devices):
        self.full = capacity // 8
        rest = capacity % 8
        self.tail = 0
        if rest:
            self.tail = 1
            while self.tail < rest:
                self.tail *= 2
        self.cuts = 8 // self.tail if self.tail else 0
        self.rows = 8 * devices
        self.groups = self.full + (1 if self.tail else 0)

    def width(self, cols):
        return self.full * cols + (cols // self.cuts if self.tail else 0)


def slot_keys(slots, expert, slot):
    keys = []
    kept = slot >= 0
    for g in range(slots.full):
        ok = kept & (slot >= 8 * g) & (slot < 8 * g + 8)
        keys.append(jnp.where(ok, expert * 8 + slot - 8 * g, -1))
    if slots.tail:
        rest = slot - 8 * slots.full
        for i in range(slots.cuts):
            keys.append(jnp.where(kept & (rest >= 0), expert * 8 + i * slots.tail + rest, -1))
    return jnp.stack(keys, axis=0).astype(jnp.int32)


def one_hot(keys_ref, i, rows):
    n = keys_ref.shape[1]
    return lax.broadcasted_iota(jnp.int32, (rows, n), 0) == keys_ref[i : i + 1, :]


def send(group, cols, src, dst, sems):
    at = slice(group * cols, min((group + 1) * cols, src.shape[1]))
    copy = pltpu.make_async_copy(src.at[:, at], dst.at[:, at], sems.at[group])
    copy.start()
    return copy


def pack_kernel(slots, parts, chunk, keys_ref, own_ref, *refs):
    recv, (packed_ref, rows_ref, x_ref, out_ref, sem, out_sem) = refs[:parts], refs[-6:]
    total = own_ref[...]
    for r in recv:
        total = total + r[...].astype(f32)
    x = total.astype(bf16)
    x_ref[...] = x
    cols = x.shape[1]
    copy = pltpu.make_async_copy(x_ref, rows_ref.at[:, chunk * cols : (chunk + 1) * cols], sem)
    copy.start()

    sent = []

    def place(hot, part):
        hot = hot.astype(f32)
        return dot(hot.astype(bf16), part), jnp.sum(hot, axis=1, keepdims=True)

    for g in range(slots.full):
        rows, live = place(one_hot(keys_ref, g, slots.rows), x)
        out_ref[:, g * cols : (g + 1) * cols] = jnp.where(live > 0, rows, EMPTY).astype(bf16)
        sent.append(send(g, cols, out_ref, packed_ref, out_sem))
    if slots.tail:
        cut = cols // slots.cuts
        acc = live_all = None
        for i in range(slots.cuts):
            rows, live = place(one_hot(keys_ref, slots.full + i, slots.rows), x[:, i * cut : (i + 1) * cut])
            acc = rows if acc is None else acc + rows
            live_all = live if live_all is None else live_all + live
        out_ref[:, slots.full * cols :] = jnp.where(live_all > 0, acc, EMPTY).astype(bf16)
        sent.append(send(slots.full, cols, out_ref, packed_ref, out_sem))
    copy.wait()
    for part in sent:
        part.wait()


def pack(slots, keys, own, received, rows_out, chunk):
    tokens, cols = own.shape
    width = slots.width(cols)
    parts = len(received)
    args = [keys, own, *received]
    ins = [VMEM] * len(args)
    alias = {}
    if rows_out is not None:
        alias = {len(args): 1}
        args.append(rows_out)
        ins.append(ANY)
    return call(
        functools.partial(pack_kernel, slots, parts, chunk),
        [
            jax.ShapeDtypeStruct((slots.rows, width), bf16),
            jax.ShapeDtypeStruct((tokens, cols * CHUNKS), bf16),
        ],
        4 * slots.rows * tokens * cols,
        8 * tokens * cols + 2 * slots.rows * width,
        ins,
        [HBM, ANY],
        [
            pltpu.VMEM((tokens, cols), bf16),
            pltpu.VMEM((slots.rows, width), bf16),
            pltpu.SemaphoreType.DMA,
            pltpu.SemaphoreType.DMA((slots.groups,)),
        ],
        alias,
    )(*args)


def spread(slots, block):
    cols = block.shape[1]
    full, cuts = slots.full, slots.cuts
    n = cols * cuts // (full * cuts + 1) if slots.tail else cols // full
    out = [block[:, g * n : (g + 1) * n].astype(f32) for g in range(full)]
    if slots.tail:
        rest = block[:, full * n :].astype(f32)
        rows = rest.shape[0]
        out.append(
            jnp.concatenate(
                [rest]
                + [pltpu.roll(rest, rows - i * slots.tail, 0) for i in range(1, cuts)],
                axis=1,
            )
        )
    return out


def tail_rows(shape):
    return lax.broadcasted_iota(jnp.int32, shape, 0) % 8


def live_rows(slots, groups):
    out = []
    for g, rows in enumerate(groups):
        live = rows[:, :1] < EMPTY / 2
        if slots.tail and g == slots.full:
            live = live & (tail_rows(live.shape) < slots.tail)
        out.append(live)
    return out


def row_tiles(ref, scr, sems, start):
    n = scr.shape[0] // TILES
    copies = []
    for t in range(TILES):
        copies.append(
            pltpu.make_async_copy(
                ref.at[start + t * n : start + (t + 1) * n], scr.at[t * n : (t + 1) * n], sems.at[t]
            )
        )
        copies[-1].start()
    return copies


def centered_rows(slots, block_ref, bias):
    groups = spread(slots, block_ref[...])
    live = live_rows(slots, groups)
    rows = [jnp.where(a, r - bias, 0.0).astype(bf16) for a, r in zip(live, groups)]
    return jnp.concatenate(rows, axis=0), live


def times(x, w_scr, copies, sum_scr):
    n = w_scr.shape[0] // len(copies)
    for t, copy in enumerate(copies):
        copy.wait()
        at = slice(t * n, (t + 1) * n)
        sum_scr[...] += dot(x[:, at], w_scr[at])


def encode_kernel(slots, block_ref, bias_ref, w_ref, out_ref, kept_ref, w_scr, o_scr, sems, kept_sem, out_sem):
    cols = w_scr.shape[0]
    copies = row_tiles(w_ref.at[0], w_scr, sems, 0)
    kept = pltpu.make_async_copy(block_ref, kept_ref, kept_sem)
    kept.start()
    x, _ = centered_rows(slots, block_ref, bias_ref[:, :cols])
    o_scr[...] = jnp.zeros_like(o_scr)
    times(x, w_scr, copies, o_scr)
    out = pltpu.make_async_copy(o_scr, out_ref, out_sem)
    out.start()
    kept.wait()
    out.wait()


def encode(slots, block, dec_bias, enc, cols):
    hidden = enc.shape[2]
    n = slots.rows * slots.groups
    one = pltpu.SemaphoreType.DMA
    return call(
        functools.partial(encode_kernel, slots),
        [jax.ShapeDtypeStruct((n, hidden), f32), jax.ShapeDtypeStruct(block.shape, bf16)],
        2 * n * cols * hidden,
        2 * cols * hidden + 2 * block.size + 4 * n * hidden,
        [VMEM, VMEM, HBM],
        [HBM, HBM],
        [
            pltpu.VMEM((cols, hidden), bf16),
            pltpu.VMEM((n, hidden), f32),
            pltpu.SemaphoreType.DMA((TILES,)),
            one,
            one,
        ],
        limit=ALMOST_ALL,
    )(block, dec_bias, enc)


def middle_kernel(
    slots, block_ref, bias_ref, enc_bias_ref, enc_ref, prev_ref, dec_ref,
    latent_out, packed_ref, kept_ref,
    e_scr, d_scr, p_scr, latent_scr, pack_scr, e_sems, d_sems, p_sem, kept_sem, latent_sem, sems,
):
    cols = e_scr.shape[0]
    _, model = d_scr.shape
    prev = pltpu.make_async_copy(prev_ref, p_scr, p_sem)
    prev.start()
    e_copies = row_tiles(enc_ref.at[0], e_scr, e_sems, model - cols)
    cuts = slots.cuts or 2
    cut = model // cuts
    d_copies = []
    for t in range(cuts):
        at = slice(t * cut, (t + 1) * cut)
        d_copies.append(
            pltpu.make_async_copy(dec_ref.at[0, :, at], d_scr.at[:, at], d_sems.at[t])
        )
        d_copies[-1].start()
    kept = pltpu.make_async_copy(block_ref, kept_ref, kept_sem)
    kept.start()
    x, live = centered_rows(slots, block_ref, bias_ref[:, model - cols :])
    n = slots.rows
    prev.wait()
    times(x, e_scr, e_copies, p_scr)
    for g, a in enumerate(live):
        rows = slice(g * n, (g + 1) * n)
        pre = jnp.maximum(p_scr[rows] + enc_bias_ref[...], 0.0)
        latent_scr[rows] = jnp.where(a, pre, 0.0).astype(bf16)
    latent = pltpu.make_async_copy(latent_scr, latent_out, latent_sem)
    latent.start()
    sent = []
    rest = None
    which = tail_rows((n, 1)) // slots.tail if slots.tail else None
    for t in range(cuts):
        at = slice(t * cut, (t + 1) * cut)
        d_copies[t].wait()
        out = dot(latent_scr[...], d_scr[:, at]) + bias_ref[:, at]
        for g in range(slots.full):
            here = slice(g * model + at.start, g * model + at.stop)
            pack_scr[:, here] = out[g * n : (g + 1) * n].astype(bf16)
            sent.append(
                pltpu.make_async_copy(
                    pack_scr.at[:, here], packed_ref.at[:, here], sems.at[len(sent)]
                )
            )
            sent[-1].start()
        if slots.tail:
            part = out[slots.full * n :]
            rest = part if t == 0 else jnp.where(which == t, pltpu.roll(part, t * slots.tail, 0), rest)
    if slots.tail:
        here = slice(slots.full * model, slots.full * model + cut)
        pack_scr[:, here] = rest.astype(bf16)
        sent.append(
            pltpu.make_async_copy(pack_scr.at[:, here], packed_ref.at[:, here], sems.at[len(sent)])
        )
        sent[-1].start()
    kept.wait()
    latent.wait()
    for one in sent:
        one.wait()


def middle(slots, block, dec_bias, enc_bias, enc, prev, dec, cols):
    _, model, hidden = enc.shape
    n = slots.rows * slots.groups
    out = (slots.rows, slots.width(model))
    one = pltpu.SemaphoreType.DMA
    cuts = slots.cuts or 2
    return call(
        functools.partial(middle_kernel, slots),
        [
            jax.ShapeDtypeStruct((n, hidden), bf16),
            jax.ShapeDtypeStruct(out, bf16),
            jax.ShapeDtypeStruct(block.shape, bf16),
        ],
        2 * n * (cols + model) * hidden,
        2 * (cols + model) * hidden + 6 * block.size + 6 * n * hidden,
        [VMEM] * 3 + [HBM] * 3,
        [HBM] * 3,
        [
            pltpu.VMEM((cols, hidden), bf16),
            pltpu.VMEM((hidden, model), bf16),
            pltpu.VMEM((n, hidden), f32),
            pltpu.VMEM((n, hidden), bf16),
            pltpu.VMEM(out, bf16),
            pltpu.SemaphoreType.DMA((TILES,)),
            pltpu.SemaphoreType.DMA((cuts,)),
            one, one, one,
            pltpu.SemaphoreType.DMA((slots.full * cuts + 1,)),
        ],
        limit=ALMOST_ALL,
    )(block, dec_bias, enc_bias, enc, prev, dec)


def grad_kernel(slots, latent_ref, built_ref, *refs):
    *arrived, out_ref, scr, sems = refs
    cols = scr.shape[2]
    built = spread(slots, built_ref[...])
    copies = []
    for j, block_ref in enumerate(arrived):
        at = slice(j * cols, (j + 1) * cols)
        groups = spread(slots, block_ref[...])
        residue = jnp.concatenate(
            [
                jnp.where(a, r[:, at] - rows, 0.0).astype(bf16)
                for a, r, rows in zip(live_rows(slots, groups), built, groups)
            ],
            axis=0,
        )
        scr[j] = dot(latent_ref[...], residue, ((0,), (0,))).astype(bf16)
        copies.append(pltpu.make_async_copy(scr.at[j], out_ref.at[0, :, at], sems.at[j]))
        copies[-1].start()
    for copy in copies:
        copy.wait()


def decoder_grad(slots, latent, rebuilt, arrived, model):
    n, hidden = latent.shape
    parts = len(arrived)
    return call(
        functools.partial(grad_kernel, slots),
        jax.ShapeDtypeStruct((1, hidden, model), bf16),
        2 * n * hidden * model,
        2 * hidden * model + 2 * n * (hidden + model),
        [VMEM] * (2 + parts),
        ANY,
        [pltpu.VMEM((parts, hidden, model // parts), bf16), pltpu.SemaphoreType.DMA((parts,))],
    )(latent, rebuilt, *arrived)


def finish_kernel(
    slots, keys_ref, kept_ref, block_ref, bias_ref, rows_ref, recon_out, error_out,
    recon_scr, error_scr, rows_scr, sems, rows_sem,
):
    came = pltpu.make_async_copy(rows_ref, rows_scr, rows_sem)
    came.start()
    model = rows_scr.shape[1]
    cuts = slots.cuts or 2
    cut = model // cuts
    hot = [
        one_hot(keys_ref, i, slots.rows).astype(f32).astype(bf16)
        for i in range(keys_ref.shape[0])
    ]
    turn = lambda i, part: dot(hot[i], part, ((0,), (0,)))
    copies = []
    for t in range(cuts):
        at = slice(t * cut, (t + 1) * cut)
        total = 0.0
        for g in range(slots.full):
            total = total + turn(g, block_ref[:, g * model + at.start : g * model + at.stop])
        if slots.tail:
            total = total + turn(slots.full + t, block_ref[:, slots.full * model :])
        recon = jnp.where(kept_ref[...] > 0, total, bias_ref[:, at]).astype(bf16)
        recon_scr[:, at] = recon
        if t == 0:
            came.wait()
        error_scr[:, at] = (recon.astype(f32) - rows_scr[:, at].astype(f32)).astype(bf16)
        for k, (scr, out) in enumerate(((recon_scr, recon_out), (error_scr, error_out))):
            copies.append(pltpu.make_async_copy(scr.at[:, at], out.at[:, at], sems.at[t, k]))
            copies[-1].start()
    for copy in copies:
        copy.wait()


def finish(slots, keys, kept, block, dec_bias, rows):
    tokens, model = rows.shape
    scr = pltpu.VMEM((tokens, model), bf16)
    return call(
        functools.partial(finish_kernel, slots),
        [jax.ShapeDtypeStruct((tokens, model), bf16)] * 2,
        4 * slots.rows * tokens * model,
        6 * tokens * model + 2 * block.size,
        [VMEM] * 4 + [HBM],
        [HBM, HBM],
        [scr, scr, scr, pltpu.SemaphoreType.DMA((slots.cuts or 2, 2)), pltpu.SemaphoreType.DMA],
        limit=ALMOST_ALL,
    )(keys, kept, block, dec_bias, rows)


def shards(
    query_rows,
    key_rows,
    value_matrix,
    doc_ids,
    out_weight,
    enc_weight,
    enc_bias,
    dec_weight,
    dec_bias,
    expert_ids,
    slot_ids,
):
    q, k, v = query_rows[0], key_rows[0], value_matrix[0]
    tokens = q.shape[0]
    size, exp_size = lax.axis_size("seq"), lax.axis_size("exp")
    chips = size // CORES
    devices = size * exp_size
    me = lax.axis_index("seq")
    chip, core = me // CORES, me % CORES
    q_cols, kv_cols = q.shape[1] // chips, k.shape[1] // chips
    heads = q.shape[1] // k.shape[1]
    groups = kv_cols // HEAD_DIMENSION
    span = tokens * size
    model = out_weight.shape[1]
    cols = model // CHUNKS

    def over(d):
        return [
            (a * CORES + b, ((a + d) % chips) * CORES + b)
            for a in range(chips)
            for b in range(CORES)
        ]

    swap = [(a, a ^ 1) for a in range(size)]

    def cut(x, at, n):
        return lax.dynamic_slice(x, (0, at * n), (x.shape[0], n))

    pair = lambda at: jnp.concatenate([cut(k, at, kv_cols), cut(v, at, kv_cols)], axis=1)
    kv_parts, q_parts = [pair(chip)], [q]
    for d in range(1, chips):
        to = (chip + d) % chips
        kv_parts.append(lax.ppermute(pair(to), "seq", over(d)))
        q_parts.append(lax.ppermute(cut(q, to, q_cols), "seq", over(d)))
    mine = jnp.concatenate(kv_parts, axis=0)
    theirs = lax.ppermute(mine, "seq", swap)

    ring = [2 * i for i in range(exp_size // 2)] + [2 * i + 1 for i in reversed(range(exp_size // 2))]
    exp_me = lax.axis_index("exp")
    place = jnp.where(exp_me % 2 == 0, exp_me // 2, exp_size - 1 - exp_me // 2)
    offsets = [0]
    for step in range(1, exp_size // 2):
        offsets += [-step, step]
    offsets.append(exp_size // 2)
    spot = (place + jnp.array(offsets, jnp.int32)) % exp_size
    order = jnp.where(spot < exp_size // 2, 2 * spot, 2 * (exp_size - 1 - spot) + 1)
    deep = out_weight.shape[0]
    order = jnp.concatenate(
        [(c * exp_size + order) * deep for c in (core, 1 - core)]
    ).astype(jnp.int32)
    w_blocks = [
        ring_gather(out_weight[:, j * cols : (j + 1) * cols], ring, swap, j % 2 == 1)
        for j in range(CHUNKS)
    ]

    doc_col = jnp.concatenate([doc_ids, jnp.full((1, KEY_BLOCK), -1, jnp.int32)], axis=1)
    doc_row = doc_ids.reshape(span, 1)
    starts = jnp.sum(
        (doc_ids < doc_ids[0, ::ROW_BLOCK][:, None]).astype(jnp.int32), axis=1
    ) // KEY_STEP
    seats = jnp.stack(
        [
            ((chip - a) % chips) * CORES + c
            for a in range(chips)
            for c in (core, 1 - core)
        ]
    )
    attended = []
    for d in range(chips):
        lane = chip * q_cols if d == 0 else 0 * chip
        scal = jnp.concatenate([jnp.stack([seats[d * CORES], lane]), seats]).astype(jnp.int32)
        attended.append([])
        for g in range(groups):
            attended[d].append(
                attend(scal, starts, q_parts[d], heads, g, mine, theirs, doc_col, doc_row, chips)
            )

    capacity = 2 * tokens // devices
    slots = Slots(capacity, devices)
    keys = slot_keys(slots, expert_ids[0], slot_ids[0])
    kept = (slot_ids[0] >= 0).astype(jnp.int32).reshape(tokens, 1)
    bias_row = dec_bias[None]
    whole_rows = None
    arrived = []

    def to_all(block):
        return lax.all_to_all(
            block.reshape(devices, 8, block.shape[1]), ("seq", "exp"), 0, 0, tiled=True
        ).reshape(block.shape)

    for j in range(CHUNKS):
        w_all, *sends = project_far(order, *w_blocks[j], attended[1:])
        received = [
            lax.ppermute(part, "seq", over(chips - d)) for d, part in enumerate(sends, start=1)
        ]
        own = project_own(attended[0], w_all)
        packed, whole_rows = pack(slots, keys, own, received, whole_rows, j)
        arrived.append(to_all(packed))

    pre, arrived[0] = encode(slots, arrived[0], bias_row, enc_weight, cols)
    latent, packed, arrived[1] = middle(
        slots, arrived[1], bias_row, enc_bias, enc_weight, pre, dec_weight, model - cols
    )
    returned = to_all(packed)
    dec_grad = decoder_grad(slots, latent, packed, arrived, model)
    recon, error = finish(slots, keys, kept, returned, bias_row, whole_rows)
    return (whole_rows[None], recon[None], error[None], dec_grad)


def solution(mesh):
    return jax.shard_map(
        shards,
        mesh=mesh,
        in_specs=(
            P("exp", "seq", None),
            P("exp", "seq", None),
            P("exp", "seq", None),
            P("exp", None),
            P(("seq", "exp"), None),
            P(("seq", "exp"), None, None),
            P(("seq", "exp"), None),
            P(("seq", "exp"), None, None),
            P(),
            P("exp", "seq"),
            P("exp", "seq"),
        ),
        out_specs=(
            P("exp", "seq", None),
            P("exp", "seq", None),
            P("exp", "seq", None),
            P(("seq", "exp"), None, None),
        ),
        check_vma=False,
    )
```

time: 293 us -> 203 us (0.69)
  waiting for transfers between devices: 156 us -> 104 us
  Pallas kernels: 0 us -> 41.8 us
  matrix products: 41 us -> 0 us
  local copies, waits for them, and re-layouts: 41.1 us -> 12 us
  starting transfers between devices: 21 us -> 40.9 us
  other arithmetic: 18.7 us -> 2.17 us
  between operations: 14.3 us -> 1.28 us
    ppermute x0 -> x35, waiting for transfers between devices: none -> 57.5 us  [the longest x7 26.6 us: ring_gather(): fw = lax.ppermute(fw, 'exp', ahead)]
    all_to_all x5 -> x3, waiting for transfers between devices: 102 us -> 46.6 us  [to_all(): lax.all_to_all(block.reshape(devices, 8, block.shape[1]), ('seq', 'exp'),...]
    pallas_call x0 -> x14, Pallas kernels: none -> 41.8 us  [the longest x4 9.53 us: attend(): call(functools.partial(attention_kernel, heads, parts, group), jax.ShapeD...]
    reduce_scatter x1 -> x0, waiting for transfers between devices: 35.9 us -> none  [shards(): lax.psum_scatter(jnp.dot(attended, own_rows, preferred_element_type=jnp.f...]
    dot_general x5 -> x0, matrix products: 28.8 us -> none  [the longest x1 8.54 us: attend_block(): jnp.einsum('hqk,kd->qhd', normed, value_part, preferred_element_type=jnp....]
    ppermute x0 -> x35, starting transfers between devices: none -> 25.5 us  [the longest x7 17.4 us: ring_gather(): fw = lax.ppermute(fw, 'exp', ahead)]
    all_gather x1 -> x0, waiting for transfers between devices: 17.3 us -> none  [shards(): own_rows = lax.all_gather(out_weight, 'exp', axis=0, tiled=True)]
    unnamed x2 -> x1, other arithmetic: 12.6 us -> 0.01 us
  transfers between devices with their start and end apart: 7 -> 38, of which waited for: 6 -> 12; matrix products, arithmetic and copies ran while one was open for 25% -> 3% of each run, Pallas kernels for 0% -> 14%
where the time goes in v2:
time: 203 us; the launch traced here: 202 us
  waiting for transfers between devices  104 us (51%)
  Pallas kernels  41.8 us (21%)
  starting transfers between devices  40.9 us (20%)
  local copies, waits for them, and re-layouts  12 us (6%)
  other arithmetic  2.17 us (1%)
    all_to_all x3, waiting for transfers between devices, to_all(): lax.all_to_all(block.reshape(devices, 8, block.shape[1]), ('seq', 'exp'),...  46.6 us
    ppermute x7, waiting for transfers between devices, ring_gather(): fw = lax.ppermute(fw, 'exp', ahead)  26.6 us
    ppermute x7, waiting for transfers between devices, ring_gather(): bw = lax.ppermute(bw, 'exp', back)  18.5 us
    ppermute x7, starting transfers between devices, ring_gather(): fw = lax.ppermute(fw, 'exp', ahead)  17.4 us
    all_to_all x3, starting transfers between devices, to_all(): lax.all_to_all(block.reshape(devices, 8, block.shape[1]), ('seq', 'exp'),...  15.3 us
    pallas_call x4, Pallas kernels, attend(): call(functools.partial(attention_kernel, heads, parts, group), jax.ShapeD...  9.53 us
    pallas_call x1, Pallas kernels, middle(): call(functools.partial(middle_kernel, slots), [jax.ShapeDtypeStruct((n, h...  9.39 us
    ppermute x2, waiting for transfers between devices, shards(): lax.ppermute(part, 'seq', over(chips - d))  8.54 us
  transfers between devices with their start and end apart: 38, of which 12 were waited for; matrix products, arithmetic and copies ran while one was open for 3% of the time, Pallas kernels for 14%

profile of v2, /device:TPU:0, one launch (start us, length us, event | category | flops | bytes accessed | tf_op | source)
XLA Modules:
  0.0 202.3 jit_solution(59998596945200848)
XLA Ops:
  0.6 1.1 fusion.1
  1.7 3.1 %collective-permute-start.19 = (bf16[128,1024]{1,0:T(8,128)(2,1)S(1)}, bf16[128,1024]{1,0:T(8,128)(2,1)S(1)}, u32[]{:S(2)}, u32[]{:S(2)}) collective-permute-start(bf16[128,1024]{1,0:T(8,128)(2,1)S(1)} %get-tuple-element.36.refs_0_), channel_id=1, source_target_pairs={{0,2},{2,4},{4,6},{6,7},{7,5},{5,3},{3,1},{1,0},{8,10},{10,12},{12... | collective-permute-start | bytes 786440 | tf_op jit(solution)/shard_map/ppermute | solution.py:152
  4.8 1.1 dynamic-slice_bitcast_fusion.3
  5.9 5.2 %collective-permute-done.19.refs_1_ = bf16[128,1024]{1,0:T(8,128)(2,1)S(1)} collective-permute-done((bf16[128,1024]{1,0:T(8,128)(2,1)S(1)}, bf16[128,1024]{1,0:T(8,128)(2,1)S(1)}, u32[]{:S(2)}, u32[]{:S(2)}) %collective-permute-start.19) | collective-permute-done | bytes 262176 | tf_op jit(solution)/shard_map/ppermute | solution.py:152
  11.1 1.8 collective-permute-start.21
  12.9 1.6 collective-permute-start
  14.4 2.1 %dynamic-slice_bitcast_fusion = bf16[192,2048]{1,0:T(8,128)(2,1)} fusion(bf16[1,192,4096]{2,1,0:T(8,128)(2,1)} %param.12, s32[]{:T(128)S(6)} %select_n.93), kind=kLoop, calls=%fused_computation | loop fusion | bytes 1572868 | tf_op jit(solution)/shard_map/dynamic_slice | solution.py:633
  16.5 0.5 collective-permute-start.17
  17.1 2.4 %collective-permute-done = bf16[192,512]{1,0:T(8,128)(2,1)S(1)} collective-permute-done((bf16[192,512]{1,0:T(8,128)(2,1)S(1)}, bf16[192,512]{1,0:T(8,128)(2,1)S(1)}, u32[]{:S(2)}, u32[]{:S(2)}) %collective-permute-start) | collective-permute-done | bytes 196640 | tf_op jit(solution)/shard_map/ppermute | solution.py:639
  19.5 0.4 collective-permute-start.22
  19.9 1.7 collective-permute-start.23
  21.6 1.2 add_multiply_fusion.1
  22.9 5.4 %collective-permute-done.22.refs_4_ = bf16[128,1024]{1,0:T(8,128)(2,1)} collective-permute-done((bf16[128,1024]{1,0:T(8,128)(2,1)S(1)}, bf16[128,1024]{1,0:T(8,128)(2,1)}, u32[]{:S(2)}, u32[]{:S(2)}) %collective-permute-start.22) | collective-permute-done | bytes 262176 | tf_op jit(solution)/shard_map/ppermute | solution.py:155
  28.3 0.7 copy-done.9
  29.0 0.4 collective-permute-start.24
  29.4 1.7 collective-permute-start.25
  31.1 0.1 slice.9
  31.2 0.2 copy.22.drow_ref
  31.4 0.1 concatenate.23.scal
  31.6 0.7 pad_add_fusion.1.order
  32.3 0.2 convert_reduce_fusion
  32.6 0.5 collective-permute-start.30
  33.0 5.0 %collective-permute-done.24.refs_6_ = bf16[128,1024]{1,0:T(8,128)(2,1)} collective-permute-done((bf16[128,1024]{1,0:T(8,128)(2,1)}, bf16[128,1024]{1,0:T(8,128)(2,1)}, u32[]{:S(2)}, u32[]{:S(2)}) %collective-permute-start.24) | collective-permute-done | bytes 262176 | tf_op jit(solution)/shard_map/ppermute | solution.py:155
  38.1 0.5 collective-permute-start.32
  38.7 3.0 %shard_map.149.refs_16_ = bf16[192,1024]{1,0:T(8,128)(2,1)S(1)} custom-call(s32[6]{0:T(128)S(1)} %concatenate.29.scal, s32[12]{0:T(128)S(1)} %and_select_fusion.2.first, bf16[192,2048]{1,0:T(8,128)(2,1)S(1)} %collective-permute-done.17.q_ref, bf16[384,512]{1,0:T(8,128)(2,1)S(1)} %pad_maximum_fusion.mine_ref, ...), custom_call_target="tpu_custom_call" | custom-call | flops 301989888 | bytes 1572864 | tf_op jit(solution)/shard_map/pallas_call | solution.py:132
  41.7 3.0 %shard_map.150.refs_17_ = bf16[192,1024]{1,0:T(8,128)(2,1)S(1)} custom-call(s32[6]{0:T(128)S(1)} %concatenate.29.scal, s32[12]{0:T(128)S(1)} %and_select_fusion.2.first, bf16[192,2048]{1,0:T(8,128)(2,1)S(1)} %collective-permute-done.17.q_ref, bf16[384,512]{1,0:T(8,128)(2,1)S(1)} %pad_maximum_fusion.mine_ref, ...), custom_call_target="tpu_custom_call" | custom-call | flops 301989888 | bytes 1572864 | tf_op jit(solution)/shard_map/pallas_call | solution.py:132
  44.7 1.6 collective-permute-start.2
  46.3 0.5 collective-permute-start.3
  46.8 2.7 %shard_map.153 = (bf16[2048,1024]{1,0:T(8,128)(2,1)S(1)}, bf16[192,1024]{1,0:T(8,128)(2,1)S(1)}) custom-call(s32[16]{0:T(128)S(1)} %pad_add_fusion.1.order, bf16[128,1024]{1,0:T(8,128)(2,1)S(1)} %get-tuple-element.36.refs_0_, bf16[128,1024]{1,0:T(8,128)(2,1)S(1)} %collective-permute-done.19.refs_1_, bf16[128,1024]{1,0:T(8,128)(2,1)S(1)} %copy-done.6, ...), custom_call_target="tpu_custom_call" | custom-call | flops 805306368 | bytes 9175040 | tf_op jit(solution)/shard_map/pallas_call | solution.py:183
  49.6 5.2 %collective-permute-done.3.refs_2_ = bf16[128,1024]{1,0:T(8,128)(2,1)} collective-permute-done((bf16[128,1024]{1,0:T(8,128)(2,1)S(1)}, bf16[128,1024]{1,0:T(8,128)(2,1)}, u32[]{:S(2)}, u32[]{:S(2)}) %collective-permute-start.3) | collective-permute-done | bytes 262176 | tf_op jit(solution)/shard_map/ppermute | solution.py:155
  54.8 0.4 collective-permute-start.5
  55.2 1.9 shard_map.147.refs_0_
  57.1 1.7 shard_map.148.refs_1_
  58.9 1.0 shard_map.154.own_ref
  59.9 1.3 shard_map.155
  61.2 7.7 %all-to-all-start.1 = ((bf16[32,8,1536]{2,1,0:T(8,128)(2,1)}), bf16[32,8,1536]{2,1,0:T(8,128)(2,1)S(1)}, u32[]{:S(2)}, u32[]{:S(2)}) async-start(bf16[32,8,1536]{2,1,0:T(8,128)(2,1)} %bitcast.18), calls=%async_computation.1 | async-start | bytes 1572864 | tf_op jit(solution)/shard_map/all_to_all | solution.py:693
  68.9 1.8 collective-permute-start.4
  70.7 0.3 collective-permute-start.7
  71.0 0.5 collective-permute-start.10
  71.5 16.5 %collective-permute-done.4.refs_3_ = bf16[128,1024]{1,0:T(8,128)(2,1)S(1)} collective-permute-done((bf16[128,1024]{1,0:T(8,128)(2,1)}, bf16[128,1024]{1,0:T(8,128)(2,1)S(1)}, u32[]{:S(2)}, u32[]{:S(2)}) %collective-permute-start.4) | collective-permute-done | bytes 262176 | tf_op jit(solution)/shard_map/ppermute | solution.py:152
  88.0 5.7 %collective-permute-start.6 = (bf16[128,1024]{1,0:T(8,128)(2,1)S(1)}, bf16[128,1024]{1,0:T(8,128)(2,1)S(1)}, u32[]{:S(2)}, u32[]{:S(2)}) collective-permute-start(bf16[128,1024]{1,0:T(8,128)(2,1)S(1)} %collective-permute-done.4.refs_3_), channel_id=1, source_target_pairs={{0,2},{2,4},{4,6},{6,7},{7,5},{5,3},{3,1},{1,0},{8,10},{10,12},{12... | collective-permute-start | bytes 786440 | tf_op jit(solution)/shard_map/ppermute | solution.py:152
  93.8 0.5 collective-permute-start.13
  94.4 4.9 %collective-permute-done.6.refs_5_ = bf16[128,1024]{1,0:T(8,128)(2,1)S(1)} collective-permute-done((bf16[128,1024]{1,0:T(8,128)(2,1)S(1)}, bf16[128,1024]{1,0:T(8,128)(2,1)S(1)}, u32[]{:S(2)}, u32[]{:S(2)}) %collective-permute-start.6) | collective-permute-done | bytes 262176 | tf_op jit(solution)/shard_map/ppermute | solution.py:152
  99.3 2.8 %collective-permute-done.8.refs_7_ = bf16[128,1024]{1,0:T(8,128)(2,1)S(1)} collective-permute-done((bf16[128,1024]{1,0:T(8,128)(2,1)S(1)}, bf16[128,1024]{1,0:T(8,128)(2,1)S(1)}, u32[]{:S(2)}, u32[]{:S(2)}) %collective-permute-start.8) | collective-permute-done | bytes 262176 | tf_op jit(solution)/shard_map/ppermute | solution.py:155
  102.1 1.5 collective-permute-done.16.refs_15_
  103.6 2.3 %shard_map.151 = (bf16[2048,1024]{1,0:T(8,128)(2,1)S(1)}, bf16[192,1024]{1,0:T(8,128)(2,1)S(1)}) custom-call(s32[16]{0:T(128)S(1)} %pad_add_fusion.1.order, bf16[128,1024]{1,0:T(8,128)(2,1)S(1)} %get-tuple-element.37.refs_0_, bf16[128,1024]{1,0:T(8,128)(2,1)} %collective-permute-done.2.refs_1_, bf16[128,1024]{1,0:T(8,128)(2,1)} %collective-permute-done.3.refs_2_, ...), custom_call_target="tpu_custom_call" | custom-call | flops 805306368 | bytes 9175040 | tf_op jit(solution)/shard_map/pallas_call | solution.py:183
  105.9 1.7 collective-permute-start.18
  107.6 1.0 shard_map.152.own_ref
  108.6 8.5 %collective-permute-done.18.refs_0_ = bf16[192,1024]{1,0:T(8,128)(2,1)S(1)} collective-permute-done((bf16[192,1024]{1,0:T(8,128)(2,1)S(1)}, bf16[192,1024]{1,0:T(8,128)(2,1)S(1)}, u32[]{:S(2)}, u32[]{:S(2)}) %collective-permute-start.18) | collective-permute-done | bytes 393248 | tf_op jit(solution)/shard_map/ppermute | solution.py:700
  117.2 1.3 shard_map.156
  118.5 4.9 %all-to-all-start = ((bf16[32,8,1536]{2,1,0:T(8,128)(2,1)}), bf16[32,8,1536]{2,1,0:T(8,128)(2,1)S(1)}, u32[]{:S(2)}, u32[]{:S(2)}) async-start(bf16[32,8,1536]{2,1,0:T(8,128)(2,1)} %bitcast.15), calls=%async_computation | async-start | bytes 1572864 | tf_op jit(solution)/shard_map/all_to_all | solution.py:693
  123.4 5.3 %shard_map.157 = (f32[512,1024]{1,0:T(8,128)}, bf16[256,1536]{1,0:T(8,128)(2,1)}) custom-call(bf16[256,1536]{1,0:T(8,128)(2,1)} %bitcast.34, f32[1,2048]{1,0:T(1,128)} %bitcast.37, bf16[1,2048,1024]{2,1,0:T(8,128)(2,1)} %enc_ref.1), custom_call_target="tpu_custom_call" | custom-call | flops 1073741824 | bytes 4980736 | tf_op jit(solution)/shard_map/pallas_call | solution.py:398
  128.7 16.3 %all-to-all-done = bf16[32,8,1536]{2,1,0:T(8,128)(2,1)S(1)} async-done(((bf16[32,8,1536]{2,1,0:T(8,128)(2,1)}), bf16[32,8,1536]{2,1,0:T(8,128)(2,1)S(1)}, u32[]{:S(2)}, u32[]{:S(2)}) %all-to-all-start) | async-done | bytes 786464 | tf_op jit(solution)/shard_map/all_to_all | solution.py:693
  145.0 0.9 copy-done.14
  145.9 9.4 %shard_map.158 = (bf16[512,1024]{1,0:T(8,128)(2,1)}, bf16[256,3072]{1,0:T(8,128)(2,1)}, bf16[256,1536]{1,0:T(8,128)(2,1)}) custom-call(bf16[256,1536]{1,0:T(8,128)(2,1)} %bitcast.36, f32[1,2048]{1,0:T(1,128)} %bitcast.38, f32[1,1024]{1,0:T(1,128)} %enc_bias_ref.1, bf16[1,2048,1024]{2,1,0:T(8,128)(2,1)} %enc_ref.1, f32[512,1024]{1,0:T(8,128)} %get-tuple-element.27.prev_ref, ...), custom_call_target="tpu_custom_call" | custom-call | flops 3221225472 | bytes 11796480 | tf_op jit(solution)/shard_map/pallas_call | solution.py:485
  155.3 2.7 %all-to-all-start.2 = ((bf16[32,8,3072]{2,1,0:T(8,128)(2,1)}), bf16[32,8,3072]{2,1,0:T(8,128)(2,1)S(1)}, u32[]{:S(2)}, u32[]{:S(2)}) async-start(bf16[32,8,3072]{2,1,0:T(8,128)(2,1)} %bitcast.32), calls=%async_computation.2 | async-start | bytes 3145728 | tf_op jit(solution)/shard_map/all_to_all | solution.py:693
  158.1 0.8 copy.26.kept_ref
  158.8 1.4 copy-done.1
  160.2 1.2 copy-done.2
  161.5 1.1 copy-done.4
  162.6 4.0 %shard_map.160 = bf16[1,1024,2048]{2,1,0:T(8,128)(2,1)} custom-call(bf16[512,1024]{1,0:T(8,128)(2,1)S(1)} %copy-done.2, bf16[256,3072]{1,0:T(8,128)(2,1)S(1)} %copy-done.1, bf16[256,1536]{1,0:T(8,128)(2,1)S(1)} %copy-done.3, bf16[256,1536]{1,0:T(8,128)(2,1)S(1)} %copy-done.4), custom_call_target="tpu_custom_call" | custom-call | flops 2147483648 | bytes 7340032 | tf_op jit(solution)/shard_map/pallas_call | solution.py:536
  166.6 30.2 %all-to-all-done.2 = bf16[32,8,3072]{2,1,0:T(8,128)(2,1)S(1)} async-done(((bf16[32,8,3072]{2,1,0:T(8,128)(2,1)}), bf16[32,8,3072]{2,1,0:T(8,128)(2,1)S(1)}, u32[]{:S(2)}, u32[]{:S(2)}) %all-to-all-start.2) | async-done | bytes 1572896 | tf_op jit(solution)/shard_map/all_to_all | solution.py:693
  196.8 1.2 copy-done.12
  198.0 4.1 %shard_map.159 = (bf16[192,2048]{1,0:T(8,128)(2,1)}, bf16[192,2048]{1,0:T(8,128)(2,1)}) custom-call(s32[3,192]{1,0:T(4,128)} %copy-done.11, s32[192,1]{1,0:T(8,128)} %copy.26.kept_ref, bf16[256,3072]{1,0:T(8,128)(2,1)} %bitcast.33, f32[1,2048]{1,0:T(1,128)} %bitcast.39, bf16[192,2048]{1,0:T(8,128)(2,1)} %get-tuple-element.24.rows_ref), custom_call_target="tpu_custom_call" | custom-call | flops 402653184 | bytes 3932160 | tf_op jit(solution)/shard_map/pallas_call | solution.py:584
  (84 shorter events, 0.8 us)
Async XLA Ops:
  0.6 30.4 %copy-start.15 = (s32[1,768]{1,0:T(1,128)S(1)}, s32[1,768]{1,0:T(1,128)}, u32[]{:S(2)}) copy-start(s32[1,768]{1,0:T(1,128)} %param.15) | copy-start | bytes 9220
  1.7 9.4 %collective-permute-start.19 = (bf16[128,1024]{1,0:T(8,128)(2,1)S(1)}, bf16[128,1024]{1,0:T(8,128)(2,1)S(1)}, u32[]{:S(2)}, u32[]{:S(2)}) collective-permute-start(bf16[128,1024]{1,0:T(8,128)(2,1)S(1)} %get-tuple-element.36.refs_0_), channel_id=1, source_target_pairs={{0,2},{2,4},{4,6},{6,7},{7,5},{5,3},{3,1},{1,0},{8,10},{10,12},{12... | collective-permute-start | bytes 786440 | tf_op jit(solution)/shard_map/ppermute | solution.py:152
  4.8 14.7 %collective-permute-start.20 = (bf16[128,1024]{1,0:T(8,128)(2,1)S(1)}, bf16[128,1024]{1,0:T(8,128)(2,1)S(1)}, u32[]{:S(2)}, u32[]{:S(2)}) collective-permute-start(bf16[128,1024]{1,0:T(8,128)(2,1)S(1)} %get-tuple-element.36.refs_0_), channel_id=1, source_target_pairs={{0,1},{2,0},{4,2},{6,4},{7,6},{5,7},{3,5},{1,3},{8,9},{10,8},{12,1... | collective-permute-start | bytes 786440 | tf_op jit(solution)/shard_map/ppermute | solution.py:155
  4.8 18.0 %collective-permute-start.26 = (bf16[128,1024]{1,0:T(8,128)(2,1)S(1)}, bf16[128,1024]{1,0:T(8,128)(2,1)S(1)}, u32[]{:S(2)}, u32[]{:S(2)}) collective-permute-start(bf16[128,1024]{1,0:T(8,128)(2,1)S(1)} %get-tuple-element.36.refs_0_), channel_id=1, source_target_pairs={{0,8},{8,0},{16,24},{24,16},{1,9},{9,1},{17,25},{25,17},{2,10},{10... | collective-permute-start | bytes 786440 | tf_op jit(solution)/shard_map/ppermute | solution.py:157
  11.1 8.8 %collective-permute-start.21 = (bf16[128,1024]{1,0:T(8,128)(2,1)S(1)}, bf16[128,1024]{1,0:T(8,128)(2,1)}, u32[]{:S(2)}, u32[]{:S(2)}) collective-permute-start(bf16[128,1024]{1,0:T(8,128)(2,1)S(1)} %collective-permute-done.19.refs_1_), channel_id=1, source_target_pairs={{0,2},{2,4},{4,6},{6,7},{7,5},{5,3},{3,1},{1,0},{8,10},{10,12},{12... | collective-permute-start | bytes 786440 | tf_op jit(solution)/shard_map/ppermute | solution.py:152
  12.9 6.6 %collective-permute-start = (bf16[192,512]{1,0:T(8,128)(2,1)S(1)}, bf16[192,512]{1,0:T(8,128)(2,1)S(1)}, u32[]{:S(2)}, u32[]{:S(2)}) collective-permute-start(bf16[192,512]{1,0:T(8,128)(2,1)S(1)} %pad_maximum_fusion.1), channel_id=1, source_target_pairs={{0,16},{8,24},{16,0},{24,8},{1,17},{9,25},{17,1},{25,9},{2,18},{10... | collective-permute-start | bytes 589832 | tf_op jit(solution)/shard_map/ppermute | solution.py:639
  16.5 21.5 %collective-permute-start.17 = (bf16[192,2048]{1,0:T(8,128)(2,1)}, bf16[192,2048]{1,0:T(8,128)(2,1)S(1)}, u32[]{:S(2)}, u32[]{:S(2)}) collective-permute-start(bf16[192,2048]{1,0:T(8,128)(2,1)} %dynamic-slice_bitcast_fusion), channel_id=1, source_target_pairs={{0,16},{8,24},{16,0},{24,8},{1,17},{9,25},{17,1},{25,9},{2,18},{10... | collective-permute-start | bytes 2359304 | tf_op jit(solution)/shard_map/ppermute | solution.py:640
  19.5 8.8 %collective-permute-start.27 = (bf16[128,1024]{1,0:T(8,128)(2,1)S(1)}, bf16[128,1024]{1,0:T(8,128)(2,1)S(1)}, u32[]{:S(2)}, u32[]{:S(2)}) collective-permute-start(bf16[128,1024]{1,0:T(8,128)(2,1)S(1)} %collective-permute-done.19.refs_1_), channel_id=1, source_target_pairs={{0,8},{8,0},{16,24},{24,16},{1,9},{9,1},{17,25},{25,17},{2,10},{10... | collective-permute-start | bytes 786440 | tf_op jit(solution)/shard_map/ppermute | solution.py:157
  19.5 19.2 %copy-start.5 = (bf16[128,1024]{1,0:T(8,128)(2,1)}, bf16[128,1024]{1,0:T(8,128)(2,1)S(1)}, u32[]{:S(2)}) copy-start(bf16[128,1024]{1,0:T(8,128)(2,1)S(1)} %collective-permute-done.20.refs_2_) | copy-start | bytes 786436
  19.5 8.8 %collective-permute-start.22 = (bf16[128,1024]{1,0:T(8,128)(2,1)S(1)}, bf16[128,1024]{1,0:T(8,128)(2,1)}, u32[]{:S(2)}, u32[]{:S(2)}) collective-permute-start(bf16[128,1024]{1,0:T(8,128)(2,1)S(1)} %collective-permute-done.20.refs_2_), channel_id=1, source_target_pairs={{0,1},{2,0},{4,2},{6,4},{7,6},{5,7},{3,5},{1,3},{8,9},{10,8},{12,1... | collective-permute-start | bytes 786440 | tf_op jit(solution)/shard_map/ppermute | solution.py:155
  19.9 9.5 %collective-permute-start.23 = (bf16[128,1024]{1,0:T(8,128)(2,1)}, bf16[128,1024]{1,0:T(8,128)(2,1)}, u32[]{:S(2)}, u32[]{:S(2)}) collective-permute-start(bf16[128,1024]{1,0:T(8,128)(2,1)} %collective-permute-done.21.refs_3_), channel_id=1, source_target_pairs={{0,2},{2,4},{4,6},{6,7},{7,5},{5,3},{3,1},{1,0},{8,10},{10,12},{12... | collective-permute-start | bytes 786440 | tf_op jit(solution)/shard_map/ppermute | solution.py:152
  22.8 15.9 %copy-start.7 = (bf16[128,1024]{1,0:T(8,128)(2,1)}, bf16[128,1024]{1,0:T(8,128)(2,1)S(1)}, u32[]{:S(2)}) copy-start(bf16[128,1024]{1,0:T(8,128)(2,1)S(1)} %collective-permute-done.26.refs_8_) | copy-start | bytes 786436
  22.8 9.7 %collective-permute-start.1 = (bf16[384,512]{1,0:T(8,128)(2,1)S(1)}, bf16[384,512]{1,0:T(8,128)(2,1)S(1)}, u32[]{:S(2)}, u32[]{:S(2)}) collective-permute-start(bf16[384,512]{1,0:T(8,128)(2,1)S(1)} %pad_maximum_fusion.mine_ref), channel_id=1, source_target_pairs={{0,8},{8,0},{16,24},{24,16},{1,9},{9,1},{17,25},{25,17},{2,10},{10... | collective-permute-start | bytes 1179656 | tf_op jit(solution)/shard_map/ppermute | solution.py:642
  28.3 4.2 %collective-permute-start.28 = (bf16[128,1024]{1,0:T(8,128)(2,1)S(1)}, bf16[128,1024]{1,0:T(8,128)(2,1)}, u32[]{:S(2)}, u32[]{:S(2)}) collective-permute-start(bf16[128,1024]{1,0:T(8,128)(2,1)S(1)} %collective-permute-done.20.refs_2_), channel_id=1, source_target_pairs={{0,8},{8,0},{16,24},{24,16},{1,9},{9,1},{17,25},{25,17},{2,10},{10... | collective-permute-start | bytes 786440 | tf_op jit(solution)/shard_map/ppermute | solution.py:157
  28.3 0.7 copy-start.9
  29.0 9.0 %collective-permute-start.24 = (bf16[128,1024]{1,0:T(8,128)(2,1)}, bf16[128,1024]{1,0:T(8,128)(2,1)}, u32[]{:S(2)}, u32[]{:S(2)}) collective-permute-start(bf16[128,1024]{1,0:T(8,128)(2,1)} %collective-permute-done.22.refs_4_), channel_id=1, source_target_pairs={{0,1},{2,0},{4,2},{6,4},{7,6},{5,7},{3,5},{1,3},{8,9},{10,8},{12,1... | collective-permute-start | bytes 786440 | tf_op jit(solution)/shard_map/ppermute | solution.py:155
  29.4 9.2 %collective-permute-start.25 = (bf16[128,1024]{1,0:T(8,128)(2,1)}, bf16[128,1024]{1,0:T(8,128)(2,1)}, u32[]{:S(2)}, u32[]{:S(2)}) collective-permute-start(bf16[128,1024]{1,0:T(8,128)(2,1)} %collective-permute-done.23.refs_5_), channel_id=1, source_target_pairs={{0,2},{2,4},{4,6},{6,7},{7,5},{5,3},{3,1},{1,0},{8,10},{10,12},{12... | collective-permute-start | bytes 786440 | tf_op jit(solution)/shard_map/ppermute | solution.py:152
  31.6 15.2 %copy-start.10 = (bf16[128,1024]{1,0:T(8,128)(2,1)S(1)}, bf16[128,1024]{1,0:T(8,128)(2,1)}, u32[]{:S(2)}) copy-start(bf16[128,1024]{1,0:T(8,128)(2,1)} %copy-done.9) | copy-start | bytes 786436
  32.5 12.2 %collective-permute-start.29 = (bf16[128,1024]{1,0:T(8,128)(2,1)}, bf16[128,1024]{1,0:T(8,128)(2,1)S(1)}, u32[]{:S(2)}, u32[]{:S(2)}) collective-permute-start(bf16[128,1024]{1,0:T(8,128)(2,1)} %collective-permute-done.21.refs_3_), channel_id=1, source_target_pairs={{0,8},{8,0},{16,24},{24,16},{1,9},{9,1},{17,25},{25,17},{2,10},{10... | collective-permute-start | bytes 786440 | tf_op jit(solution)/shard_map/ppermute | solution.py:157
  32.6 13.7 %collective-permute-start.30 = (bf16[128,1024]{1,0:T(8,128)(2,1)}, bf16[128,1024]{1,0:T(8,128)(2,1)S(1)}, u32[]{:S(2)}, u32[]{:S(2)}) collective-permute-start(bf16[128,1024]{1,0:T(8,128)(2,1)} %collective-permute-done.22.refs_4_), channel_id=1, source_target_pairs={{0,8},{8,0},{16,24},{24,16},{1,9},{9,1},{17,25},{25,17},{2,10},{10... | collective-permute-start | bytes 786440 | tf_op jit(solution)/shard_map/ppermute | solution.py:157
  38.1 8.7 %collective-permute-start.31 = (bf16[128,1024]{1,0:T(8,128)(2,1)}, bf16[128,1024]{1,0:T(8,128)(2,1)S(1)}, u32[]{:S(2)}, u32[]{:S(2)}) collective-permute-start(bf16[128,1024]{1,0:T(8,128)(2,1)} %collective-permute-done.23.refs_5_), channel_id=1, source_target_pairs={{0,8},{8,0},{16,24},{24,16},{1,9},{9,1},{17,25},{25,17},{2,10},{10... | collective-permute-start | bytes 786440 | tf_op jit(solution)/shard_map/ppermute | solution.py:157
  38.1 8.7 %collective-permute-start.32 = (bf16[128,1024]{1,0:T(8,128)(2,1)}, bf16[128,1024]{1,0:T(8,128)(2,1)S(1)}, u32[]{:S(2)}, u32[]{:S(2)}) collective-permute-start(bf16[128,1024]{1,0:T(8,128)(2,1)} %collective-permute-done.24.refs_6_), channel_id=1, source_target_pairs={{0,8},{8,0},{16,24},{24,16},{1,9},{9,1},{17,25},{25,17},{2,10},{10... | collective-permute-start | bytes 786440 | tf_op jit(solution)/shard_map/ppermute | solution.py:157
  38.6 8.2 %collective-permute-start.33 = (bf16[128,1024]{1,0:T(8,128)(2,1)}, bf16[128,1024]{1,0:T(8,128)(2,1)S(1)}, u32[]{:S(2)}, u32[]{:S(2)}) collective-permute-start(bf16[128,1024]{1,0:T(8,128)(2,1)} %collective-permute-done.25.refs_7_), channel_id=1, source_target_pairs={{0,8},{8,0},{16,24},{24,16},{1,9},{9,1},{17,25},{25,17},{2,10},{10... | collective-permute-start | bytes 786440 | tf_op jit(solution)/shard_map/ppermute | solution.py:157
  38.7 8.1 %copy-start.6 = (bf16[128,1024]{1,0:T(8,128)(2,1)S(1)}, bf16[128,1024]{1,0:T(8,128)(2,1)}, u32[]{:S(2)}) copy-start(bf16[128,1024]{1,0:T(8,128)(2,1)} %copy-done.5) | copy-start | bytes 786436
  38.7 8.1 %copy-start.8 = (bf16[128,1024]{1,0:T(8,128)(2,1)S(1)}, bf16[128,1024]{1,0:T(8,128)(2,1)}, u32[]{:S(2)}) copy-start(bf16[128,1024]{1,0:T(8,128)(2,1)} %copy-done.7) | copy-start | bytes 786436
  41.7 7.9 %copy-start.16 = (s32[1,192]{1,0:T(1,128)S(1)}, s32[1,192]{1,0:T(1,128)}, u32[]{:S(2)}) copy-start(s32[1,192]{1,0:T(1,128)} %param.22) | copy-start | bytes 2308
  41.7 7.9 %copy-start.18 = (s32[1,192]{1,0:T(1,128)S(1)}, s32[1,192]{1,0:T(1,128)}, u32[]{:S(2)}) copy-start(s32[1,192]{1,0:T(1,128)} %param.21) | copy-start | bytes 2308
  41.7 13.5 %copy-start = (bf16[1,192,4096]{2,1,0:T(8,128)(2,1)S(1)}, bf16[1,192,4096]{2,1,0:T(8,128)(2,1)}, u32[]{:S(2)}) copy-start(bf16[1,192,4096]{2,1,0:T(8,128)(2,1)} %param.12) | copy-start | bytes 4718596
  44.7 24.2 %collective-permute-start.2 = (bf16[128,1024]{1,0:T(8,128)(2,1)S(1)}, bf16[128,1024]{1,0:T(8,128)(2,1)}, u32[]{:S(2)}, u32[]{:S(2)}) collective-permute-start(bf16[128,1024]{1,0:T(8,128)(2,1)S(1)} %get-tuple-element.37.refs_0_), channel_id=1, source_target_pairs={{0,2},{2,4},{4,6},{6,7},{7,5},{5,3},{3,1},{1,0},{8,10},{10,12},{12... | collective-permute-start | bytes 786440 | tf_op jit(solution)/shard_map/ppermute | solution.py:152
  46.3 8.5 %collective-permute-start.3 = (bf16[128,1024]{1,0:T(8,128)(2,1)S(1)}, bf16[128,1024]{1,0:T(8,128)(2,1)}, u32[]{:S(2)}, u32[]{:S(2)}) collective-permute-start(bf16[128,1024]{1,0:T(8,128)(2,1)S(1)} %get-tuple-element.37.refs_0_), channel_id=1, source_target_pairs={{0,1},{2,0},{4,2},{6,4},{7,6},{5,7},{3,5},{1,3},{8,9},{10,8},{12,1... | collective-permute-start | bytes 786440 | tf_op jit(solution)/shard_map/ppermute | solution.py:155
  49.5 10.4 %collective-permute-start.34 = (bf16[192,1024]{1,0:T(8,128)(2,1)S(1)}, bf16[192,1024]{1,0:T(8,128)(2,1)S(1)}, u32[]{:S(2)}, u32[]{:S(2)}) collective-permute-start(bf16[192,1024]{1,0:T(8,128)(2,1)S(1)} %get-tuple-element.22), channel_id=1, source_target_pairs={{0,16},{8,24},{16,0},{24,8},{1,17},{9,25},{17,1},{25,9},{2,18},{10... | collective-permute-start | bytes 1179656 | tf_op jit(solution)/shard_map/ppermute | solution.py:700
  49.6 67.6 %copy-start.11 = (s32[3,192]{1,0:T(4,128)}, s32[3,192]{1,0:T(4,128)S(1)}, u32[]{:S(2)}) copy-start(s32[3,192]{1,0:T(4,128)S(1)} %pad_add_fusion.keys_ref) | copy-start | bytes 6916
  54.8 15.9 %collective-permute-start.5 = (bf16[128,1024]{1,0:T(8,128)(2,1)}, bf16[128,1024]{1,0:T(8,128)(2,1)S(1)}, u32[]{:S(2)}, u32[]{:S(2)}) collective-permute-start(bf16[128,1024]{1,0:T(8,128)(2,1)} %collective-permute-done.3.refs_2_), channel_id=1, source_target_pairs={{0,1},{2,0},{4,2},{6,4},{7,6},{5,7},{3,5},{1,3},{8,9},{10,8},{12,1... | collective-permute-start | bytes 786440 | tf_op jit(solution)/shard_map/ppermute | solution.py:155
  61.2 57.3 %all-to-all-start.1 = ((bf16[32,8,1536]{2,1,0:T(8,128)(2,1)}), bf16[32,8,1536]{2,1,0:T(8,128)(2,1)S(1)}, u32[]{:S(2)}, u32[]{:S(2)}) async-start(bf16[32,8,1536]{2,1,0:T(8,128)(2,1)} %bitcast.18), calls=%async_computation.1 | async-start | bytes 1572864 | tf_op jit(solution)/shard_map/all_to_all | solution.py:693
  68.9 19.1 %collective-permute-start.4 = (bf16[128,1024]{1,0:T(8,128)(2,1)}, bf16[128,1024]{1,0:T(8,128)(2,1)S(1)}, u32[]{:S(2)}, u32[]{:S(2)}) collective-permute-start(bf16[128,1024]{1,0:T(8,128)(2,1)} %collective-permute-done.2.refs_1_), channel_id=1, source_target_pairs={{0,2},{2,4},{4,6},{6,7},{7,5},{5,3},{3,1},{1,0},{8,10},{10,12},{12... | collective-permute-start | bytes 786440 | tf_op jit(solution)/shard_map/ppermute | solution.py:152
  70.7 22.9 %collective-permute-start.7 = (bf16[128,1024]{1,0:T(8,128)(2,1)S(1)}, bf16[128,1024]{1,0:T(8,128)(2,1)S(1)}, u32[]{:S(2)}, u32[]{:S(2)}) collective-permute-start(bf16[128,1024]{1,0:T(8,128)(2,1)S(1)} %collective-permute-done.5.refs_4_), channel_id=1, source_target_pairs={{0,1},{2,0},{4,2},{6,4},{7,6},{5,7},{3,5},{1,3},{8,9},{10,8},{12,1... | collective-permute-start | bytes 786440 | tf_op jit(solution)/shard_map/ppermute | solution.py:155
  71.0 22.7 %collective-permute-start.9 = (bf16[128,1024]{1,0:T(8,128)(2,1)S(1)}, bf16[128,1024]{1,0:T(8,128)(2,1)S(1)}, u32[]{:S(2)}, u32[]{:S(2)}) collective-permute-start(bf16[128,1024]{1,0:T(8,128)(2,1)S(1)} %get-tuple-element.37.refs_0_), channel_id=1, source_target_pairs={{0,8},{8,0},{16,24},{24,16},{1,9},{9,1},{17,25},{25,17},{2,10},{10... | collective-permute-start | bytes 786440 | tf_op jit(solution)/shard_map/ppermute | solution.py:157
  71.0 22.8 %collective-permute-start.10 = (bf16[128,1024]{1,0:T(8,128)(2,1)}, bf16[128,1024]{1,0:T(8,128)(2,1)S(1)}, u32[]{:S(2)}, u32[]{:S(2)}) collective-permute-start(bf16[128,1024]{1,0:T(8,128)(2,1)} %collective-permute-done.2.refs_1_), channel_id=1, source_target_pairs={{0,8},{8,0},{16,24},{24,16},{1,9},{9,1},{17,25},{25,17},{2,10},{10... | collective-permute-start | bytes 786440 | tf_op jit(solution)/shard_map/ppermute | solution.py:157
  71.5 22.8 %collective-permute-start.11 = (bf16[128,1024]{1,0:T(8,128)(2,1)}, bf16[128,1024]{1,0:T(8,128)(2,1)S(1)}, u32[]{:S(2)}, u32[]{:S(2)}) collective-permute-start(bf16[128,1024]{1,0:T(8,128)(2,1)} %collective-permute-done.3.refs_2_), channel_id=1, source_target_pairs={{0,8},{8,0},{16,24},{24,16},{1,9},{9,1},{17,25},{25,17},{2,10},{10... | collective-permute-start | bytes 786440 | tf_op jit(solution)/shard_map/ppermute | solution.py:157
  88.0 11.3 %collective-permute-start.6 = (bf16[128,1024]{1,0:T(8,128)(2,1)S(1)}, bf16[128,1024]{1,0:T(8,128)(2,1)S(1)}, u32[]{:S(2)}, u32[]{:S(2)}) collective-permute-start(bf16[128,1024]{1,0:T(8,128)(2,1)S(1)} %collective-permute-done.4.refs_3_), channel_id=1, source_target_pairs={{0,2},{2,4},{4,6},{6,7},{7,5},{5,3},{3,1},{1,0},{8,10},{10,12},{12... | collective-permute-start | bytes 786440 | tf_op jit(solution)/shard_map/ppermute | solution.py:152
  93.7 8.4 %collective-permute-start.8 = (bf16[128,1024]{1,0:T(8,128)(2,1)S(1)}, bf16[128,1024]{1,0:T(8,128)(2,1)S(1)}, u32[]{:S(2)}, u32[]{:S(2)}) collective-permute-start(bf16[128,1024]{1,0:T(8,128)(2,1)S(1)} %collective-permute-done.7.refs_6_), channel_id=1, source_target_pairs={{0,1},{2,0},{4,2},{6,4},{7,6},{5,7},{3,5},{1,3},{8,9},{10,8},{12,1... | collective-permute-start | bytes 786440 | tf_op jit(solution)/shard_map/ppermute | solution.py:155
  93.7 8.4 %collective-permute-start.12 = (bf16[128,1024]{1,0:T(8,128)(2,1)S(1)}, bf16[128,1024]{1,0:T(8,128)(2,1)S(1)}, u32[]{:S(2)}, u32[]{:S(2)}) collective-permute-start(bf16[128,1024]{1,0:T(8,128)(2,1)S(1)} %collective-permute-done.4.refs_3_), channel_id=1, source_target_pairs={{0,8},{8,0},{16,24},{24,16},{1,9},{9,1},{17,25},{25,17},{2,10},{10... | collective-permute-start | bytes 786440 | tf_op jit(solution)/shard_map/ppermute | solution.py:157
  93.8 8.3 %collective-permute-start.13 = (bf16[128,1024]{1,0:T(8,128)(2,1)S(1)}, bf16[128,1024]{1,0:T(8,128)(2,1)S(1)}, u32[]{:S(2)}, u32[]{:S(2)}) collective-permute-start(bf16[128,1024]{1,0:T(8,128)(2,1)S(1)} %collective-permute-done.5.refs_4_), channel_id=1, source_target_pairs={{0,8},{8,0},{16,24},{24,16},{1,9},{9,1},{17,25},{25,17},{2,10},{10... | collective-permute-start | bytes 786440 | tf_op jit(solution)/shard_map/ppermute | solution.py:157
  94.3 7.9 %collective-permute-start.15 = (bf16[128,1024]{1,0:T(8,128)(2,1)S(1)}, bf16[128,1024]{1,0:T(8,128)(2,1)S(1)}, u32[]{:S(2)}, u32[]{:S(2)}) collective-permute-start(bf16[128,1024]{1,0:T(8,128)(2,1)S(1)} %collective-permute-done.7.refs_6_), channel_id=1, source_target_pairs={{0,8},{8,0},{16,24},{24,16},{1,9},{9,1},{17,25},{25,17},{2,10},{10... | collective-permute-start | bytes 786440 | tf_op jit(solution)/shard_map/ppermute | solution.py:157
  99.3 2.9 %collective-permute-start.14 = (bf16[128,1024]{1,0:T(8,128)(2,1)S(1)}, bf16[128,1024]{1,0:T(8,128)(2,1)S(1)}, u32[]{:S(2)}, u32[]{:S(2)}) collective-permute-start(bf16[128,1024]{1,0:T(8,128)(2,1)S(1)} %collective-permute-done.6.refs_5_), channel_id=1, source_target_pairs={{0,8},{8,0},{16,24},{24,16},{1,9},{9,1},{17,25},{25,17},{2,10},{10... | collective-permute-start | bytes 786440 | tf_op jit(solution)/shard_map/ppermute | solution.py:157
  102.1 1.5 collective-permute-start.16
  105.9 11.2 %collective-permute-start.18 = (bf16[192,1024]{1,0:T(8,128)(2,1)S(1)}, bf16[192,1024]{1,0:T(8,128)(2,1)S(1)}, u32[]{:S(2)}, u32[]{:S(2)}) collective-permute-start(bf16[192,1024]{1,0:T(8,128)(2,1)S(1)} %get-tuple-element.20), channel_id=1, source_target_pairs={{0,16},{8,24},{16,0},{24,8},{1,17},{9,25},{17,1},{25,9},{2,18},{10... | collective-permute-start | bytes 1179656 | tf_op jit(solution)/shard_map/ppermute | solution.py:700
  118.5 5.0 %copy-start.13 = (bf16[32,8,1536]{2,1,0:T(8,128)(2,1)}, bf16[32,8,1536]{2,1,0:T(8,128)(2,1)S(1)}, u32[]{:S(2)}) copy-start(bf16[32,8,1536]{2,1,0:T(8,128)(2,1)S(1)} %all-to-all-done.1) | copy-start | bytes 2359300
  118.5 26.6 %all-to-all-start = ((bf16[32,8,1536]{2,1,0:T(8,128)(2,1)}), bf16[32,8,1536]{2,1,0:T(8,128)(2,1)S(1)}, u32[]{:S(2)}, u32[]{:S(2)}) async-start(bf16[32,8,1536]{2,1,0:T(8,128)(2,1)} %bitcast.15), calls=%async_computation | async-start | bytes 1572864 | tf_op jit(solution)/shard_map/all_to_all | solution.py:693
  145.0 0.9 copy-start.14
  145.9 12.1 %copy-start.17 = (s32[1,192]{1,0:T(1,128)S(1)}, s32[1,192]{1,0:T(1,128)}, u32[]{:S(2)}) copy-start(s32[1,192]{1,0:T(1,128)} %param.22) | copy-start | bytes 2308
  145.9 12.9 %copy-start.3 = (bf16[256,1536]{1,0:T(8,128)(2,1)S(1)}, bf16[256,1536]{1,0:T(8,128)(2,1)}, u32[]{:S(2)}) copy-start(bf16[256,1536]{1,0:T(8,128)(2,1)} %get-tuple-element.32.refs_0_) | copy-start | bytes 2359300
  155.3 41.5 %all-to-all-start.2 = ((bf16[32,8,3072]{2,1,0:T(8,128)(2,1)}), bf16[32,8,3072]{2,1,0:T(8,128)(2,1)S(1)}, u32[]{:S(2)}, u32[]{:S(2)}) async-start(bf16[32,8,3072]{2,1,0:T(8,128)(2,1)} %bitcast.32), calls=%async_computation.2 | async-start | bytes 3145728 | tf_op jit(solution)/shard_map/all_to_all | solution.py:693
  158.8 1.4 copy-start.1
  160.2 1.2 copy-start.2
  161.5 1.1 copy-start.4
  196.8 1.2 copy-start.12

commit v3 on v2

--- a/solution.py
+++ b/solution.py
@@ -12,13 +12,12 @@
 HEAD_DIMENSION = 128
 CORES = 2
 KEY_BLOCK = 256
-KEY_STEP = 128
+KEY_STEP = 16
 ROW_BLOCK = 64
 EMPTY = 1e30
 MASKED = -1e30
 CHUNKS = 2
 LIMIT = 20 * 2**20
-ALMOST_ALL = 61_400_000
 VMEM, SMEM, ANY, HBM = pltpu.VMEM, pltpu.SMEM, pl.ANY, pltpu.HBM
 TILES = 4
 
@@ -38,6 +37,10 @@
         cost_estimate=pl.CostEstimate(flops=int(flops), bytes_accessed=int(moved), transcendentals=0),
         compiler_params=pltpu.CompilerParams(vmem_limit_bytes=limit or LIMIT),
     )
+
+
+def in_hbm(x):
+    return pltpu.with_memory_space_constraint(x, pltpu.HBM)
 
 
 def dot(a, b, dims=((1,), (0,))):
@@ -74,13 +77,16 @@
         lane = [pl.multiple_of(scal[1] + (group * heads + h) * hd, hd) for h in range(heads)]
         return jnp.concatenate([q_ref[at, pl.ds(n, hd)] for n in lane], axis=0)
 
-    def scores(i, q, col):
+    def doc_starts(i):
+        here = pl.multiple_of(base + i * ROW_BLOCK, ROW_BLOCK)
+        earlier = dcol_ref[...] < drow_ref[pl.ds(here, ROW_BLOCK), :]
+        return jnp.sum(earlier.astype(f32), axis=1, keepdims=True).astype(jnp.int32)
+
+    def scores(i, q, col, begin):
         col = pl.multiple_of(col, KEY_STEP)
-        here = pl.multiple_of(base + i * ROW_BLOCK, ROW_BLOCK)
         s = dot(q, k_scr[pl.ds(col, KEY_BLOCK), :], ((1,), (1,))) * scale
-        visible = (row_in + here >= lane_pos + col) & (
-            drow_ref[pl.ds(here, ROW_BLOCK), :] == dcol_ref[:, pl.ds(col, KEY_BLOCK)]
-        )
+        key_pos = lane_pos + col
+        visible = (row_in + (base + i * ROW_BLOCK) >= key_pos) & (key_pos >= begin)
         s = jnp.where(visible[None], s.reshape(heads, ROW_BLOCK, KEY_BLOCK), MASKED)
         return s.reshape(rows, KEY_BLOCK)
 
@@ -89,19 +95,22 @@
 
     starts = [first[scal[0] * blocks + i] * KEY_STEP for i in range(blocks)]
     for i in range(blocks):
-        s = scores(i, queries(i), starts[i])
+        s = scores(i, queries(i), starts[i], doc_starts(i))
         top = jnp.max(s, axis=1, keepdims=True)
         p = jnp.exp2(s - top)
         m_scr[i] = top
         l_scr[i] = jnp.sum(p, axis=1, keepdims=True)
         a_scr[i] = dot(p.astype(bf16), values(starts[i]))
 
+    trips = 1
     for i in range(blocks):
-        trips = (base + (i + 1) * ROW_BLOCK - starts[i] + KEY_BLOCK - 1) // KEY_BLOCK
-
-        def more(j, carry):
-            col = starts[i] + j * KEY_BLOCK
-            s = scores(i, queries(i), col)
+        need = (base + (i + 1) * ROW_BLOCK - starts[i] + KEY_BLOCK - 1) // KEY_BLOCK
+        trips = jnp.maximum(trips, need)
+
+    def more(j, carry):
+        for i in range(blocks):
+            col = jnp.minimum(starts[i] + j * KEY_BLOCK, span)
+            s = scores(i, queries(i), col, doc_starts(i))
             old = m_scr[i]
             top = jnp.maximum(old, jnp.max(s, axis=1, keepdims=True))
             p = jnp.exp2(s - top)
@@ -109,9 +118,9 @@
             m_scr[i] = top
             l_scr[i] = l_scr[i] * fade + jnp.sum(p, axis=1, keepdims=True)
             a_scr[i] = a_scr[i] * fade + dot(p.astype(bf16), values(col))
-            return carry
-
-        lax.fori_loop(1, trips, more, 0)
+        return carry
+
+    lax.fori_loop(1, trips, more, 0)
 
     for i in range(blocks):
         out = (a_scr[i] * (1.0 / l_scr[i])).astype(bf16)
@@ -300,7 +309,7 @@
     return call(
         functools.partial(pack_kernel, slots, parts, chunk),
         [
-            jax.ShapeDtypeStruct((slots.rows, width), bf16),
+            pltpu.HBM((slots.rows, width), bf16),
             jax.ShapeDtypeStruct((tokens, cols * CHUNKS), bf16),
         ],
         4 * slots.rows * tokens * cols,
@@ -369,48 +378,34 @@
     return jnp.concatenate(rows, axis=0), live
 
 
-def times(x, w_scr, copies, sum_scr):
-    n = w_scr.shape[0] // len(copies)
-    for t, copy in enumerate(copies):
-        copy.wait()
-        at = slice(t * n, (t + 1) * n)
-        sum_scr[...] += dot(x[:, at], w_scr[at])
-
-
-def encode_kernel(slots, block_ref, bias_ref, w_ref, out_ref, kept_ref, w_scr, o_scr, sems, kept_sem, out_sem):
+def encode_kernel(slots, block_ref, bias_ref, w_ref, out_ref, kept_ref, w_scr, sems, kept_sem):
     cols = w_scr.shape[0]
     copies = row_tiles(w_ref.at[0], w_scr, sems, 0)
     kept = pltpu.make_async_copy(block_ref, kept_ref, kept_sem)
     kept.start()
     x, _ = centered_rows(slots, block_ref, bias_ref[:, :cols])
-    o_scr[...] = jnp.zeros_like(o_scr)
-    times(x, w_scr, copies, o_scr)
-    out = pltpu.make_async_copy(o_scr, out_ref, out_sem)
-    out.start()
+    for copy in copies:
+        copy.wait()
+    out_ref[...] = dot(x, w_scr[...]).astype(bf16)
     kept.wait()
-    out.wait()
 
 
 def encode(slots, block, dec_bias, enc, cols):
     hidden = enc.shape[2]
     n = slots.rows * slots.groups
-    one = pltpu.SemaphoreType.DMA
     return call(
         functools.partial(encode_kernel, slots),
-        [jax.ShapeDtypeStruct((n, hidden), f32), jax.ShapeDtypeStruct(block.shape, bf16)],
+        [jax.ShapeDtypeStruct((n, hidden), bf16), pltpu.HBM(block.shape, bf16)],
         2 * n * cols * hidden,
         2 * cols * hidden + 2 * block.size + 4 * n * hidden,
         [VMEM, VMEM, HBM],
-        [HBM, HBM],
+        [VMEM, HBM],
         [
             pltpu.VMEM((cols, hidden), bf16),
-            pltpu.VMEM((n, hidden), f32),
             pltpu.SemaphoreType.DMA((TILES,)),
-            one,
-            one,
+            pltpu.SemaphoreType.DMA,
         ],
-        limit=ALMOST_ALL,
-    )(block, dec_bias, enc)
+    )(block, dec_bias, in_hbm(enc))
 
 
 def middle_kernel(
@@ -420,9 +415,9 @@
 ):
     cols = e_scr.shape[0]
     _, model = d_scr.shape
+    e_copies = row_tiles(enc_ref.at[0], e_scr, e_sems, model - cols)
     prev = pltpu.make_async_copy(prev_ref, p_scr, p_sem)
     prev.start()
-    e_copies = row_tiles(enc_ref.at[0], e_scr, e_sems, model - cols)
     cuts = slots.cuts or 2
     cut = model // cuts
     d_copies = []
@@ -433,14 +428,16 @@
         )
         d_copies[-1].start()
     kept = pltpu.make_async_copy(block_ref, kept_ref, kept_sem)
-    kept.start()
     x, live = centered_rows(slots, block_ref, bias_ref[:, model - cols :])
     n = slots.rows
+    for copy in e_copies:
+        copy.wait()
+    kept.start()
     prev.wait()
-    times(x, e_scr, e_copies, p_scr)
+    total = dot(x, e_scr[...]) + p_scr[...].astype(f32) + enc_bias_ref[...]
     for g, a in enumerate(live):
         rows = slice(g * n, (g + 1) * n)
-        pre = jnp.maximum(p_scr[rows] + enc_bias_ref[...], 0.0)
+        pre = jnp.maximum(total[rows], 0.0)
         latent_scr[rows] = jnp.where(a, pre, 0.0).astype(bf16)
     latent = pltpu.make_async_copy(latent_scr, latent_out, latent_sem)
     latent.start()
@@ -485,9 +482,9 @@
     return call(
         functools.partial(middle_kernel, slots),
         [
-            jax.ShapeDtypeStruct((n, hidden), bf16),
-            jax.ShapeDtypeStruct(out, bf16),
-            jax.ShapeDtypeStruct(block.shape, bf16),
+            pltpu.HBM((n, hidden), bf16),
+            pltpu.HBM(out, bf16),
+            pltpu.HBM(block.shape, bf16),
         ],
         2 * n * (cols + model) * hidden,
         2 * (cols + model) * hidden + 6 * block.size + 6 * n * hidden,
@@ -496,7 +493,7 @@
         [
             pltpu.VMEM((cols, hidden), bf16),
             pltpu.VMEM((hidden, model), bf16),
-            pltpu.VMEM((n, hidden), f32),
+            pltpu.VMEM((n, hidden), bf16),
             pltpu.VMEM((n, hidden), bf16),
             pltpu.VMEM(out, bf16),
             pltpu.SemaphoreType.DMA((TILES,)),
@@ -504,8 +501,7 @@
             one, one, one,
             pltpu.SemaphoreType.DMA((slots.full * cuts + 1,)),
         ],
-        limit=ALMOST_ALL,
-    )(block, dec_bias, enc_bias, enc, prev, dec)
+    )(block, dec_bias, enc_bias, in_hbm(enc), in_hbm(prev), in_hbm(dec))
 
 
 def grad_kernel(slots, latent_ref, built_ref, *refs):
@@ -589,8 +585,7 @@
         [VMEM] * 4 + [HBM],
         [HBM, HBM],
         [scr, scr, scr, pltpu.SemaphoreType.DMA((slots.cuts or 2, 2)), pltpu.SemaphoreType.DMA],
-        limit=ALMOST_ALL,
-    )(keys, kept, block, dec_bias, rows)
+    )(keys, kept, block, dec_bias, in_hbm(rows))
 
 
 def shards(
@@ -659,7 +654,7 @@
         for j in range(CHUNKS)
     ]
 
-    doc_col = jnp.concatenate([doc_ids, jnp.full((1, KEY_BLOCK), -1, jnp.int32)], axis=1)
+    doc_col = doc_ids
     doc_row = doc_ids.reshape(span, 1)
     starts = jnp.sum(
         (doc_ids < doc_ids[0, ::ROW_BLOCK][:, None]).astype(jnp.int32), axis=1

time: 203 us -> 198 us (0.975)
  Pallas kernels: 41.8 us -> 39.2 us
    all_to_all x3, starting transfers between devices: 15.3 us -> 12.1 us  [to_all(): lax.all_to_all(block.reshape(devices, 8, block.shape[1]), ('seq', 'exp'),...]
    pallas_call x4, Pallas kernels: 9.53 us -> 12.4 us  [attend(): call(functools.partial(attention_kernel, heads, parts, group), jax.ShapeD...]
    pallas_call x1, Pallas kernels: 5.29 us -> 3.1 us  [encode(): call(functools.partial(encode_kernel, slots), [jax.ShapeDtypeStruct((n, h...]
    unnamed x38 -> x36, local copies, waits for them, and re-layouts: 6.6 us -> 5.49 us
  transfers between devices with their start and end apart: 38 -> 38, of which waited for: 12 -> 13; matrix products, arithmetic and copies ran while one was open for 3% -> 3% of each run, Pallas kernels for 14% -> 15%
where the time goes in v3:
time: 198 us
  waiting for transfers between devices  106 us (54%)
  Pallas kernels  39.2 us (20%)
  starting transfers between devices  38.9 us (20%)
  local copies, waits for them, and re-layouts  10.3 us (5%)
  other arithmetic  2.32 us (1%)
    all_to_all x3, waiting for transfers between devices, to_all(): lax.all_to_all(block.reshape(devices, 8, block.shape[1]), ('seq', 'exp'),...  48.4 us
    ppermute x7, waiting for transfers between devices, ring_gather(): fw = lax.ppermute(fw, 'exp', ahead)  26.6 us
    ppermute x7, starting transfers between devices, ring_gather(): fw = lax.ppermute(fw, 'exp', ahead)  17.4 us
    ppermute x7, waiting for transfers between devices, ring_gather(): bw = lax.ppermute(bw, 'exp', back)  17.1 us
    pallas_call x4, Pallas kernels, attend(): call(functools.partial(attention_kernel, heads, parts, group), jax.ShapeD...  12.4 us
    all_to_all x3, starting transfers between devices, to_all(): lax.all_to_all(block.reshape(devices, 8, block.shape[1]), ('seq', 'exp'),...  12.1 us
    ppermute x2, waiting for transfers between devices, shards(): lax.ppermute(part, 'seq', over(chips - d))  9.52 us
    pallas_call x1, Pallas kernels, middle(): call(functools.partial(middle_kernel, slots), [pltpu.HBM((n, hidden), bf1...  7.55 us
  transfers between devices with their start and end apart: 38, of which 13 were waited for; matrix products, arithmetic and copies ran while one was open for 3% of the time, Pallas kernels for 15%

profile of v3, /device:TPU:0, one launch (start us, length us, event | category | flops | bytes accessed | tf_op | source)
XLA Modules:
  0.0 197.6 jit_solution(10425737780202835618)
XLA Ops:
  0.6 1.1 fusion.1
  1.7 3.1 %collective-permute-start.19 = (bf16[128,1024]{1,0:T(8,128)(2,1)S(1)}, bf16[128,1024]{1,0:T(8,128)(2,1)S(1)}, u32[]{:S(2)}, u32[]{:S(2)}) collective-permute-start(bf16[128,1024]{1,0:T(8,128)(2,1)S(1)} %get-tuple-element.36.refs_0_), channel_id=1, source_target_pairs={{0,2},{2,4},{4,6},{6,7},{7,5},{5,3},{3,1},{1,0},{8,10},{10,12},{12... | collective-permute-start | bytes 786440 | tf_op jit(solution)/shard_map/ppermute | solution.py:161
  4.8 1.1 dynamic-slice_bitcast_fusion.3
  5.9 5.2 %collective-permute-done.19.refs_1_ = bf16[128,1024]{1,0:T(8,128)(2,1)S(1)} collective-permute-done((bf16[128,1024]{1,0:T(8,128)(2,1)S(1)}, bf16[128,1024]{1,0:T(8,128)(2,1)S(1)}, u32[]{:S(2)}, u32[]{:S(2)}) %collective-permute-start.19) | collective-permute-done | bytes 262176 | tf_op jit(solution)/shard_map/ppermute | solution.py:161
  11.1 1.8 collective-permute-start.21
  12.9 1.6 collective-permute-start
  14.4 2.1 %dynamic-slice_bitcast_fusion = bf16[192,2048]{1,0:T(8,128)(2,1)} fusion(bf16[1,192,4096]{2,1,0:T(8,128)(2,1)} %param.12, s32[]{:T(128)S(6)} %select_n.93), kind=kLoop, calls=%fused_computation | loop fusion | bytes 1572868 | tf_op jit(solution)/shard_map/dynamic_slice | solution.py:628
  16.5 0.5 collective-permute-start.17
  17.1 2.4 %collective-permute-done = bf16[192,512]{1,0:T(8,128)(2,1)S(1)} collective-permute-done((bf16[192,512]{1,0:T(8,128)(2,1)S(1)}, bf16[192,512]{1,0:T(8,128)(2,1)S(1)}, u32[]{:S(2)}, u32[]{:S(2)}) %collective-permute-start) | collective-permute-done | bytes 196640 | tf_op jit(solution)/shard_map/ppermute | solution.py:634
  19.5 0.4 collective-permute-start.22
  19.9 1.7 collective-permute-start.23
  21.6 1.2 add_multiply_fusion.1
  23.0 5.4 %collective-permute-done.22.refs_4_ = bf16[128,1024]{1,0:T(8,128)(2,1)} collective-permute-done((bf16[128,1024]{1,0:T(8,128)(2,1)S(1)}, bf16[128,1024]{1,0:T(8,128)(2,1)}, u32[]{:S(2)}, u32[]{:S(2)}) %collective-permute-start.22) | collective-permute-done | bytes 262176 | tf_op jit(solution)/shard_map/ppermute | solution.py:164
  28.3 0.7 copy-done.9
  29.0 0.4 collective-permute-start.24
  29.4 1.7 collective-permute-start.25
  31.1 0.1 slice.9
  31.2 0.2 copy.22.drow_ref
  31.4 0.1 concatenate.20.scal
  31.5 0.8 pad_add_fusion.1.order
  32.3 0.2 convert_reduce_fusion
  32.6 0.5 collective-permute-start.30
  33.1 5.0 %collective-permute-done.24.refs_6_ = bf16[128,1024]{1,0:T(8,128)(2,1)} collective-permute-done((bf16[128,1024]{1,0:T(8,128)(2,1)}, bf16[128,1024]{1,0:T(8,128)(2,1)}, u32[]{:S(2)}, u32[]{:S(2)}) %collective-permute-start.24) | collective-permute-done | bytes 262176 | tf_op jit(solution)/shard_map/ppermute | solution.py:164
  38.1 0.5 collective-permute-start.32
  38.7 4.4 %shard_map.149.refs_16_ = bf16[192,1024]{1,0:T(8,128)(2,1)S(1)} custom-call(s32[6]{0:T(128)S(1)} %concatenate.25.scal, s32[12]{0:T(128)S(1)} %and_select_fusion.2.first, bf16[192,2048]{1,0:T(8,128)(2,1)S(1)} %collective-permute-done.17.q_ref, bf16[384,512]{1,0:T(8,128)(2,1)S(1)} %pad_maximum_fusion.mine_ref, ...), custom_call_target="tpu_custom_call" | custom-call | flops 301989888 | bytes 1572864 | tf_op jit(solution)/shard_map/pallas_call | solution.py:141
  43.1 4.4 %shard_map.150.refs_17_ = bf16[192,1024]{1,0:T(8,128)(2,1)S(1)} custom-call(s32[6]{0:T(128)S(1)} %concatenate.25.scal, s32[12]{0:T(128)S(1)} %and_select_fusion.2.first, bf16[192,2048]{1,0:T(8,128)(2,1)S(1)} %collective-permute-done.17.q_ref, bf16[384,512]{1,0:T(8,128)(2,1)S(1)} %pad_maximum_fusion.mine_ref, ...), custom_call_target="tpu_custom_call" | custom-call | flops 301989888 | bytes 1572864 | tf_op jit(solution)/shard_map/pallas_call | solution.py:141
  47.5 1.6 collective-permute-start.2
  49.1 0.5 collective-permute-start.3
  49.6 2.7 %shard_map.153 = (bf16[2048,1024]{1,0:T(8,128)(2,1)S(1)}, bf16[192,1024]{1,0:T(8,128)(2,1)S(1)}) custom-call(s32[16]{0:T(128)S(1)} %pad_add_fusion.1.order, bf16[128,1024]{1,0:T(8,128)(2,1)S(1)} %get-tuple-element.36.refs_0_, bf16[128,1024]{1,0:T(8,128)(2,1)S(1)} %collective-permute-done.19.refs_1_, bf16[128,1024]{1,0:T(8,128)(2,1)S(1)} %copy-done.6, ...), custom_call_target="tpu_custom_call" | custom-call | flops 805306368 | bytes 9175040 | tf_op jit(solution)/shard_map/pallas_call | solution.py:192
  52.4 4.0 %collective-permute-done.3.refs_2_ = bf16[128,1024]{1,0:T(8,128)(2,1)} collective-permute-done((bf16[128,1024]{1,0:T(8,128)(2,1)S(1)}, bf16[128,1024]{1,0:T(8,128)(2,1)}, u32[]{:S(2)}, u32[]{:S(2)}) %collective-permute-start.3) | collective-permute-done | bytes 262176 | tf_op jit(solution)/shard_map/ppermute | solution.py:164
  56.4 1.7 collective-permute-start.5
  58.0 2.0 shard_map.147.refs_0_
  60.0 1.8 shard_map.148.refs_1_
  61.8 1.0 shard_map.154.own_ref
  62.8 1.0 collective-permute-done.34.refs_0_
  63.8 1.3 shard_map.155
  65.1 4.5 %all-to-all-start.1 = ((bf16[32,8,1536]{2,1,0:T(8,128)(2,1)}), bf16[32,8,1536]{2,1,0:T(8,128)(2,1)S(1)}, u32[]{:S(2)}, u32[]{:S(2)}) async-start(bf16[32,8,1536]{2,1,0:T(8,128)(2,1)} %bitcast.41), calls=%async_computation.1 | async-start | bytes 1572864 | tf_op jit(solution)/shard_map/all_to_all | solution.py:688
  69.6 1.8 collective-permute-start.4
  71.4 0.3 collective-permute-start.7
  71.7 0.5 collective-permute-start.10
  72.2 16.5 %collective-permute-done.4.refs_3_ = bf16[128,1024]{1,0:T(8,128)(2,1)S(1)} collective-permute-done((bf16[128,1024]{1,0:T(8,128)(2,1)}, bf16[128,1024]{1,0:T(8,128)(2,1)S(1)}, u32[]{:S(2)}, u32[]{:S(2)}) %collective-permute-start.4) | collective-permute-done | bytes 262176 | tf_op jit(solution)/shard_map/ppermute | solution.py:161
  88.7 5.7 %collective-permute-start.6 = (bf16[128,1024]{1,0:T(8,128)(2,1)S(1)}, bf16[128,1024]{1,0:T(8,128)(2,1)S(1)}, u32[]{:S(2)}, u32[]{:S(2)}) collective-permute-start(bf16[128,1024]{1,0:T(8,128)(2,1)S(1)} %collective-permute-done.4.refs_3_), channel_id=1, source_target_pairs={{0,2},{2,4},{4,6},{6,7},{7,5},{5,3},{3,1},{1,0},{8,10},{10,12},{12... | collective-permute-start | bytes 786440 | tf_op jit(solution)/shard_map/ppermute | solution.py:161
  94.5 0.5 collective-permute-start.13
  95.0 4.9 %collective-permute-done.6.refs_5_ = bf16[128,1024]{1,0:T(8,128)(2,1)S(1)} collective-permute-done((bf16[128,1024]{1,0:T(8,128)(2,1)S(1)}, bf16[128,1024]{1,0:T(8,128)(2,1)S(1)}, u32[]{:S(2)}, u32[]{:S(2)}) %collective-permute-start.6) | collective-permute-done | bytes 262176 | tf_op jit(solution)/shard_map/ppermute | solution.py:161
  100.0 2.8 %collective-permute-done.8.refs_7_ = bf16[128,1024]{1,0:T(8,128)(2,1)S(1)} collective-permute-done((bf16[128,1024]{1,0:T(8,128)(2,1)S(1)}, bf16[128,1024]{1,0:T(8,128)(2,1)S(1)}, u32[]{:S(2)}, u32[]{:S(2)}) %collective-permute-start.8) | collective-permute-done | bytes 262176 | tf_op jit(solution)/shard_map/ppermute | solution.py:164
  102.8 1.5 collective-permute-done.16.refs_15_
  104.3 2.3 %shard_map.151 = (bf16[2048,1024]{1,0:T(8,128)(2,1)S(1)}, bf16[192,1024]{1,0:T(8,128)(2,1)S(1)}) custom-call(s32[16]{0:T(128)S(1)} %pad_add_fusion.1.order, bf16[128,1024]{1,0:T(8,128)(2,1)S(1)} %get-tuple-element.37.refs_0_, bf16[128,1024]{1,0:T(8,128)(2,1)} %collective-permute-done.2.refs_1_, bf16[128,1024]{1,0:T(8,128)(2,1)} %collective-permute-done.3.refs_2_, ...), custom_call_target="tpu_custom_call" | custom-call | flops 805306368 | bytes 9175040 | tf_op jit(solution)/shard_map/pallas_call | solution.py:192
  106.6 1.7 collective-permute-start.18
  108.3 1.0 shard_map.152.own_ref
  109.3 8.5 %collective-permute-done.18.refs_0_ = bf16[192,1024]{1,0:T(8,128)(2,1)S(1)} collective-permute-done((bf16[192,1024]{1,0:T(8,128)(2,1)S(1)}, bf16[192,1024]{1,0:T(8,128)(2,1)S(1)}, u32[]{:S(2)}, u32[]{:S(2)}) %collective-permute-start.18) | collective-permute-done | bytes 393248 | tf_op jit(solution)/shard_map/ppermute | solution.py:695
  117.9 1.3 shard_map.156
  119.1 4.9 %all-to-all-start = ((bf16[32,8,1536]{2,1,0:T(8,128)(2,1)}), bf16[32,8,1536]{2,1,0:T(8,128)(2,1)S(1)}, u32[]{:S(2)}, u32[]{:S(2)}) async-start(bf16[32,8,1536]{2,1,0:T(8,128)(2,1)} %bitcast.42), calls=%async_computation | async-start | bytes 1572864 | tf_op jit(solution)/shard_map/all_to_all | solution.py:688
  124.1 3.1 %shard_map.157 = (bf16[512,1024]{1,0:T(8,128)(2,1)S(1)}, bf16[256,1536]{1,0:T(8,128)(2,1)}) custom-call(bf16[256,1536]{1,0:T(8,128)(2,1)S(1)} %bitcast.34, f32[1,2048]{1,0:T(1,128)S(1)} %bitcast.37, bf16[1,2048,1024]{2,1,0:T(8,128)(2,1)} %enc_ref.1), custom_call_target="tpu_custom_call" | custom-call | flops 1073741824 | bytes 4980736 | tf_op jit(solution)/shard_map/pallas_call | solution.py:396
  127.2 1.0 copy-done.13
  128.2 17.5 %all-to-all-done = bf16[32,8,1536]{2,1,0:T(8,128)(2,1)S(1)} async-done(((bf16[32,8,1536]{2,1,0:T(8,128)(2,1)}), bf16[32,8,1536]{2,1,0:T(8,128)(2,1)S(1)}, u32[]{:S(2)}, u32[]{:S(2)}) %all-to-all-start) | async-done | bytes 786464 | tf_op jit(solution)/shard_map/all_to_all | solution.py:688
  145.7 7.6 %shard_map.158 = (bf16[512,1024]{1,0:T(8,128)(2,1)}, bf16[256,3072]{1,0:T(8,128)(2,1)}, bf16[256,1536]{1,0:T(8,128)(2,1)}) custom-call(bf16[256,1536]{1,0:T(8,128)(2,1)S(1)} %bitcast.35, f32[1,2048]{1,0:T(1,128)S(1)} %bitcast.38, f32[1,1024]{1,0:T(1,128)S(1)} %copy-done.14, bf16[1,2048,1024]{2,1,0:T(8,128)(2,1)} %enc_ref.1, bf16[512,1024]{1,0:T(8,128)(2,1)} %copy-done.13, ...), custom_call_target="tpu_custom_call" | custom-call | flops 3221225472 | bytes 11796480 | tf_op jit(solution)/shard_map/pallas_call | solution.py:482
  153.3 2.7 %all-to-all-start.2 = ((bf16[32,8,3072]{2,1,0:T(8,128)(2,1)}), bf16[32,8,3072]{2,1,0:T(8,128)(2,1)S(1)}, u32[]{:S(2)}, u32[]{:S(2)}) async-start(bf16[32,8,3072]{2,1,0:T(8,128)(2,1)} %bitcast.33), calls=%async_computation.2 | async-start | bytes 3145728 | tf_op jit(solution)/shard_map/all_to_all | solution.py:688
  156.0 0.1 copy.26.kept_ref
  156.2 1.4 copy-done.1
  157.6 1.2 copy-done.2
  158.8 1.1 copy-done.4
  159.9 4.0 %shard_map.160 = bf16[1,1024,2048]{2,1,0:T(8,128)(2,1)} custom-call(bf16[512,1024]{1,0:T(8,128)(2,1)S(1)} %copy-done.2, bf16[256,3072]{1,0:T(8,128)(2,1)S(1)} %copy-done.1, bf16[256,1536]{1,0:T(8,128)(2,1)S(1)} %copy-done.3, bf16[256,1536]{1,0:T(8,128)(2,1)S(1)} %copy-done.4), custom_call_target="tpu_custom_call" | custom-call | flops 2147483648 | bytes 7340032 | tf_op jit(solution)/shard_map/pallas_call | solution.py:532
  163.9 30.9 %all-to-all-done.2 = bf16[32,8,3072]{2,1,0:T(8,128)(2,1)S(1)} async-done(((bf16[32,8,3072]{2,1,0:T(8,128)(2,1)}), bf16[32,8,3072]{2,1,0:T(8,128)(2,1)S(1)}, u32[]{:S(2)}, u32[]{:S(2)}) %all-to-all-start.2) | async-done | bytes 1572896 | tf_op jit(solution)/shard_map/all_to_all | solution.py:688
  194.8 2.6 %shard_map.159 = (bf16[192,2048]{1,0:T(8,128)(2,1)}, bf16[192,2048]{1,0:T(8,128)(2,1)}) custom-call(s32[3,192]{1,0:T(4,128)S(1)} %pad_add_fusion.keys_ref, s32[192,1]{1,0:T(8,128)S(1)} %copy.26.kept_ref, bf16[256,3072]{1,0:T(8,128)(2,1)S(1)} %bitcast.32, f32[1,2048]{1,0:T(1,128)S(1)} %bitcast.39, bf16[192,2048]{1,0:T(8,128)(2,1)} %get-tuple-element.24.rows_ref), custom_call_target="tpu_custom_call" | custom-call | flops 402653184 | bytes 3932160 | tf_op jit(solution)/shard_map/pallas_call | solution.py:580
  (81 shorter events, 0.8 us)
Async XLA Ops:
  0.6 30.4 %copy-start.11 = (s32[1,768]{1,0:T(1,128)S(1)}, s32[1,768]{1,0:T(1,128)}, u32[]{:S(2)}) copy-start(s32[1,768]{1,0:T(1,128)} %dcol_ref.7) | copy-start | bytes 9220
  1.7 9.4 %collective-permute-start.19 = (bf16[128,1024]{1,0:T(8,128)(2,1)S(1)}, bf16[128,1024]{1,0:T(8,128)(2,1)S(1)}, u32[]{:S(2)}, u32[]{:S(2)}) collective-permute-start(bf16[128,1024]{1,0:T(8,128)(2,1)S(1)} %get-tuple-element.36.refs_0_), channel_id=1, source_target_pairs={{0,2},{2,4},{4,6},{6,7},{7,5},{5,3},{3,1},{1,0},{8,10},{10,12},{12... | collective-permute-start | bytes 786440 | tf_op jit(solution)/shard_map/ppermute | solution.py:161
  4.8 14.7 %collective-permute-start.20 = (bf16[128,1024]{1,0:T(8,128)(2,1)S(1)}, bf16[128,1024]{1,0:T(8,128)(2,1)S(1)}, u32[]{:S(2)}, u32[]{:S(2)}) collective-permute-start(bf16[128,1024]{1,0:T(8,128)(2,1)S(1)} %get-tuple-element.36.refs_0_), channel_id=1, source_target_pairs={{0,1},{2,0},{4,2},{6,4},{7,6},{5,7},{3,5},{1,3},{8,9},{10,8},{12,1... | collective-permute-start | bytes 786440 | tf_op jit(solution)/shard_map/ppermute | solution.py:164
  4.8 18.0 %collective-permute-start.26 = (bf16[128,1024]{1,0:T(8,128)(2,1)S(1)}, bf16[128,1024]{1,0:T(8,128)(2,1)S(1)}, u32[]{:S(2)}, u32[]{:S(2)}) collective-permute-start(bf16[128,1024]{1,0:T(8,128)(2,1)S(1)} %get-tuple-element.36.refs_0_), channel_id=1, source_target_pairs={{0,8},{8,0},{16,24},{24,16},{1,9},{9,1},{17,25},{25,17},{2,10},{10... | collective-permute-start | bytes 786440 | tf_op jit(solution)/shard_map/ppermute | solution.py:166
  11.1 8.8 %collective-permute-start.21 = (bf16[128,1024]{1,0:T(8,128)(2,1)S(1)}, bf16[128,1024]{1,0:T(8,128)(2,1)}, u32[]{:S(2)}, u32[]{:S(2)}) collective-permute-start(bf16[128,1024]{1,0:T(8,128)(2,1)S(1)} %collective-permute-done.19.refs_1_), channel_id=1, source_target_pairs={{0,2},{2,4},{4,6},{6,7},{7,5},{5,3},{3,1},{1,0},{8,10},{10,12},{12... | collective-permute-start | bytes 786440 | tf_op jit(solution)/shard_map/ppermute | solution.py:161
  12.9 6.6 %collective-permute-start = (bf16[192,512]{1,0:T(8,128)(2,1)S(1)}, bf16[192,512]{1,0:T(8,128)(2,1)S(1)}, u32[]{:S(2)}, u32[]{:S(2)}) collective-permute-start(bf16[192,512]{1,0:T(8,128)(2,1)S(1)} %pad_maximum_fusion.1), channel_id=1, source_target_pairs={{0,16},{8,24},{16,0},{24,8},{1,17},{9,25},{17,1},{25,9},{2,18},{10... | collective-permute-start | bytes 589832 | tf_op jit(solution)/shard_map/ppermute | solution.py:634
  16.5 21.5 %collective-permute-start.17 = (bf16[192,2048]{1,0:T(8,128)(2,1)}, bf16[192,2048]{1,0:T(8,128)(2,1)S(1)}, u32[]{:S(2)}, u32[]{:S(2)}) collective-permute-start(bf16[192,2048]{1,0:T(8,128)(2,1)} %dynamic-slice_bitcast_fusion), channel_id=1, source_target_pairs={{0,16},{8,24},{16,0},{24,8},{1,17},{9,25},{17,1},{25,9},{2,18},{10... | collective-permute-start | bytes 2359304 | tf_op jit(solution)/shard_map/ppermute | solution.py:635
  19.5 8.8 %collective-permute-start.27 = (bf16[128,1024]{1,0:T(8,128)(2,1)S(1)}, bf16[128,1024]{1,0:T(8,128)(2,1)S(1)}, u32[]{:S(2)}, u32[]{:S(2)}) collective-permute-start(bf16[128,1024]{1,0:T(8,128)(2,1)S(1)} %collective-permute-done.19.refs_1_), channel_id=1, source_target_pairs={{0,8},{8,0},{16,24},{24,16},{1,9},{9,1},{17,25},{25,17},{2,10},{10... | collective-permute-start | bytes 786440 | tf_op jit(solution)/shard_map/ppermute | solution.py:166
  19.5 19.2 %copy-start.5 = (bf16[128,1024]{1,0:T(8,128)(2,1)}, bf16[128,1024]{1,0:T(8,128)(2,1)S(1)}, u32[]{:S(2)}) copy-start(bf16[128,1024]{1,0:T(8,128)(2,1)S(1)} %collective-permute-done.20.refs_2_) | copy-start | bytes 786436
  19.5 8.8 %collective-permute-start.22 = (bf16[128,1024]{1,0:T(8,128)(2,1)S(1)}, bf16[128,1024]{1,0:T(8,128)(2,1)}, u32[]{:S(2)}, u32[]{:S(2)}) collective-permute-start(bf16[128,1024]{1,0:T(8,128)(2,1)S(1)} %collective-permute-done.20.refs_2_), channel_id=1, source_target_pairs={{0,1},{2,0},{4,2},{6,4},{7,6},{5,7},{3,5},{1,3},{8,9},{10,8},{12,1... | collective-permute-start | bytes 786440 | tf_op jit(solution)/shard_map/ppermute | solution.py:164
  19.9 9.5 %collective-permute-start.23 = (bf16[128,1024]{1,0:T(8,128)(2,1)}, bf16[128,1024]{1,0:T(8,128)(2,1)}, u32[]{:S(2)}, u32[]{:S(2)}) collective-permute-start(bf16[128,1024]{1,0:T(8,128)(2,1)} %collective-permute-done.21.refs_3_), channel_id=1, source_target_pairs={{0,2},{2,4},{4,6},{6,7},{7,5},{5,3},{3,1},{1,0},{8,10},{10,12},{12... | collective-permute-start | bytes 786440 | tf_op jit(solution)/shard_map/ppermute | solution.py:161
  22.9 15.8 %copy-start.7 = (bf16[128,1024]{1,0:T(8,128)(2,1)}, bf16[128,1024]{1,0:T(8,128)(2,1)S(1)}, u32[]{:S(2)}) copy-start(bf16[128,1024]{1,0:T(8,128)(2,1)S(1)} %collective-permute-done.26.refs_8_) | copy-start | bytes 786436
  22.9 9.7 %collective-permute-start.1 = (bf16[384,512]{1,0:T(8,128)(2,1)S(1)}, bf16[384,512]{1,0:T(8,128)(2,1)S(1)}, u32[]{:S(2)}, u32[]{:S(2)}) collective-permute-start(bf16[384,512]{1,0:T(8,128)(2,1)S(1)} %pad_maximum_fusion.mine_ref), channel_id=1, source_target_pairs={{0,8},{8,0},{16,24},{24,16},{1,9},{9,1},{17,25},{25,17},{2,10},{10... | collective-permute-start | bytes 1179656 | tf_op jit(solution)/shard_map/ppermute | solution.py:637
  28.3 4.2 %collective-permute-start.28 = (bf16[128,1024]{1,0:T(8,128)(2,1)S(1)}, bf16[128,1024]{1,0:T(8,128)(2,1)}, u32[]{:S(2)}, u32[]{:S(2)}) collective-permute-start(bf16[128,1024]{1,0:T(8,128)(2,1)S(1)} %collective-permute-done.20.refs_2_), channel_id=1, source_target_pairs={{0,8},{8,0},{16,24},{24,16},{1,9},{9,1},{17,25},{25,17},{2,10},{10... | collective-permute-start | bytes 786440 | tf_op jit(solution)/shard_map/ppermute | solution.py:166
  28.3 0.7 copy-start.9
  29.0 9.0 %collective-permute-start.24 = (bf16[128,1024]{1,0:T(8,128)(2,1)}, bf16[128,1024]{1,0:T(8,128)(2,1)}, u32[]{:S(2)}, u32[]{:S(2)}) collective-permute-start(bf16[128,1024]{1,0:T(8,128)(2,1)} %collective-permute-done.22.refs_4_), channel_id=1, source_target_pairs={{0,1},{2,0},{4,2},{6,4},{7,6},{5,7},{3,5},{1,3},{8,9},{10,8},{12,1... | collective-permute-start | bytes 786440 | tf_op jit(solution)/shard_map/ppermute | solution.py:164
  29.4 9.2 %collective-permute-start.25 = (bf16[128,1024]{1,0:T(8,128)(2,1)}, bf16[128,1024]{1,0:T(8,128)(2,1)}, u32[]{:S(2)}, u32[]{:S(2)}) collective-permute-start(bf16[128,1024]{1,0:T(8,128)(2,1)} %collective-permute-done.23.refs_5_), channel_id=1, source_target_pairs={{0,2},{2,4},{4,6},{6,7},{7,5},{5,3},{3,1},{1,0},{8,10},{10,12},{12... | collective-permute-start | bytes 786440 | tf_op jit(solution)/shard_map/ppermute | solution.py:161
  31.5 18.0 %copy-start.10 = (bf16[128,1024]{1,0:T(8,128)(2,1)S(1)}, bf16[128,1024]{1,0:T(8,128)(2,1)}, u32[]{:S(2)}) copy-start(bf16[128,1024]{1,0:T(8,128)(2,1)} %copy-done.9) | copy-start | bytes 786436
  32.5 14.9 %collective-permute-start.29 = (bf16[128,1024]{1,0:T(8,128)(2,1)}, bf16[128,1024]{1,0:T(8,128)(2,1)S(1)}, u32[]{:S(2)}, u32[]{:S(2)}) collective-permute-start(bf16[128,1024]{1,0:T(8,128)(2,1)} %collective-permute-done.21.refs_3_), channel_id=1, source_target_pairs={{0,8},{8,0},{16,24},{24,16},{1,9},{9,1},{17,25},{25,17},{2,10},{10... | collective-permute-start | bytes 786440 | tf_op jit(solution)/shard_map/ppermute | solution.py:166
  32.6 16.5 %collective-permute-start.30 = (bf16[128,1024]{1,0:T(8,128)(2,1)}, bf16[128,1024]{1,0:T(8,128)(2,1)S(1)}, u32[]{:S(2)}, u32[]{:S(2)}) collective-permute-start(bf16[128,1024]{1,0:T(8,128)(2,1)} %collective-permute-done.22.refs_4_), channel_id=1, source_target_pairs={{0,8},{8,0},{16,24},{24,16},{1,9},{9,1},{17,25},{25,17},{2,10},{10... | collective-permute-start | bytes 786440 | tf_op jit(solution)/shard_map/ppermute | solution.py:166
  38.1 11.5 %collective-permute-start.31 = (bf16[128,1024]{1,0:T(8,128)(2,1)}, bf16[128,1024]{1,0:T(8,128)(2,1)S(1)}, u32[]{:S(2)}, u32[]{:S(2)}) collective-permute-start(bf16[128,1024]{1,0:T(8,128)(2,1)} %collective-permute-done.23.refs_5_), channel_id=1, source_target_pairs={{0,8},{8,0},{16,24},{24,16},{1,9},{9,1},{17,25},{25,17},{2,10},{10... | collective-permute-start | bytes 786440 | tf_op jit(solution)/shard_map/ppermute | solution.py:166
  38.1 11.5 %collective-permute-start.32 = (bf16[128,1024]{1,0:T(8,128)(2,1)}, bf16[128,1024]{1,0:T(8,128)(2,1)S(1)}, u32[]{:S(2)}, u32[]{:S(2)}) collective-permute-start(bf16[128,1024]{1,0:T(8,128)(2,1)} %collective-permute-done.24.refs_6_), channel_id=1, source_target_pairs={{0,8},{8,0},{16,24},{24,16},{1,9},{9,1},{17,25},{25,17},{2,10},{10... | collective-permute-start | bytes 786440 | tf_op jit(solution)/shard_map/ppermute | solution.py:166
  38.6 11.0 %collective-permute-start.33 = (bf16[128,1024]{1,0:T(8,128)(2,1)}, bf16[128,1024]{1,0:T(8,128)(2,1)S(1)}, u32[]{:S(2)}, u32[]{:S(2)}) collective-permute-start(bf16[128,1024]{1,0:T(8,128)(2,1)} %collective-permute-done.25.refs_7_), channel_id=1, source_target_pairs={{0,8},{8,0},{16,24},{24,16},{1,9},{9,1},{17,25},{25,17},{2,10},{10... | collective-permute-start | bytes 786440 | tf_op jit(solution)/shard_map/ppermute | solution.py:166
  38.7 10.9 %copy-start.6 = (bf16[128,1024]{1,0:T(8,128)(2,1)S(1)}, bf16[128,1024]{1,0:T(8,128)(2,1)}, u32[]{:S(2)}) copy-start(bf16[128,1024]{1,0:T(8,128)(2,1)} %copy-done.5) | copy-start | bytes 786436
  38.7 10.9 %copy-start.8 = (bf16[128,1024]{1,0:T(8,128)(2,1)S(1)}, bf16[128,1024]{1,0:T(8,128)(2,1)}, u32[]{:S(2)}) copy-start(bf16[128,1024]{1,0:T(8,128)(2,1)} %copy-done.7) | copy-start | bytes 786436
  43.1 9.3 %copy-start.15 = (s32[1,192]{1,0:T(1,128)S(1)}, s32[1,192]{1,0:T(1,128)}, u32[]{:S(2)}) copy-start(s32[1,192]{1,0:T(1,128)} %param.22) | copy-start | bytes 2308
  43.1 9.3 %copy-start.17 = (s32[1,192]{1,0:T(1,128)S(1)}, s32[1,192]{1,0:T(1,128)}, u32[]{:S(2)}) copy-start(s32[1,192]{1,0:T(1,128)} %param.21) | copy-start | bytes 2308
  43.1 15.0 %copy-start = (bf16[1,192,4096]{2,1,0:T(8,128)(2,1)S(1)}, bf16[1,192,4096]{2,1,0:T(8,128)(2,1)}, u32[]{:S(2)}) copy-start(bf16[1,192,4096]{2,1,0:T(8,128)(2,1)} %param.12) | copy-start | bytes 4718596
  47.5 22.1 %collective-permute-start.2 = (bf16[128,1024]{1,0:T(8,128)(2,1)S(1)}, bf16[128,1024]{1,0:T(8,128)(2,1)}, u32[]{:S(2)}, u32[]{:S(2)}) collective-permute-start(bf16[128,1024]{1,0:T(8,128)(2,1)S(1)} %get-tuple-element.37.refs_0_), channel_id=1, source_target_pairs={{0,2},{2,4},{4,6},{6,7},{7,5},{5,3},{3,1},{1,0},{8,10},{10,12},{12... | collective-permute-start | bytes 786440 | tf_op jit(solution)/shard_map/ppermute | solution.py:161
  49.1 7.3 %collective-permute-start.3 = (bf16[128,1024]{1,0:T(8,128)(2,1)S(1)}, bf16[128,1024]{1,0:T(8,128)(2,1)}, u32[]{:S(2)}, u32[]{:S(2)}) collective-permute-start(bf16[128,1024]{1,0:T(8,128)(2,1)S(1)} %get-tuple-element.37.refs_0_), channel_id=1, source_target_pairs={{0,1},{2,0},{4,2},{6,4},{7,6},{5,7},{3,5},{1,3},{8,9},{10,8},{12,1... | collective-permute-start | bytes 786440 | tf_op jit(solution)/shard_map/ppermute | solution.py:164
  52.3 11.5 %collective-permute-start.34 = (bf16[192,1024]{1,0:T(8,128)(2,1)S(1)}, bf16[192,1024]{1,0:T(8,128)(2,1)S(1)}, u32[]{:S(2)}, u32[]{:S(2)}) collective-permute-start(bf16[192,1024]{1,0:T(8,128)(2,1)S(1)} %get-tuple-element.22), channel_id=1, source_target_pairs={{0,16},{8,24},{16,0},{24,8},{1,17},{9,25},{17,1},{25,9},{2,18},{10... | collective-permute-start | bytes 1179656 | tf_op jit(solution)/shard_map/ppermute | solution.py:695
  56.4 15.1 %collective-permute-start.5 = (bf16[128,1024]{1,0:T(8,128)(2,1)}, bf16[128,1024]{1,0:T(8,128)(2,1)S(1)}, u32[]{:S(2)}, u32[]{:S(2)}) collective-permute-start(bf16[128,1024]{1,0:T(8,128)(2,1)} %collective-permute-done.3.refs_2_), channel_id=1, source_target_pairs={{0,1},{2,0},{4,2},{6,4},{7,6},{5,7},{3,5},{1,3},{8,9},{10,8},{12,1... | collective-permute-start | bytes 786440 | tf_op jit(solution)/shard_map/ppermute | solution.py:164
  65.1 54.1 %all-to-all-start.1 = ((bf16[32,8,1536]{2,1,0:T(8,128)(2,1)}), bf16[32,8,1536]{2,1,0:T(8,128)(2,1)S(1)}, u32[]{:S(2)}, u32[]{:S(2)}) async-start(bf16[32,8,1536]{2,1,0:T(8,128)(2,1)} %bitcast.41), calls=%async_computation.1 | async-start | bytes 1572864 | tf_op jit(solution)/shard_map/all_to_all | solution.py:688
  69.6 19.1 %collective-permute-start.4 = (bf16[128,1024]{1,0:T(8,128)(2,1)}, bf16[128,1024]{1,0:T(8,128)(2,1)S(1)}, u32[]{:S(2)}, u32[]{:S(2)}) collective-permute-start(bf16[128,1024]{1,0:T(8,128)(2,1)} %collective-permute-done.2.refs_1_), channel_id=1, source_target_pairs={{0,2},{2,4},{4,6},{6,7},{7,5},{5,3},{3,1},{1,0},{8,10},{10,12},{12... | collective-permute-start | bytes 786440 | tf_op jit(solution)/shard_map/ppermute | solution.py:161
  71.4 22.9 %collective-permute-start.7 = (bf16[128,1024]{1,0:T(8,128)(2,1)S(1)}, bf16[128,1024]{1,0:T(8,128)(2,1)S(1)}, u32[]{:S(2)}, u32[]{:S(2)}) collective-permute-start(bf16[128,1024]{1,0:T(8,128)(2,1)S(1)} %collective-permute-done.5.refs_4_), channel_id=1, source_target_pairs={{0,1},{2,0},{4,2},{6,4},{7,6},{5,7},{3,5},{1,3},{8,9},{10,8},{12,1... | collective-permute-start | bytes 786440 | tf_op jit(solution)/shard_map/ppermute | solution.py:164
  71.7 22.7 %collective-permute-start.9 = (bf16[128,1024]{1,0:T(8,128)(2,1)S(1)}, bf16[128,1024]{1,0:T(8,128)(2,1)S(1)}, u32[]{:S(2)}, u32[]{:S(2)}) collective-permute-start(bf16[128,1024]{1,0:T(8,128)(2,1)S(1)} %get-tuple-element.37.refs_0_), channel_id=1, source_target_pairs={{0,8},{8,0},{16,24},{24,16},{1,9},{9,1},{17,25},{25,17},{2,10},{10... | collective-permute-start | bytes 786440 | tf_op jit(solution)/shard_map/ppermute | solution.py:166
  71.7 22.8 %collective-permute-start.10 = (bf16[128,1024]{1,0:T(8,128)(2,1)}, bf16[128,1024]{1,0:T(8,128)(2,1)S(1)}, u32[]{:S(2)}, u32[]{:S(2)}) collective-permute-start(bf16[128,1024]{1,0:T(8,128)(2,1)} %collective-permute-done.2.refs_1_), channel_id=1, source_target_pairs={{0,8},{8,0},{16,24},{24,16},{1,9},{9,1},{17,25},{25,17},{2,10},{10... | collective-permute-start | bytes 786440 | tf_op jit(solution)/shard_map/ppermute | solution.py:166
  72.2 22.8 %collective-permute-start.11 = (bf16[128,1024]{1,0:T(8,128)(2,1)}, bf16[128,1024]{1,0:T(8,128)(2,1)S(1)}, u32[]{:S(2)}, u32[]{:S(2)}) collective-permute-start(bf16[128,1024]{1,0:T(8,128)(2,1)} %collective-permute-done.3.refs_2_), channel_id=1, source_target_pairs={{0,8},{8,0},{16,24},{24,16},{1,9},{9,1},{17,25},{25,17},{2,10},{10... | collective-permute-start | bytes 786440 | tf_op jit(solution)/shard_map/ppermute | solution.py:166
  88.7 11.3 %collective-permute-start.6 = (bf16[128,1024]{1,0:T(8,128)(2,1)S(1)}, bf16[128,1024]{1,0:T(8,128)(2,1)S(1)}, u32[]{:S(2)}, u32[]{:S(2)}) collective-permute-start(bf16[128,1024]{1,0:T(8,128)(2,1)S(1)} %collective-permute-done.4.refs_3_), channel_id=1, source_target_pairs={{0,2},{2,4},{4,6},{6,7},{7,5},{5,3},{3,1},{1,0},{8,10},{10,12},{12... | collective-permute-start | bytes 786440 | tf_op jit(solution)/shard_map/ppermute | solution.py:161
  94.4 8.4 %collective-permute-start.8 = (bf16[128,1024]{1,0:T(8,128)(2,1)S(1)}, bf16[128,1024]{1,0:T(8,128)(2,1)S(1)}, u32[]{:S(2)}, u32[]{:S(2)}) collective-permute-start(bf16[128,1024]{1,0:T(8,128)(2,1)S(1)} %collective-permute-done.7.refs_6_), channel_id=1, source_target_pairs={{0,1},{2,0},{4,2},{6,4},{7,6},{5,7},{3,5},{1,3},{8,9},{10,8},{12,1... | collective-permute-start | bytes 786440 | tf_op jit(solution)/shard_map/ppermute | solution.py:164
  94.4 8.4 %collective-permute-start.12 = (bf16[128,1024]{1,0:T(8,128)(2,1)S(1)}, bf16[128,1024]{1,0:T(8,128)(2,1)S(1)}, u32[]{:S(2)}, u32[]{:S(2)}) collective-permute-start(bf16[128,1024]{1,0:T(8,128)(2,1)S(1)} %collective-permute-done.4.refs_3_), channel_id=1, source_target_pairs={{0,8},{8,0},{16,24},{24,16},{1,9},{9,1},{17,25},{25,17},{2,10},{10... | collective-permute-start | bytes 786440 | tf_op jit(solution)/shard_map/ppermute | solution.py:166
  94.5 8.3 %collective-permute-start.13 = (bf16[128,1024]{1,0:T(8,128)(2,1)S(1)}, bf16[128,1024]{1,0:T(8,128)(2,1)S(1)}, u32[]{:S(2)}, u32[]{:S(2)}) collective-permute-start(bf16[128,1024]{1,0:T(8,128)(2,1)S(1)} %collective-permute-done.5.refs_4_), channel_id=1, source_target_pairs={{0,8},{8,0},{16,24},{24,16},{1,9},{9,1},{17,25},{25,17},{2,10},{10... | collective-permute-start | bytes 786440 | tf_op jit(solution)/shard_map/ppermute | solution.py:166
  95.0 7.9 %collective-permute-start.15 = (bf16[128,1024]{1,0:T(8,128)(2,1)S(1)}, bf16[128,1024]{1,0:T(8,128)(2,1)S(1)}, u32[]{:S(2)}, u32[]{:S(2)}) collective-permute-start(bf16[128,1024]{1,0:T(8,128)(2,1)S(1)} %collective-permute-done.7.refs_6_), channel_id=1, source_target_pairs={{0,8},{8,0},{16,24},{24,16},{1,9},{9,1},{17,25},{25,17},{2,10},{10... | collective-permute-start | bytes 786440 | tf_op jit(solution)/shard_map/ppermute | solution.py:166
  100.0 2.9 %collective-permute-start.14 = (bf16[128,1024]{1,0:T(8,128)(2,1)S(1)}, bf16[128,1024]{1,0:T(8,128)(2,1)S(1)}, u32[]{:S(2)}, u32[]{:S(2)}) collective-permute-start(bf16[128,1024]{1,0:T(8,128)(2,1)S(1)} %collective-permute-done.6.refs_5_), channel_id=1, source_target_pairs={{0,8},{8,0},{16,24},{24,16},{1,9},{9,1},{17,25},{25,17},{2,10},{10... | collective-permute-start | bytes 786440 | tf_op jit(solution)/shard_map/ppermute | solution.py:166
  102.8 1.5 collective-permute-start.16
  106.6 11.2 %collective-permute-start.18 = (bf16[192,1024]{1,0:T(8,128)(2,1)S(1)}, bf16[192,1024]{1,0:T(8,128)(2,1)S(1)}, u32[]{:S(2)}, u32[]{:S(2)}) collective-permute-start(bf16[192,1024]{1,0:T(8,128)(2,1)S(1)} %get-tuple-element.20), channel_id=1, source_target_pairs={{0,16},{8,24},{16,0},{24,8},{1,17},{9,25},{17,1},{25,9},{2,18},{10... | collective-permute-start | bytes 1179656 | tf_op jit(solution)/shard_map/ppermute | solution.py:695
  108.3 15.8 %copy-start.12 = (f32[2048]{0:T(1024)S(1)}, f32[2048]{0:T(1024)}, u32[]{:S(2)}) copy-start(f32[2048]{0:T(1024)} %param.20) | copy-start | bytes 24580
  117.9 27.9 %copy-start.14 = (f32[1,1024]{1,0:T(1,128)S(1)}, f32[1,1024]{1,0:T(1,128)}, u32[]{:S(2)}) copy-start(f32[1,1024]{1,0:T(1,128)} %enc_bias_ref.1) | copy-start | bytes 12292
  119.1 26.6 %all-to-all-start = ((bf16[32,8,1536]{2,1,0:T(8,128)(2,1)}), bf16[32,8,1536]{2,1,0:T(8,128)(2,1)S(1)}, u32[]{:S(2)}, u32[]{:S(2)}) async-start(bf16[32,8,1536]{2,1,0:T(8,128)(2,1)} %bitcast.42), calls=%async_computation | async-start | bytes 1572864 | tf_op jit(solution)/shard_map/all_to_all | solution.py:688
  127.2 1.0 copy-start.13
  145.7 10.3 %copy-start.16 = (s32[1,192]{1,0:T(1,128)S(1)}, s32[1,192]{1,0:T(1,128)}, u32[]{:S(2)}) copy-start(s32[1,192]{1,0:T(1,128)} %param.22) | copy-start | bytes 2308
  145.7 10.4 %copy-start.3 = (bf16[256,1536]{1,0:T(8,128)(2,1)S(1)}, bf16[256,1536]{1,0:T(8,128)(2,1)}, u32[]{:S(2)}) copy-start(bf16[256,1536]{1,0:T(8,128)(2,1)} %get-tuple-element.32.refs_0_) | copy-start | bytes 2359300
  153.3 41.5 %all-to-all-start.2 = ((bf16[32,8,3072]{2,1,0:T(8,128)(2,1)}), bf16[32,8,3072]{2,1,0:T(8,128)(2,1)S(1)}, u32[]{:S(2)}, u32[]{:S(2)}) async-start(bf16[32,8,3072]{2,1,0:T(8,128)(2,1)} %bitcast.33), calls=%async_computation.2 | async-start | bytes 3145728 | tf_op jit(solution)/shard_map/all_to_all | solution.py:688
  156.2 1.4 copy-start.1
  157.6 1.2 copy-start.2
  158.8 1.1 copy-start.4

commit v4 on v3

--- a/solution.py
+++ b/solution.py
@@ -13,6 +13,7 @@
 CORES = 2
 KEY_BLOCK = 256
 KEY_STEP = 16
+MORE_KEYS = 128
 ROW_BLOCK = 64
 EMPTY = 1e30
 MASKED = -1e30
@@ -69,8 +70,6 @@
     scale = math.log2(math.e) / math.sqrt(hd)
     rows = heads * ROW_BLOCK
     blocks = tokens // ROW_BLOCK
-    lane_pos = lax.broadcasted_iota(jnp.int32, (ROW_BLOCK, KEY_BLOCK), 1)
-    row_in = lax.broadcasted_iota(jnp.int32, (ROW_BLOCK, KEY_BLOCK), 0)
 
     def queries(i):
         at = slice(i * ROW_BLOCK, (i + 1) * ROW_BLOCK)
@@ -82,45 +81,46 @@
         earlier = dcol_ref[...] < drow_ref[pl.ds(here, ROW_BLOCK), :]
         return jnp.sum(earlier.astype(f32), axis=1, keepdims=True).astype(jnp.int32)
 
-    def scores(i, q, col, begin):
+    def scores(i, q, col, begin, size):
         col = pl.multiple_of(col, KEY_STEP)
-        s = dot(q, k_scr[pl.ds(col, KEY_BLOCK), :], ((1,), (1,))) * scale
-        key_pos = lane_pos + col
-        visible = (row_in + (base + i * ROW_BLOCK) >= key_pos) & (key_pos >= begin)
-        s = jnp.where(visible[None], s.reshape(heads, ROW_BLOCK, KEY_BLOCK), MASKED)
-        return s.reshape(rows, KEY_BLOCK)
-
-    def values(col):
-        return v_scr[pl.ds(pl.multiple_of(col, KEY_STEP), KEY_BLOCK), :]
+        s = dot(q, k_scr[pl.ds(col, size), :], ((1,), (1,))) * scale
+        key_pos = lax.broadcasted_iota(jnp.int32, (ROW_BLOCK, size), 1) + col
+        row_pos = lax.broadcasted_iota(jnp.int32, (ROW_BLOCK, size), 0) + (base + i * ROW_BLOCK)
+        visible = (row_pos >= key_pos) & (key_pos >= begin)
+        s = jnp.where(visible[None], s.reshape(heads, ROW_BLOCK, size), MASKED)
+        return s.reshape(rows, size)
+
+    def values(col, size):
+        return v_scr[pl.ds(pl.multiple_of(col, KEY_STEP), size), :]
 
     starts = [first[scal[0] * blocks + i] * KEY_STEP for i in range(blocks)]
     for i in range(blocks):
-        s = scores(i, queries(i), starts[i], doc_starts(i))
+        s = scores(i, queries(i), starts[i], doc_starts(i), KEY_BLOCK)
         top = jnp.max(s, axis=1, keepdims=True)
         p = jnp.exp2(s - top)
         m_scr[i] = top
         l_scr[i] = jnp.sum(p, axis=1, keepdims=True)
-        a_scr[i] = dot(p.astype(bf16), values(starts[i]))
-
-    trips = 1
+        a_scr[i] = dot(p.astype(bf16), values(starts[i], KEY_BLOCK))
+
+    trips = 0
     for i in range(blocks):
-        need = (base + (i + 1) * ROW_BLOCK - starts[i] + KEY_BLOCK - 1) // KEY_BLOCK
-        trips = jnp.maximum(trips, need)
+        left = base + (i + 1) * ROW_BLOCK - starts[i] - KEY_BLOCK
+        trips = jnp.maximum(trips, (left + MORE_KEYS - 1) // MORE_KEYS)
 
     def more(j, carry):
         for i in range(blocks):
-            col = jnp.minimum(starts[i] + j * KEY_BLOCK, span)
-            s = scores(i, queries(i), col, doc_starts(i))
+            col = jnp.minimum(starts[i] + KEY_BLOCK + j * MORE_KEYS, span)
+            s = scores(i, queries(i), col, doc_starts(i), MORE_KEYS)
             old = m_scr[i]
             top = jnp.maximum(old, jnp.max(s, axis=1, keepdims=True))
             p = jnp.exp2(s - top)
             fade = jnp.exp2(old - top)
             m_scr[i] = top
             l_scr[i] = l_scr[i] * fade + jnp.sum(p, axis=1, keepdims=True)
-            a_scr[i] = a_scr[i] * fade + dot(p.astype(bf16), values(col))
+            a_scr[i] = a_scr[i] * fade + dot(p.astype(bf16), values(col, MORE_KEYS))
         return carry
 
-    lax.fori_loop(1, trips, more, 0)
+    lax.fori_loop(0, trips, more, 0)
 
     for i in range(blocks):
         out = (a_scr[i] * (1.0 / l_scr[i])).astype(bf16)
@@ -170,34 +170,43 @@
 def project_far_kernel(blocks, pieces, parts, order, *refs):
     w_refs, refs = refs[: 2 * blocks], refs[2 * blocks :]
     att, refs = refs[: parts * pieces], refs[parts * pieces :]
-    w_out, sends = refs[0], refs[1:]
-    for which in range(2):
-        for i in range(blocks):
-            ref = w_refs[which * blocks + i]
-            n = ref.shape[0]
-            at = pl.multiple_of(order[which * blocks + i], n)
-            w_out[pl.ds(at, n), :] = ref[...]
+    w_out, *sends, sem = refs
+    depth = w_refs[0].shape[0]
+    copies = []
+    for i, ref in enumerate(w_refs):
+        at = pl.multiple_of(order[i], depth)
+        copies.append(pltpu.make_async_copy(ref, w_out.at[pl.ds(at, depth), :], sem.at[i]))
+        copies[-1].start()
+    x = [
+        jnp.concatenate([r[...] for r in att[d * pieces : (d + 1) * pieces]], axis=1)
+        for d in range(parts)
+    ]
+    for copy in copies:
+        copy.wait()
     for d, send in enumerate(sends):
-        x = jnp.concatenate([r[...] for r in att[d * pieces : (d + 1) * pieces]], axis=1)
-        send[...] = dot(x, w_out[...]).astype(bf16)
-
-
-def project_far(order, mine, theirs, attended):
+        send[...] = dot(x[d], w_out[...]).astype(bf16)
+
+
+def project_far(order, mine, theirs, attended, hbm):
     tokens = attended[0][0].shape[0]
     pieces = len(attended[0])
     width = sum(a.shape[1] for a in attended[0])
     cols = mine[0].shape[1]
     parts = len(attended)
     flat = [a for group in attended for a in group]
+    blocks = [*mine, *theirs]
+    if hbm:
+        blocks = [in_hbm(b) for b in blocks]
     return call(
         functools.partial(project_far_kernel, len(mine), pieces, parts),
         [jax.ShapeDtypeStruct((width, cols), bf16)]
         + [jax.ShapeDtypeStruct((tokens, cols), bf16)] * parts,
         2 * parts * tokens * width * cols,
         2 * parts * tokens * width + 4 * width * cols,
-        [SMEM] + [VMEM] * (2 * len(mine) + len(flat)),
+        [SMEM] + [HBM if hbm else VMEM] * len(blocks) + [VMEM] * len(flat),
         [VMEM] * (1 + parts),
-    )(order, *mine, *theirs, *flat)
+        [pltpu.SemaphoreType.DMA((len(blocks),))],
+    )(order, *blocks, *flat)
 
 
 def project_own_kernel(*refs):
@@ -219,20 +228,21 @@
 
 
 class Slots:
+    tail = 4
+    cuts = 2
+
     def __init__(self, capacity, devices):
         self.full = capacity // 8
         rest = capacity % 8
-        self.tail = 0
-        if rest:
-            self.tail = 1
-            while self.tail < rest:
-                self.tail *= 2
-        self.cuts = 8 // self.tail if self.tail else 0
+        if rest > self.tail:
+            self.full, rest = self.full + 1, 0
+        self.has_tail = rest > 0
         self.rows = 8 * devices
-        self.groups = self.full + (1 if self.tail else 0)
+        self.groups = self.full + self.has_tail
+        self.lines = self.rows * self.full + (self.rows // 2 if self.has_tail else 0)
 
     def width(self, cols):
-        return self.full * cols + (cols // self.cuts if self.tail else 0)
+        return self.full * cols + (cols // self.cuts if self.has_tail else 0)
 
 
 def slot_keys(slots, expert, slot):
@@ -241,7 +251,7 @@
     for g in range(slots.full):
         ok = kept & (slot >= 8 * g) & (slot < 8 * g + 8)
         keys.append(jnp.where(ok, expert * 8 + slot - 8 * g, -1))
-    if slots.tail:
+    if slots.has_tail:
         rest = slot - 8 * slots.full
         for i in range(slots.cuts):
             keys.append(jnp.where(kept & (rest >= 0), expert * 8 + i * slots.tail + rest, -1))
@@ -281,7 +291,7 @@
         rows, live = place(one_hot(keys_ref, g, slots.rows), x)
         out_ref[:, g * cols : (g + 1) * cols] = jnp.where(live > 0, rows, EMPTY).astype(bf16)
         sent.append(send(g, cols, out_ref, packed_ref, out_sem))
-    if slots.tail:
+    if slots.has_tail:
         cut = cols // slots.cuts
         acc = live_all = None
         for i in range(slots.cuts):
@@ -326,36 +336,48 @@
     )(*args)
 
 
+def low_rows(shape):
+    return lax.broadcasted_iota(jnp.int32, shape, 0) % 8 < 4
+
+
+def by_pairs(x):
+    rows, n = x.shape
+    x = x.reshape(rows // 16, 2, 8, n)
+    return x[:, 0].reshape(rows // 2, n), x[:, 1].reshape(rows // 2, n)
+
+
+def turned(x):
+    return pltpu.roll(x, 4, 0), pltpu.roll(x, x.shape[0] - 4, 0)
+
+
 def spread(slots, block):
     cols = block.shape[1]
-    full, cuts = slots.full, slots.cuts
-    n = cols * cuts // (full * cuts + 1) if slots.tail else cols // full
+    full = slots.full
+    n = cols * 2 // (full * 2 + 1) if slots.has_tail else cols // full
     out = [block[:, g * n : (g + 1) * n].astype(f32) for g in range(full)]
-    if slots.tail:
-        rest = block[:, full * n :].astype(f32)
-        rows = rest.shape[0]
+    if slots.has_tail:
+        even, odd = by_pairs(block[:, full * n :].astype(f32))
+        low = low_rows((even.shape[0], 1))
         out.append(
             jnp.concatenate(
-                [rest]
-                + [pltpu.roll(rest, rows - i * slots.tail, 0) for i in range(1, cuts)],
-                axis=1,
+                [jnp.where(low, even, turned(odd)[0]), jnp.where(low, turned(even)[1], odd)], axis=1
             )
         )
     return out
 
 
-def tail_rows(shape):
-    return lax.broadcasted_iota(jnp.int32, shape, 0) % 8
-
-
-def live_rows(slots, groups):
-    out = []
-    for g, rows in enumerate(groups):
-        live = rows[:, :1] < EMPTY / 2
-        if slots.tail and g == slots.full:
-            live = live & (tail_rows(live.shape) < slots.tail)
-        out.append(live)
-    return out
+def gather_tail(halves):
+    first, second = halves
+    low = low_rows((first.shape[0], 1))
+    even = jnp.where(low, first, turned(second)[0])
+    odd = jnp.where(low, turned(first)[1], second)
+    rows, n = first.shape
+    pairs = [x.reshape(rows // 8, 1, 8, n) for x in (even, odd)]
+    return jnp.concatenate(pairs, axis=1).reshape(2 * rows, n)
+
+
+def live_rows(groups):
+    return [rows[:, :1] < EMPTY / 2 for rows in groups]
 
 
 def row_tiles(ref, scr, sems, start):
@@ -373,7 +395,7 @@
 
 def centered_rows(slots, block_ref, bias):
     groups = spread(slots, block_ref[...])
-    live = live_rows(slots, groups)
+    live = live_rows(groups)
     rows = [jnp.where(a, r - bias, 0.0).astype(bf16) for a, r in zip(live, groups)]
     return jnp.concatenate(rows, axis=0), live
 
@@ -392,7 +414,7 @@
 
 def encode(slots, block, dec_bias, enc, cols):
     hidden = enc.shape[2]
-    n = slots.rows * slots.groups
+    n = slots.lines
     return call(
         functools.partial(encode_kernel, slots),
         [jax.ShapeDtypeStruct((n, hidden), bf16), pltpu.HBM(block.shape, bf16)],
@@ -418,7 +440,7 @@
     e_copies = row_tiles(enc_ref.at[0], e_scr, e_sems, model - cols)
     prev = pltpu.make_async_copy(prev_ref, p_scr, p_sem)
     prev.start()
-    cuts = slots.cuts or 2
+    cuts = slots.cuts
     cut = model // cuts
     d_copies = []
     for t in range(cuts):
@@ -426,24 +448,34 @@
         d_copies.append(
             pltpu.make_async_copy(dec_ref.at[0, :, at], d_scr.at[:, at], d_sems.at[t])
         )
-        d_copies[-1].start()
     kept = pltpu.make_async_copy(block_ref, kept_ref, kept_sem)
     x, live = centered_rows(slots, block_ref, bias_ref[:, model - cols :])
-    n = slots.rows
     for copy in e_copies:
         copy.wait()
+    for copy in d_copies:
+        copy.start()
     kept.start()
     prev.wait()
     total = dot(x, e_scr[...]) + p_scr[...].astype(f32) + enc_bias_ref[...]
-    for g, a in enumerate(live):
-        rows = slice(g * n, (g + 1) * n)
-        pre = jnp.maximum(total[rows], 0.0)
-        latent_scr[rows] = jnp.where(a, pre, 0.0).astype(bf16)
+    at = 0
+    for a in live:
+        rows = slice(at, at + a.shape[0])
+        latent_scr[rows] = jnp.where(a, jnp.maximum(total[rows], 0.0), 0.0).astype(bf16)
+        at = rows.stop
     latent = pltpu.make_async_copy(latent_scr, latent_out, latent_sem)
     latent.start()
     sent = []
-    rest = None
-    which = tail_rows((n, 1)) // slots.tail if slots.tail else None
+    n = slots.rows
+
+    def go(here):
+        sent.append(
+            pltpu.make_async_copy(
+                pack_scr.at[:, here], packed_ref.at[:, here], sems.at[len(sent)]
+            )
+        )
+        sent[-1].start()
+
+    halves = []
     for t in range(cuts):
         at = slice(t * cut, (t + 1) * cut)
         d_copies[t].wait()
@@ -451,22 +483,12 @@
         for g in range(slots.full):
             here = slice(g * model + at.start, g * model + at.stop)
             pack_scr[:, here] = out[g * n : (g + 1) * n].astype(bf16)
-            sent.append(
-                pltpu.make_async_copy(
-                    pack_scr.at[:, here], packed_ref.at[:, here], sems.at[len(sent)]
-                )
-            )
-            sent[-1].start()
-        if slots.tail:
-            part = out[slots.full * n :]
-            rest = part if t == 0 else jnp.where(which == t, pltpu.roll(part, t * slots.tail, 0), rest)
-    if slots.tail:
+            go(here)
+        halves.append(out[slots.full * n :])
+    if slots.has_tail:
         here = slice(slots.full * model, slots.full * model + cut)
-        pack_scr[:, here] = rest.astype(bf16)
-        sent.append(
-            pltpu.make_async_copy(pack_scr.at[:, here], packed_ref.at[:, here], sems.at[len(sent)])
-        )
-        sent[-1].start()
+        pack_scr[:, here] = gather_tail(halves).astype(bf16)
+        go(here)
     kept.wait()
     latent.wait()
     for one in sent:
@@ -475,10 +497,10 @@
 
 def middle(slots, block, dec_bias, enc_bias, enc, prev, dec, cols):
     _, model, hidden = enc.shape
-    n = slots.rows * slots.groups
+    n = slots.lines
     out = (slots.rows, slots.width(model))
     one = pltpu.SemaphoreType.DMA
-    cuts = slots.cuts or 2
+    cuts = slots.cuts
     return call(
         functools.partial(middle_kernel, slots),
         [
@@ -515,7 +537,7 @@
         residue = jnp.concatenate(
             [
                 jnp.where(a, r[:, at] - rows, 0.0).astype(bf16)
-                for a, r, rows in zip(live_rows(slots, groups), built, groups)
+                for a, r, rows in zip(live_rows(groups), built, groups)
             ],
             axis=0,
         )
@@ -547,7 +569,7 @@
     came = pltpu.make_async_copy(rows_ref, rows_scr, rows_sem)
     came.start()
     model = rows_scr.shape[1]
-    cuts = slots.cuts or 2
+    cuts = slots.cuts
     cut = model // cuts
     hot = [
         one_hot(keys_ref, i, slots.rows).astype(f32).astype(bf16)
@@ -560,7 +582,7 @@
         total = 0.0
         for g in range(slots.full):
             total = total + turn(g, block_ref[:, g * model + at.start : g * model + at.stop])
-        if slots.tail:
+        if slots.has_tail:
             total = total + turn(slots.full + t, block_ref[:, slots.full * model :])
         recon = jnp.where(kept_ref[...] > 0, total, bias_ref[:, at]).astype(bf16)
         recon_scr[:, at] = recon
@@ -584,7 +606,7 @@
         6 * tokens * model + 2 * block.size,
         [VMEM] * 4 + [HBM],
         [HBM, HBM],
-        [scr, scr, scr, pltpu.SemaphoreType.DMA((slots.cuts or 2, 2)), pltpu.SemaphoreType.DMA],
+        [scr, scr, scr, pltpu.SemaphoreType.DMA((slots.cuts, 2)), pltpu.SemaphoreType.DMA],
     )(keys, kept, block, dec_bias, in_hbm(rows))
 
 
@@ -690,7 +712,7 @@
         ).reshape(block.shape)
 
     for j in range(CHUNKS):
-        w_all, *sends = project_far(order, *w_blocks[j], attended[1:])
+        w_all, *sends = project_far(order, *w_blocks[j], attended[1:], False)
         received = [
             lax.ppermute(part, "seq", over(chips - d)) for d, part in enumerate(sends, start=1)
         ]

time: 198 us -> 197 us (level)
  Pallas kernels: 39.2 us -> 35.9 us
  starting transfers between devices: 38.9 us -> 41 us
    pallas_call x4, Pallas kernels: 12.4 us -> 9.81 us  [attend(): call(functools.partial(attention_kernel, heads, parts, group), jax.ShapeD...]
    all_to_all x3, starting transfers between devices: 12.1 us -> 14.2 us  [to_all(): lax.all_to_all(block.reshape(devices, 8, block.shape[1]), ('seq', 'exp'),...]
  transfers between devices with their start and end apart: 38 -> 38, of which waited for: 13 -> 13; matrix products, arithmetic and copies ran while one was open for 3% -> 3% of each run, Pallas kernels for 15% -> 14%
where the time goes in v4:
time: 197 us
  waiting for transfers between devices  106 us (54%)
  starting transfers between devices  41 us (21%)
  Pallas kernels  35.9 us (18%)
  local copies, waits for them, and re-layouts  9.82 us (5%)
  other arithmetic  2.32 us (1%)
    all_to_all x3, waiting for transfers between devices, to_all(): lax.all_to_all(block.reshape(devices, 8, block.shape[1]), ('seq', 'exp'),...  49.2 us
    ppermute x7, waiting for transfers between devices, ring_gather(): fw = lax.ppermute(fw, 'exp', ahead)  26.6 us
    ppermute x7, starting transfers between devices, ring_gather(): fw = lax.ppermute(fw, 'exp', ahead)  17.4 us
    ppermute x7, waiting for transfers between devices, ring_gather(): bw = lax.ppermute(bw, 'exp', back)  16.8 us
    all_to_all x3, starting transfers between devices, to_all(): lax.all_to_all(block.reshape(devices, 8, block.shape[1]), ('seq', 'exp'),...  14.2 us
    pallas_call x4, Pallas kernels, attend(): call(functools.partial(attention_kernel, heads, parts, group), jax.ShapeD...  9.81 us
    ppermute x2, waiting for transfers between devices, shards(): lax.ppermute(part, 'seq', over(chips - d))  9.8 us
    pallas_call x1, Pallas kernels, middle(): call(functools.partial(middle_kernel, slots), [pltpu.HBM((n, hidden), bf1...  6.57 us
  transfers between devices with their start and end apart: 38, of which 13 were waited for; matrix products, arithmetic and copies ran while one was open for 3% of the time, Pallas kernels for 14%

profile of v4, /device:TPU:0, one launch (start us, length us, event | category | flops | bytes accessed | tf_op | source)
XLA Modules:
  0.0 196.6 jit_solution(1457563568861078172)
XLA Ops:
  0.6 1.1 fusion.1
  1.7 3.1 %collective-permute-start.19 = (bf16[128,1024]{1,0:T(8,128)(2,1)S(1)}, bf16[128,1024]{1,0:T(8,128)(2,1)S(1)}, u32[]{:S(2)}, u32[]{:S(2)}) collective-permute-start(bf16[128,1024]{1,0:T(8,128)(2,1)S(1)} %get-tuple-element.36.refs_0_), channel_id=1, source_target_pairs={{0,2},{2,4},{4,6},{6,7},{7,5},{5,3},{3,1},{1,0},{8,10},{10,12},{12... | collective-permute-start | bytes 786440 | tf_op jit(solution)/shard_map/ppermute | solution.py:161
  4.8 1.1 dynamic-slice_bitcast_fusion.3
  5.9 5.2 %collective-permute-done.19.refs_1_ = bf16[128,1024]{1,0:T(8,128)(2,1)S(1)} collective-permute-done((bf16[128,1024]{1,0:T(8,128)(2,1)S(1)}, bf16[128,1024]{1,0:T(8,128)(2,1)S(1)}, u32[]{:S(2)}, u32[]{:S(2)}) %collective-permute-start.19) | collective-permute-done | bytes 262176 | tf_op jit(solution)/shard_map/ppermute | solution.py:161
  11.1 1.8 collective-permute-start.21
  12.9 1.6 collective-permute-start
  14.4 2.1 %dynamic-slice_bitcast_fusion = bf16[192,2048]{1,0:T(8,128)(2,1)} fusion(bf16[1,192,4096]{2,1,0:T(8,128)(2,1)} %param.12, s32[]{:T(128)S(6)} %select_n.93), kind=kLoop, calls=%fused_computation | loop fusion | bytes 1572868 | tf_op jit(solution)/shard_map/dynamic_slice | solution.py:650
  16.5 0.5 collective-permute-start.17
  17.1 2.4 %collective-permute-done = bf16[192,512]{1,0:T(8,128)(2,1)S(1)} collective-permute-done((bf16[192,512]{1,0:T(8,128)(2,1)S(1)}, bf16[192,512]{1,0:T(8,128)(2,1)S(1)}, u32[]{:S(2)}, u32[]{:S(2)}) %collective-permute-start) | collective-permute-done | bytes 196640 | tf_op jit(solution)/shard_map/ppermute | solution.py:656
  19.5 0.4 collective-permute-start.22
  19.9 1.7 collective-permute-start.23
  21.6 1.2 add_multiply_fusion.1
  23.0 5.4 %collective-permute-done.22.refs_4_ = bf16[128,1024]{1,0:T(8,128)(2,1)} collective-permute-done((bf16[128,1024]{1,0:T(8,128)(2,1)S(1)}, bf16[128,1024]{1,0:T(8,128)(2,1)}, u32[]{:S(2)}, u32[]{:S(2)}) %collective-permute-start.22) | collective-permute-done | bytes 262176 | tf_op jit(solution)/shard_map/ppermute | solution.py:164
  28.3 0.7 copy-done.10
  29.0 0.4 collective-permute-start.24
  29.4 1.7 collective-permute-start.25
  31.1 0.1 slice.9
  31.2 0.2 copy.22.drow_ref
  31.4 0.1 concatenate.20.scal
  31.5 0.8 pad_add_fusion.1.order
  32.3 0.2 convert_reduce_fusion
  32.6 0.5 collective-permute-start.30
  33.1 5.0 %collective-permute-done.24.refs_6_ = bf16[128,1024]{1,0:T(8,128)(2,1)} collective-permute-done((bf16[128,1024]{1,0:T(8,128)(2,1)}, bf16[128,1024]{1,0:T(8,128)(2,1)}, u32[]{:S(2)}, u32[]{:S(2)}) %collective-permute-start.24) | collective-permute-done | bytes 262176 | tf_op jit(solution)/shard_map/ppermute | solution.py:164
  38.1 0.5 collective-permute-start.32
  38.7 3.0 %shard_map.149.refs_16_ = bf16[192,1024]{1,0:T(8,128)(2,1)S(1)} custom-call(s32[6]{0:T(128)S(1)} %concatenate.25.scal, s32[12]{0:T(128)S(1)} %and_select_fusion.2.first, bf16[192,2048]{1,0:T(8,128)(2,1)S(1)} %collective-permute-done.17.q_ref, bf16[384,512]{1,0:T(8,128)(2,1)S(1)} %pad_maximum_fusion.mine_ref, ...), custom_call_target="tpu_custom_call" | custom-call | flops 301989888 | bytes 1572864 | tf_op jit(solution)/shard_map/pallas_call | solution.py:141
  41.8 3.0 %shard_map.150.refs_17_ = bf16[192,1024]{1,0:T(8,128)(2,1)S(1)} custom-call(s32[6]{0:T(128)S(1)} %concatenate.25.scal, s32[12]{0:T(128)S(1)} %and_select_fusion.2.first, bf16[192,2048]{1,0:T(8,128)(2,1)S(1)} %collective-permute-done.17.q_ref, bf16[384,512]{1,0:T(8,128)(2,1)S(1)} %pad_maximum_fusion.mine_ref, ...), custom_call_target="tpu_custom_call" | custom-call | flops 301989888 | bytes 1572864 | tf_op jit(solution)/shard_map/pallas_call | solution.py:141
  44.8 1.6 collective-permute-start.2
  46.5 0.4 collective-permute-start.3
  47.0 3.0 %shard_map.153 = (bf16[2048,1024]{1,0:T(8,128)(2,1)S(1)}, bf16[192,1024]{1,0:T(8,128)(2,1)S(1)}) custom-call(s32[16]{0:T(128)S(1)} %pad_add_fusion.1.order, bf16[128,1024]{1,0:T(8,128)(2,1)S(1)} %get-tuple-element.36.refs_0_, bf16[128,1024]{1,0:T(8,128)(2,1)S(1)} %collective-permute-done.19.refs_1_, bf16[128,1024]{1,0:T(8,128)(2,1)S(1)} %copy-done.7, ...), custom_call_target="tpu_custom_call" | custom-call | flops 805306368 | bytes 9175040 | tf_op jit(solution)/shard_map/pallas_call | solution.py:200
  50.1 3.7 %collective-permute-done.3.refs_2_ = bf16[128,1024]{1,0:T(8,128)(2,1)} collective-permute-done((bf16[128,1024]{1,0:T(8,128)(2,1)S(1)}, bf16[128,1024]{1,0:T(8,128)(2,1)}, u32[]{:S(2)}, u32[]{:S(2)}) %collective-permute-start.3) | collective-permute-done | bytes 262176 | tf_op jit(solution)/shard_map/ppermute | solution.py:164
  53.7 1.7 collective-permute-start.5
  55.4 2.0 shard_map.147.refs_0_
  57.4 1.8 shard_map.148.refs_1_
  59.1 1.0 shard_map.154.own_ref
  60.2 1.3 collective-permute-done.34.refs_0_
  61.4 1.3 shard_map.155
  62.7 6.4 %all-to-all-start.1 = ((bf16[32,8,1536]{2,1,0:T(8,128)(2,1)}), bf16[32,8,1536]{2,1,0:T(8,128)(2,1)S(1)}, u32[]{:S(2)}, u32[]{:S(2)}) async-start(bf16[32,8,1536]{2,1,0:T(8,128)(2,1)} %bitcast.41), calls=%async_computation.1 | async-start | bytes 1572864 | tf_op jit(solution)/shard_map/all_to_all | solution.py:710
  69.2 1.8 collective-permute-start.4
  71.0 0.3 collective-permute-start.7
  71.3 0.5 collective-permute-start.10
  71.8 16.5 %collective-permute-done.4.refs_3_ = bf16[128,1024]{1,0:T(8,128)(2,1)S(1)} collective-permute-done((bf16[128,1024]{1,0:T(8,128)(2,1)}, bf16[128,1024]{1,0:T(8,128)(2,1)S(1)}, u32[]{:S(2)}, u32[]{:S(2)}) %collective-permute-start.4) | collective-permute-done | bytes 262176 | tf_op jit(solution)/shard_map/ppermute | solution.py:161
  88.3 5.7 %collective-permute-start.6 = (bf16[128,1024]{1,0:T(8,128)(2,1)S(1)}, bf16[128,1024]{1,0:T(8,128)(2,1)S(1)}, u32[]{:S(2)}, u32[]{:S(2)}) collective-permute-start(bf16[128,1024]{1,0:T(8,128)(2,1)S(1)} %collective-permute-done.4.refs_3_), channel_id=1, source_target_pairs={{0,2},{2,4},{4,6},{6,7},{7,5},{5,3},{3,1},{1,0},{8,10},{10,12},{12... | collective-permute-start | bytes 786440 | tf_op jit(solution)/shard_map/ppermute | solution.py:161
  94.0 0.5 collective-permute-start.13
  94.6 4.9 %collective-permute-done.6.refs_5_ = bf16[128,1024]{1,0:T(8,128)(2,1)S(1)} collective-permute-done((bf16[128,1024]{1,0:T(8,128)(2,1)S(1)}, bf16[128,1024]{1,0:T(8,128)(2,1)S(1)}, u32[]{:S(2)}, u32[]{:S(2)}) %collective-permute-start.6) | collective-permute-done | bytes 262176 | tf_op jit(solution)/shard_map/ppermute | solution.py:161
  99.5 2.8 %collective-permute-done.8.refs_7_ = bf16[128,1024]{1,0:T(8,128)(2,1)S(1)} collective-permute-done((bf16[128,1024]{1,0:T(8,128)(2,1)S(1)}, bf16[128,1024]{1,0:T(8,128)(2,1)S(1)}, u32[]{:S(2)}, u32[]{:S(2)}) %collective-permute-start.8) | collective-permute-done | bytes 262176 | tf_op jit(solution)/shard_map/ppermute | solution.py:164
  102.4 1.5 collective-permute-done.16.refs_15_
  103.9 2.6 %shard_map.151 = (bf16[2048,1024]{1,0:T(8,128)(2,1)S(1)}, bf16[192,1024]{1,0:T(8,128)(2,1)S(1)}) custom-call(s32[16]{0:T(128)S(1)} %pad_add_fusion.1.order, bf16[128,1024]{1,0:T(8,128)(2,1)S(1)} %get-tuple-element.37.refs_0_, bf16[128,1024]{1,0:T(8,128)(2,1)} %collective-permute-done.2.refs_1_, bf16[128,1024]{1,0:T(8,128)(2,1)} %collective-permute-done.3.refs_2_, ...), custom_call_target="tpu_custom_call" | custom-call | flops 805306368 | bytes 9175040 | tf_op jit(solution)/shard_map/pallas_call | solution.py:200
  106.5 1.7 collective-permute-start.18
  108.2 1.0 shard_map.152.own_ref
  109.2 8.5 %collective-permute-done.18.refs_0_ = bf16[192,1024]{1,0:T(8,128)(2,1)S(1)} collective-permute-done((bf16[192,1024]{1,0:T(8,128)(2,1)S(1)}, bf16[192,1024]{1,0:T(8,128)(2,1)S(1)}, u32[]{:S(2)}, u32[]{:S(2)}) %collective-permute-start.18) | collective-permute-done | bytes 393248 | tf_op jit(solution)/shard_map/ppermute | solution.py:717
  117.7 1.3 shard_map.156
  119.0 4.7 %all-to-all-start = ((bf16[32,8,1536]{2,1,0:T(8,128)(2,1)}), bf16[32,8,1536]{2,1,0:T(8,128)(2,1)S(1)}, u32[]{:S(2)}, u32[]{:S(2)}) async-start(bf16[32,8,1536]{2,1,0:T(8,128)(2,1)} %bitcast.42), calls=%async_computation | async-start | bytes 1572864 | tf_op jit(solution)/shard_map/all_to_all | solution.py:710
  123.8 2.8 %shard_map.157 = (bf16[384,1024]{1,0:T(8,128)(2,1)S(1)}, bf16[256,1536]{1,0:T(8,128)(2,1)}) custom-call(bf16[256,1536]{1,0:T(8,128)(2,1)S(1)} %bitcast.34, f32[1,2048]{1,0:T(1,128)S(1)} %bitcast.37, bf16[1,2048,1024]{2,1,0:T(8,128)(2,1)} %enc_ref.1), custom_call_target="tpu_custom_call" | custom-call | flops 805306368 | bytes 4456448 | tf_op jit(solution)/shard_map/pallas_call | solution.py:418
  126.6 0.9 copy-done.5
  127.5 18.1 %all-to-all-done = bf16[32,8,1536]{2,1,0:T(8,128)(2,1)S(1)} async-done(((bf16[32,8,1536]{2,1,0:T(8,128)(2,1)}), bf16[32,8,1536]{2,1,0:T(8,128)(2,1)S(1)}, u32[]{:S(2)}, u32[]{:S(2)}) %all-to-all-start) | async-done | bytes 786464 | tf_op jit(solution)/shard_map/all_to_all | solution.py:710
  145.6 6.6 %shard_map.158 = (bf16[384,1024]{1,0:T(8,128)(2,1)}, bf16[256,3072]{1,0:T(8,128)(2,1)}, bf16[256,1536]{1,0:T(8,128)(2,1)}) custom-call(bf16[256,1536]{1,0:T(8,128)(2,1)S(1)} %bitcast.35, f32[1,2048]{1,0:T(1,128)S(1)} %bitcast.38, f32[1,1024]{1,0:T(1,128)S(1)} %copy-done.14, bf16[1,2048,1024]{2,1,0:T(8,128)(2,1)} %enc_ref.1, bf16[384,1024]{1,0:T(8,128)(2,1)} %copy-done.5, ...), custom_call_target="tpu_custom_call" | custom-call | flops 2415919104 | bytes 11010048 | tf_op jit(solution)/shard_map/pallas_call | solution.py:504
  152.2 3.1 %all-to-all-start.2 = ((bf16[32,8,3072]{2,1,0:T(8,128)(2,1)}), bf16[32,8,3072]{2,1,0:T(8,128)(2,1)S(1)}, u32[]{:S(2)}, u32[]{:S(2)}) async-start(bf16[32,8,3072]{2,1,0:T(8,128)(2,1)} %bitcast.33), calls=%async_computation.2 | async-start | bytes 3145728 | tf_op jit(solution)/shard_map/all_to_all | solution.py:710
  155.3 0.1 copy.26.kept_ref
  155.4 1.1 copy-done.2
  156.6 1.1 copy-done.3
  157.7 1.1 copy-done.4
  158.8 3.9 %shard_map.160 = bf16[1,1024,2048]{2,1,0:T(8,128)(2,1)} custom-call(bf16[384,1024]{1,0:T(8,128)(2,1)S(1)} %copy-done.3, bf16[256,3072]{1,0:T(8,128)(2,1)S(1)} %copy-done.1, bf16[256,1536]{1,0:T(8,128)(2,1)S(1)} %copy-done.2, bf16[256,1536]{1,0:T(8,128)(2,1)S(1)} %copy-done.4), custom_call_target="tpu_custom_call" | custom-call | flops 1610612736 | bytes 6553600 | tf_op jit(solution)/shard_map/pallas_call | solution.py:554
  162.8 31.1 %all-to-all-done.2 = bf16[32,8,3072]{2,1,0:T(8,128)(2,1)S(1)} async-done(((bf16[32,8,3072]{2,1,0:T(8,128)(2,1)}), bf16[32,8,3072]{2,1,0:T(8,128)(2,1)S(1)}, u32[]{:S(2)}, u32[]{:S(2)}) %all-to-all-start.2) | async-done | bytes 1572896 | tf_op jit(solution)/shard_map/all_to_all | solution.py:710
  193.9 2.6 %shard_map.159 = (bf16[192,2048]{1,0:T(8,128)(2,1)}, bf16[192,2048]{1,0:T(8,128)(2,1)}) custom-call(s32[3,192]{1,0:T(4,128)S(1)} %pad_add_fusion.keys_ref, s32[192,1]{1,0:T(8,128)S(1)} %copy.26.kept_ref, bf16[256,3072]{1,0:T(8,128)(2,1)S(1)} %bitcast.32, f32[1,2048]{1,0:T(1,128)S(1)} %bitcast.39, bf16[192,2048]{1,0:T(8,128)(2,1)} %get-tuple-element.24.rows_ref), custom_call_target="tpu_custom_call" | custom-call | flops 402653184 | bytes 3932160 | tf_op jit(solution)/shard_map/pallas_call | solution.py:602
  (81 shorter events, 0.8 us)
Async XLA Ops:
  0.6 30.4 %copy-start.12 = (s32[1,768]{1,0:T(1,128)S(1)}, s32[1,768]{1,0:T(1,128)}, u32[]{:S(2)}) copy-start(s32[1,768]{1,0:T(1,128)} %dcol_ref.7) | copy-start | bytes 9220
  1.7 9.4 %collective-permute-start.19 = (bf16[128,1024]{1,0:T(8,128)(2,1)S(1)}, bf16[128,1024]{1,0:T(8,128)(2,1)S(1)}, u32[]{:S(2)}, u32[]{:S(2)}) collective-permute-start(bf16[128,1024]{1,0:T(8,128)(2,1)S(1)} %get-tuple-element.36.refs_0_), channel_id=1, source_target_pairs={{0,2},{2,4},{4,6},{6,7},{7,5},{5,3},{3,1},{1,0},{8,10},{10,12},{12... | collective-permute-start | bytes 786440 | tf_op jit(solution)/shard_map/ppermute | solution.py:161
  4.8 14.7 %collective-permute-start.20 = (bf16[128,1024]{1,0:T(8,128)(2,1)S(1)}, bf16[128,1024]{1,0:T(8,128)(2,1)S(1)}, u32[]{:S(2)}, u32[]{:S(2)}) collective-permute-start(bf16[128,1024]{1,0:T(8,128)(2,1)S(1)} %get-tuple-element.36.refs_0_), channel_id=1, source_target_pairs={{0,1},{2,0},{4,2},{6,4},{7,6},{5,7},{3,5},{1,3},{8,9},{10,8},{12,1... | collective-permute-start | bytes 786440 | tf_op jit(solution)/shard_map/ppermute | solution.py:164
  4.8 18.0 %collective-permute-start.26 = (bf16[128,1024]{1,0:T(8,128)(2,1)S(1)}, bf16[128,1024]{1,0:T(8,128)(2,1)S(1)}, u32[]{:S(2)}, u32[]{:S(2)}) collective-permute-start(bf16[128,1024]{1,0:T(8,128)(2,1)S(1)} %get-tuple-element.36.refs_0_), channel_id=1, source_target_pairs={{0,8},{8,0},{16,24},{24,16},{1,9},{9,1},{17,25},{25,17},{2,10},{10... | collective-permute-start | bytes 786440 | tf_op jit(solution)/shard_map/ppermute | solution.py:166
  11.1 8.8 %collective-permute-start.21 = (bf16[128,1024]{1,0:T(8,128)(2,1)S(1)}, bf16[128,1024]{1,0:T(8,128)(2,1)}, u32[]{:S(2)}, u32[]{:S(2)}) collective-permute-start(bf16[128,1024]{1,0:T(8,128)(2,1)S(1)} %collective-permute-done.19.refs_1_), channel_id=1, source_target_pairs={{0,2},{2,4},{4,6},{6,7},{7,5},{5,3},{3,1},{1,0},{8,10},{10,12},{12... | collective-permute-start | bytes 786440 | tf_op jit(solution)/shard_map/ppermute | solution.py:161
  12.9 6.6 %collective-permute-start = (bf16[192,512]{1,0:T(8,128)(2,1)S(1)}, bf16[192,512]{1,0:T(8,128)(2,1)S(1)}, u32[]{:S(2)}, u32[]{:S(2)}) collective-permute-start(bf16[192,512]{1,0:T(8,128)(2,1)S(1)} %pad_maximum_fusion.1), channel_id=1, source_target_pairs={{0,16},{8,24},{16,0},{24,8},{1,17},{9,25},{17,1},{25,9},{2,18},{10... | collective-permute-start | bytes 589832 | tf_op jit(solution)/shard_map/ppermute | solution.py:656
  16.5 21.5 %collective-permute-start.17 = (bf16[192,2048]{1,0:T(8,128)(2,1)}, bf16[192,2048]{1,0:T(8,128)(2,1)S(1)}, u32[]{:S(2)}, u32[]{:S(2)}) collective-permute-start(bf16[192,2048]{1,0:T(8,128)(2,1)} %dynamic-slice_bitcast_fusion), channel_id=1, source_target_pairs={{0,16},{8,24},{16,0},{24,8},{1,17},{9,25},{17,1},{25,9},{2,18},{10... | collective-permute-start | bytes 2359304 | tf_op jit(solution)/shard_map/ppermute | solution.py:657
  19.5 8.8 %collective-permute-start.27 = (bf16[128,1024]{1,0:T(8,128)(2,1)S(1)}, bf16[128,1024]{1,0:T(8,128)(2,1)S(1)}, u32[]{:S(2)}, u32[]{:S(2)}) collective-permute-start(bf16[128,1024]{1,0:T(8,128)(2,1)S(1)} %collective-permute-done.19.refs_1_), channel_id=1, source_target_pairs={{0,8},{8,0},{16,24},{24,16},{1,9},{9,1},{17,25},{25,17},{2,10},{10... | collective-permute-start | bytes 786440 | tf_op jit(solution)/shard_map/ppermute | solution.py:166
  19.5 19.2 %copy-start.6 = (bf16[128,1024]{1,0:T(8,128)(2,1)}, bf16[128,1024]{1,0:T(8,128)(2,1)S(1)}, u32[]{:S(2)}) copy-start(bf16[128,1024]{1,0:T(8,128)(2,1)S(1)} %collective-permute-done.20.refs_2_) | copy-start | bytes 786436
  19.5 8.8 %collective-permute-start.22 = (bf16[128,1024]{1,0:T(8,128)(2,1)S(1)}, bf16[128,1024]{1,0:T(8,128)(2,1)}, u32[]{:S(2)}, u32[]{:S(2)}) collective-permute-start(bf16[128,1024]{1,0:T(8,128)(2,1)S(1)} %collective-permute-done.20.refs_2_), channel_id=1, source_target_pairs={{0,1},{2,0},{4,2},{6,4},{7,6},{5,7},{3,5},{1,3},{8,9},{10,8},{12,1... | collective-permute-start | bytes 786440 | tf_op jit(solution)/shard_map/ppermute | solution.py:164
  19.9 9.5 %collective-permute-start.23 = (bf16[128,1024]{1,0:T(8,128)(2,1)}, bf16[128,1024]{1,0:T(8,128)(2,1)}, u32[]{:S(2)}, u32[]{:S(2)}) collective-permute-start(bf16[128,1024]{1,0:T(8,128)(2,1)} %collective-permute-done.21.refs_3_), channel_id=1, source_target_pairs={{0,2},{2,4},{4,6},{6,7},{7,5},{5,3},{3,1},{1,0},{8,10},{10,12},{12... | collective-permute-start | bytes 786440 | tf_op jit(solution)/shard_map/ppermute | solution.py:161
  22.9 15.8 %copy-start.8 = (bf16[128,1024]{1,0:T(8,128)(2,1)}, bf16[128,1024]{1,0:T(8,128)(2,1)S(1)}, u32[]{:S(2)}) copy-start(bf16[128,1024]{1,0:T(8,128)(2,1)S(1)} %collective-permute-done.26.refs_8_) | copy-start | bytes 786436
  22.9 9.7 %collective-permute-start.1 = (bf16[384,512]{1,0:T(8,128)(2,1)S(1)}, bf16[384,512]{1,0:T(8,128)(2,1)S(1)}, u32[]{:S(2)}, u32[]{:S(2)}) collective-permute-start(bf16[384,512]{1,0:T(8,128)(2,1)S(1)} %pad_maximum_fusion.mine_ref), channel_id=1, source_target_pairs={{0,8},{8,0},{16,24},{24,16},{1,9},{9,1},{17,25},{25,17},{2,10},{10... | collective-permute-start | bytes 1179656 | tf_op jit(solution)/shard_map/ppermute | solution.py:659
  28.3 4.2 %collective-permute-start.28 = (bf16[128,1024]{1,0:T(8,128)(2,1)S(1)}, bf16[128,1024]{1,0:T(8,128)(2,1)}, u32[]{:S(2)}, u32[]{:S(2)}) collective-permute-start(bf16[128,1024]{1,0:T(8,128)(2,1)S(1)} %collective-permute-done.20.refs_2_), channel_id=1, source_target_pairs={{0,8},{8,0},{16,24},{24,16},{1,9},{9,1},{17,25},{25,17},{2,10},{10... | collective-permute-start | bytes 786440 | tf_op jit(solution)/shard_map/ppermute | solution.py:166
  28.3 0.7 copy-start.10
  29.0 9.0 %collective-permute-start.24 = (bf16[128,1024]{1,0:T(8,128)(2,1)}, bf16[128,1024]{1,0:T(8,128)(2,1)}, u32[]{:S(2)}, u32[]{:S(2)}) collective-permute-start(bf16[128,1024]{1,0:T(8,128)(2,1)} %collective-permute-done.22.refs_4_), channel_id=1, source_target_pairs={{0,1},{2,0},{4,2},{6,4},{7,6},{5,7},{3,5},{1,3},{8,9},{10,8},{12,1... | collective-permute-start | bytes 786440 | tf_op jit(solution)/shard_map/ppermute | solution.py:164
  29.4 9.2 %collective-permute-start.25 = (bf16[128,1024]{1,0:T(8,128)(2,1)}, bf16[128,1024]{1,0:T(8,128)(2,1)}, u32[]{:S(2)}, u32[]{:S(2)}) collective-permute-start(bf16[128,1024]{1,0:T(8,128)(2,1)} %collective-permute-done.23.refs_5_), channel_id=1, source_target_pairs={{0,2},{2,4},{4,6},{6,7},{7,5},{5,3},{3,1},{1,0},{8,10},{10,12},{12... | collective-permute-start | bytes 786440 | tf_op jit(solution)/shard_map/ppermute | solution.py:161
  31.5 15.4 %copy-start.11 = (bf16[128,1024]{1,0:T(8,128)(2,1)S(1)}, bf16[128,1024]{1,0:T(8,128)(2,1)}, u32[]{:S(2)}) copy-start(bf16[128,1024]{1,0:T(8,128)(2,1)} %copy-done.10) | copy-start | bytes 786436
  32.5 12.3 %collective-permute-start.29 = (bf16[128,1024]{1,0:T(8,128)(2,1)}, bf16[128,1024]{1,0:T(8,128)(2,1)S(1)}, u32[]{:S(2)}, u32[]{:S(2)}) collective-permute-start(bf16[128,1024]{1,0:T(8,128)(2,1)} %collective-permute-done.21.refs_3_), channel_id=1, source_target_pairs={{0,8},{8,0},{16,24},{24,16},{1,9},{9,1},{17,25},{25,17},{2,10},{10... | collective-permute-start | bytes 786440 | tf_op jit(solution)/shard_map/ppermute | solution.py:166
  32.6 13.8 %collective-permute-start.30 = (bf16[128,1024]{1,0:T(8,128)(2,1)}, bf16[128,1024]{1,0:T(8,128)(2,1)S(1)}, u32[]{:S(2)}, u32[]{:S(2)}) collective-permute-start(bf16[128,1024]{1,0:T(8,128)(2,1)} %collective-permute-done.22.refs_4_), channel_id=1, source_target_pairs={{0,8},{8,0},{16,24},{24,16},{1,9},{9,1},{17,25},{25,17},{2,10},{10... | collective-permute-start | bytes 786440 | tf_op jit(solution)/shard_map/ppermute | solution.py:166
  38.1 8.9 %collective-permute-start.31 = (bf16[128,1024]{1,0:T(8,128)(2,1)}, bf16[128,1024]{1,0:T(8,128)(2,1)S(1)}, u32[]{:S(2)}, u32[]{:S(2)}) collective-permute-start(bf16[128,1024]{1,0:T(8,128)(2,1)} %collective-permute-done.23.refs_5_), channel_id=1, source_target_pairs={{0,8},{8,0},{16,24},{24,16},{1,9},{9,1},{17,25},{25,17},{2,10},{10... | collective-permute-start | bytes 786440 | tf_op jit(solution)/shard_map/ppermute | solution.py:166
  38.1 8.9 %collective-permute-start.32 = (bf16[128,1024]{1,0:T(8,128)(2,1)}, bf16[128,1024]{1,0:T(8,128)(2,1)S(1)}, u32[]{:S(2)}, u32[]{:S(2)}) collective-permute-start(bf16[128,1024]{1,0:T(8,128)(2,1)} %collective-permute-done.24.refs_6_), channel_id=1, source_target_pairs={{0,8},{8,0},{16,24},{24,16},{1,9},{9,1},{17,25},{25,17},{2,10},{10... | collective-permute-start | bytes 786440 | tf_op jit(solution)/shard_map/ppermute | solution.py:166
  38.6 8.3 %collective-permute-start.33 = (bf16[128,1024]{1,0:T(8,128)(2,1)}, bf16[128,1024]{1,0:T(8,128)(2,1)S(1)}, u32[]{:S(2)}, u32[]{:S(2)}) collective-permute-start(bf16[128,1024]{1,0:T(8,128)(2,1)} %collective-permute-done.25.refs_7_), channel_id=1, source_target_pairs={{0,8},{8,0},{16,24},{24,16},{1,9},{9,1},{17,25},{25,17},{2,10},{10... | collective-permute-start | bytes 786440 | tf_op jit(solution)/shard_map/ppermute | solution.py:166
  38.7 8.3 %copy-start.7 = (bf16[128,1024]{1,0:T(8,128)(2,1)S(1)}, bf16[128,1024]{1,0:T(8,128)(2,1)}, u32[]{:S(2)}) copy-start(bf16[128,1024]{1,0:T(8,128)(2,1)} %copy-done.6) | copy-start | bytes 786436
  38.7 8.3 %copy-start.9 = (bf16[128,1024]{1,0:T(8,128)(2,1)S(1)}, bf16[128,1024]{1,0:T(8,128)(2,1)}, u32[]{:S(2)}) copy-start(bf16[128,1024]{1,0:T(8,128)(2,1)} %copy-done.8) | copy-start | bytes 786436
  41.7 8.3 %copy-start.15 = (s32[1,192]{1,0:T(1,128)S(1)}, s32[1,192]{1,0:T(1,128)}, u32[]{:S(2)}) copy-start(s32[1,192]{1,0:T(1,128)} %param.22) | copy-start | bytes 2308
  41.8 8.3 %copy-start.17 = (s32[1,192]{1,0:T(1,128)S(1)}, s32[1,192]{1,0:T(1,128)}, u32[]{:S(2)}) copy-start(s32[1,192]{1,0:T(1,128)} %param.21) | copy-start | bytes 2308
  41.8 13.6 %copy-start = (bf16[1,192,4096]{2,1,0:T(8,128)(2,1)S(1)}, bf16[1,192,4096]{2,1,0:T(8,128)(2,1)}, u32[]{:S(2)}) copy-start(bf16[1,192,4096]{2,1,0:T(8,128)(2,1)} %param.12) | copy-start | bytes 4718596
  44.8 24.3 %collective-permute-start.2 = (bf16[128,1024]{1,0:T(8,128)(2,1)S(1)}, bf16[128,1024]{1,0:T(8,128)(2,1)}, u32[]{:S(2)}, u32[]{:S(2)}) collective-permute-start(bf16[128,1024]{1,0:T(8,128)(2,1)S(1)} %get-tuple-element.37.refs_0_), channel_id=1, source_target_pairs={{0,2},{2,4},{4,6},{6,7},{7,5},{5,3},{3,1},{1,0},{8,10},{10,12},{12... | collective-permute-start | bytes 786440 | tf_op jit(solution)/shard_map/ppermute | solution.py:161
  46.5 7.3 %collective-permute-start.3 = (bf16[128,1024]{1,0:T(8,128)(2,1)S(1)}, bf16[128,1024]{1,0:T(8,128)(2,1)}, u32[]{:S(2)}, u32[]{:S(2)}) collective-permute-start(bf16[128,1024]{1,0:T(8,128)(2,1)S(1)} %get-tuple-element.37.refs_0_), channel_id=1, source_target_pairs={{0,1},{2,0},{4,2},{6,4},{7,6},{5,7},{3,5},{1,3},{8,9},{10,8},{12,1... | collective-permute-start | bytes 786440 | tf_op jit(solution)/shard_map/ppermute | solution.py:164
  49.9 11.5 %collective-permute-start.34 = (bf16[192,1024]{1,0:T(8,128)(2,1)S(1)}, bf16[192,1024]{1,0:T(8,128)(2,1)S(1)}, u32[]{:S(2)}, u32[]{:S(2)}) collective-permute-start(bf16[192,1024]{1,0:T(8,128)(2,1)S(1)} %get-tuple-element.22), channel_id=1, source_target_pairs={{0,16},{8,24},{16,0},{24,8},{1,17},{9,25},{17,1},{25,9},{2,18},{10... | collective-permute-start | bytes 1179656 | tf_op jit(solution)/shard_map/ppermute | solution.py:717
  53.7 17.3 %collective-permute-start.5 = (bf16[128,1024]{1,0:T(8,128)(2,1)}, bf16[128,1024]{1,0:T(8,128)(2,1)S(1)}, u32[]{:S(2)}, u32[]{:S(2)}) collective-permute-start(bf16[128,1024]{1,0:T(8,128)(2,1)} %collective-permute-done.3.refs_2_), channel_id=1, source_target_pairs={{0,1},{2,0},{4,2},{6,4},{7,6},{5,7},{3,5},{1,3},{8,9},{10,8},{12,1... | collective-permute-start | bytes 786440 | tf_op jit(solution)/shard_map/ppermute | solution.py:164
  62.7 56.3 %all-to-all-start.1 = ((bf16[32,8,1536]{2,1,0:T(8,128)(2,1)}), bf16[32,8,1536]{2,1,0:T(8,128)(2,1)S(1)}, u32[]{:S(2)}, u32[]{:S(2)}) async-start(bf16[32,8,1536]{2,1,0:T(8,128)(2,1)} %bitcast.41), calls=%async_computation.1 | async-start | bytes 1572864 | tf_op jit(solution)/shard_map/all_to_all | solution.py:710
  69.2 19.1 %collective-permute-start.4 = (bf16[128,1024]{1,0:T(8,128)(2,1)}, bf16[128,1024]{1,0:T(8,128)(2,1)S(1)}, u32[]{:S(2)}, u32[]{:S(2)}) collective-permute-start(bf16[128,1024]{1,0:T(8,128)(2,1)} %collective-permute-done.2.refs_1_), channel_id=1, source_target_pairs={{0,2},{2,4},{4,6},{6,7},{7,5},{5,3},{3,1},{1,0},{8,10},{10,12},{12... | collective-permute-start | bytes 786440 | tf_op jit(solution)/shard_map/ppermute | solution.py:161
  71.0 22.9 %collective-permute-start.7 = (bf16[128,1024]{1,0:T(8,128)(2,1)S(1)}, bf16[128,1024]{1,0:T(8,128)(2,1)S(1)}, u32[]{:S(2)}, u32[]{:S(2)}) collective-permute-start(bf16[128,1024]{1,0:T(8,128)(2,1)S(1)} %collective-permute-done.5.refs_4_), channel_id=1, source_target_pairs={{0,1},{2,0},{4,2},{6,4},{7,6},{5,7},{3,5},{1,3},{8,9},{10,8},{12,1... | collective-permute-start | bytes 786440 | tf_op jit(solution)/shard_map/ppermute | solution.py:164
  71.3 22.7 %collective-permute-start.9 = (bf16[128,1024]{1,0:T(8,128)(2,1)S(1)}, bf16[128,1024]{1,0:T(8,128)(2,1)S(1)}, u32[]{:S(2)}, u32[]{:S(2)}) collective-permute-start(bf16[128,1024]{1,0:T(8,128)(2,1)S(1)} %get-tuple-element.37.refs_0_), channel_id=1, source_target_pairs={{0,8},{8,0},{16,24},{24,16},{1,9},{9,1},{17,25},{25,17},{2,10},{10... | collective-permute-start | bytes 786440 | tf_op jit(solution)/shard_map/ppermute | solution.py:166
  71.3 22.8 %collective-permute-start.10 = (bf16[128,1024]{1,0:T(8,128)(2,1)}, bf16[128,1024]{1,0:T(8,128)(2,1)S(1)}, u32[]{:S(2)}, u32[]{:S(2)}) collective-permute-start(bf16[128,1024]{1,0:T(8,128)(2,1)} %collective-permute-done.2.refs_1_), channel_id=1, source_target_pairs={{0,8},{8,0},{16,24},{24,16},{1,9},{9,1},{17,25},{25,17},{2,10},{10... | collective-permute-start | bytes 786440 | tf_op jit(solution)/shard_map/ppermute | solution.py:166
  71.8 22.8 %collective-permute-start.11 = (bf16[128,1024]{1,0:T(8,128)(2,1)}, bf16[128,1024]{1,0:T(8,128)(2,1)S(1)}, u32[]{:S(2)}, u32[]{:S(2)}) collective-permute-start(bf16[128,1024]{1,0:T(8,128)(2,1)} %collective-permute-done.3.refs_2_), channel_id=1, source_target_pairs={{0,8},{8,0},{16,24},{24,16},{1,9},{9,1},{17,25},{25,17},{2,10},{10... | collective-permute-start | bytes 786440 | tf_op jit(solution)/shard_map/ppermute | solution.py:166
  88.3 11.3 %collective-permute-start.6 = (bf16[128,1024]{1,0:T(8,128)(2,1)S(1)}, bf16[128,1024]{1,0:T(8,128)(2,1)S(1)}, u32[]{:S(2)}, u32[]{:S(2)}) collective-permute-start(bf16[128,1024]{1,0:T(8,128)(2,1)S(1)} %collective-permute-done.4.refs_3_), channel_id=1, source_target_pairs={{0,2},{2,4},{4,6},{6,7},{7,5},{5,3},{3,1},{1,0},{8,10},{10,12},{12... | collective-permute-start | bytes 786440 | tf_op jit(solution)/shard_map/ppermute | solution.py:161
  94.0 8.4 %collective-permute-start.8 = (bf16[128,1024]{1,0:T(8,128)(2,1)S(1)}, bf16[128,1024]{1,0:T(8,128)(2,1)S(1)}, u32[]{:S(2)}, u32[]{:S(2)}) collective-permute-start(bf16[128,1024]{1,0:T(8,128)(2,1)S(1)} %collective-permute-done.7.refs_6_), channel_id=1, source_target_pairs={{0,1},{2,0},{4,2},{6,4},{7,6},{5,7},{3,5},{1,3},{8,9},{10,8},{12,1... | collective-permute-start | bytes 786440 | tf_op jit(solution)/shard_map/ppermute | solution.py:164
  94.0 8.4 %collective-permute-start.12 = (bf16[128,1024]{1,0:T(8,128)(2,1)S(1)}, bf16[128,1024]{1,0:T(8,128)(2,1)S(1)}, u32[]{:S(2)}, u32[]{:S(2)}) collective-permute-start(bf16[128,1024]{1,0:T(8,128)(2,1)S(1)} %collective-permute-done.4.refs_3_), channel_id=1, source_target_pairs={{0,8},{8,0},{16,24},{24,16},{1,9},{9,1},{17,25},{25,17},{2,10},{10... | collective-permute-start | bytes 786440 | tf_op jit(solution)/shard_map/ppermute | solution.py:166
  94.0 8.3 %collective-permute-start.13 = (bf16[128,1024]{1,0:T(8,128)(2,1)S(1)}, bf16[128,1024]{1,0:T(8,128)(2,1)S(1)}, u32[]{:S(2)}, u32[]{:S(2)}) collective-permute-start(bf16[128,1024]{1,0:T(8,128)(2,1)S(1)} %collective-permute-done.5.refs_4_), channel_id=1, source_target_pairs={{0,8},{8,0},{16,24},{24,16},{1,9},{9,1},{17,25},{25,17},{2,10},{10... | collective-permute-start | bytes 786440 | tf_op jit(solution)/shard_map/ppermute | solution.py:166
  94.5 7.9 %collective-permute-start.15 = (bf16[128,1024]{1,0:T(8,128)(2,1)S(1)}, bf16[128,1024]{1,0:T(8,128)(2,1)S(1)}, u32[]{:S(2)}, u32[]{:S(2)}) collective-permute-start(bf16[128,1024]{1,0:T(8,128)(2,1)S(1)} %collective-permute-done.7.refs_6_), channel_id=1, source_target_pairs={{0,8},{8,0},{16,24},{24,16},{1,9},{9,1},{17,25},{25,17},{2,10},{10... | collective-permute-start | bytes 786440 | tf_op jit(solution)/shard_map/ppermute | solution.py:166
  99.5 2.9 %collective-permute-start.14 = (bf16[128,1024]{1,0:T(8,128)(2,1)S(1)}, bf16[128,1024]{1,0:T(8,128)(2,1)S(1)}, u32[]{:S(2)}, u32[]{:S(2)}) collective-permute-start(bf16[128,1024]{1,0:T(8,128)(2,1)S(1)} %collective-permute-done.6.refs_5_), channel_id=1, source_target_pairs={{0,8},{8,0},{16,24},{24,16},{1,9},{9,1},{17,25},{25,17},{2,10},{10... | collective-permute-start | bytes 786440 | tf_op jit(solution)/shard_map/ppermute | solution.py:166
  102.4 1.5 collective-permute-start.16
  106.5 11.2 %collective-permute-start.18 = (bf16[192,1024]{1,0:T(8,128)(2,1)S(1)}, bf16[192,1024]{1,0:T(8,128)(2,1)S(1)}, u32[]{:S(2)}, u32[]{:S(2)}) collective-permute-start(bf16[192,1024]{1,0:T(8,128)(2,1)S(1)} %get-tuple-element.20), channel_id=1, source_target_pairs={{0,16},{8,24},{16,0},{24,8},{1,17},{9,25},{17,1},{25,9},{2,18},{10... | collective-permute-start | bytes 1179656 | tf_op jit(solution)/shard_map/ppermute | solution.py:717
  108.2 15.5 %copy-start.13 = (f32[2048]{0:T(1024)S(1)}, f32[2048]{0:T(1024)}, u32[]{:S(2)}) copy-start(f32[2048]{0:T(1024)} %param.20) | copy-start | bytes 24580
  117.7 27.9 %copy-start.14 = (f32[1,1024]{1,0:T(1,128)S(1)}, f32[1,1024]{1,0:T(1,128)}, u32[]{:S(2)}) copy-start(f32[1,1024]{1,0:T(1,128)} %enc_bias_ref.1) | copy-start | bytes 12292
  119.0 26.6 %all-to-all-start = ((bf16[32,8,1536]{2,1,0:T(8,128)(2,1)}), bf16[32,8,1536]{2,1,0:T(8,128)(2,1)S(1)}, u32[]{:S(2)}, u32[]{:S(2)}) async-start(bf16[32,8,1536]{2,1,0:T(8,128)(2,1)} %bitcast.42), calls=%async_computation | async-start | bytes 1572864 | tf_op jit(solution)/shard_map/all_to_all | solution.py:710
  126.6 0.9 copy-start.5
  145.6 9.7 %copy-start.16 = (s32[1,192]{1,0:T(1,128)S(1)}, s32[1,192]{1,0:T(1,128)}, u32[]{:S(2)}) copy-start(s32[1,192]{1,0:T(1,128)} %param.22) | copy-start | bytes 2308
  152.2 3.2 %copy-start.1 = (bf16[256,3072]{1,0:T(8,128)(2,1)S(1)}, bf16[256,3072]{1,0:T(8,128)(2,1)}, u32[]{:S(2)}) copy-start(bf16[256,3072]{1,0:T(8,128)(2,1)} %get-tuple-element.28.built_ref) | copy-start | bytes 4718596
  152.2 41.6 %all-to-all-start.2 = ((bf16[32,8,3072]{2,1,0:T(8,128)(2,1)}), bf16[32,8,3072]{2,1,0:T(8,128)(2,1)S(1)}, u32[]{:S(2)}, u32[]{:S(2)}) async-start(bf16[32,8,3072]{2,1,0:T(8,128)(2,1)} %bitcast.33), calls=%async_computation.2 | async-start | bytes 3145728 | tf_op jit(solution)/shard_map/all_to_all | solution.py:710
  155.4 1.1 copy-start.2
  156.6 1.1 copy-start.3
  157.7 1.1 copy-start.4

commit v5 on v4

--- a/solution.py
+++ b/solution.py
@@ -440,23 +440,27 @@
     e_copies = row_tiles(enc_ref.at[0], e_scr, e_sems, model - cols)
     prev = pltpu.make_async_copy(prev_ref, p_scr, p_sem)
     prev.start()
-    cuts = slots.cuts
-    cut = model // cuts
+    tile = model // TILES
     d_copies = []
-    for t in range(cuts):
-        at = slice(t * cut, (t + 1) * cut)
+    for t in range(TILES):
+        at = slice(t * tile, (t + 1) * tile)
         d_copies.append(
             pltpu.make_async_copy(dec_ref.at[0, :, at], d_scr.at[:, at], d_sems.at[t])
         )
     kept = pltpu.make_async_copy(block_ref, kept_ref, kept_sem)
     x, live = centered_rows(slots, block_ref, bias_ref[:, model - cols :])
-    for copy in e_copies:
+    total = enc_bias_ref[...]
+    deep = cols // TILES
+    for t, copy in enumerate(e_copies):
         copy.wait()
-    for copy in d_copies:
-        copy.start()
+        if t == 0:
+            for later in d_copies:
+                later.start()
+        at = slice(t * deep, (t + 1) * deep)
+        total = total + dot(x[:, at], e_scr[at])
     kept.start()
     prev.wait()
-    total = dot(x, e_scr[...]) + p_scr[...].astype(f32) + enc_bias_ref[...]
+    total = total + p_scr[...].astype(f32)
     at = 0
     for a in live:
         rows = slice(at, at + a.shape[0])
@@ -475,20 +479,23 @@
         )
         sent[-1].start()
 
-    halves = []
-    for t in range(cuts):
-        at = slice(t * cut, (t + 1) * cut)
+    rest = []
+    for t in range(TILES):
+        at = slice(t * tile, (t + 1) * tile)
         d_copies[t].wait()
         out = dot(latent_scr[...], d_scr[:, at]) + bias_ref[:, at]
         for g in range(slots.full):
             here = slice(g * model + at.start, g * model + at.stop)
             pack_scr[:, here] = out[g * n : (g + 1) * n].astype(bf16)
             go(here)
-        halves.append(out[slots.full * n :])
+        rest.append(out[slots.full * n :])
     if slots.has_tail:
-        here = slice(slots.full * model, slots.full * model + cut)
-        pack_scr[:, here] = gather_tail(halves).astype(bf16)
-        go(here)
+        half = TILES // slots.cuts
+        for t in range(half):
+            at = slots.full * model + t * tile
+            here = slice(at, at + tile)
+            pack_scr[:, here] = gather_tail((rest[t], rest[half + t])).astype(bf16)
+            go(here)
     kept.wait()
     latent.wait()
     for one in sent:
@@ -500,7 +507,6 @@
     n = slots.lines
     out = (slots.rows, slots.width(model))
     one = pltpu.SemaphoreType.DMA
-    cuts = slots.cuts
     return call(
         functools.partial(middle_kernel, slots),
         [
@@ -519,9 +525,9 @@
             pltpu.VMEM((n, hidden), bf16),
             pltpu.VMEM(out, bf16),
             pltpu.SemaphoreType.DMA((TILES,)),
-            pltpu.SemaphoreType.DMA((cuts,)),
+            pltpu.SemaphoreType.DMA((TILES,)),
             one, one, one,
-            pltpu.SemaphoreType.DMA((slots.full * cuts + 1,)),
+            pltpu.SemaphoreType.DMA((slots.full * TILES + TILES,)),
         ],
     )(block, dec_bias, enc_bias, in_hbm(enc), in_hbm(prev), in_hbm(dec))
 
@@ -569,21 +575,22 @@
     came = pltpu.make_async_copy(rows_ref, rows_scr, rows_sem)
     came.start()
     model = rows_scr.shape[1]
-    cuts = slots.cuts
-    cut = model // cuts
+    tile = model // TILES
+    half = TILES // slots.cuts
     hot = [
         one_hot(keys_ref, i, slots.rows).astype(f32).astype(bf16)
         for i in range(keys_ref.shape[0])
     ]
     turn = lambda i, part: dot(hot[i], part, ((0,), (0,)))
     copies = []
-    for t in range(cuts):
-        at = slice(t * cut, (t + 1) * cut)
+    for t in range(TILES):
+        at = slice(t * tile, (t + 1) * tile)
         total = 0.0
         for g in range(slots.full):
             total = total + turn(g, block_ref[:, g * model + at.start : g * model + at.stop])
         if slots.has_tail:
-            total = total + turn(slots.full + t, block_ref[:, slots.full * model :])
+            here = slots.full * model + t % half * tile
+            total = total + turn(slots.full + t // half, block_ref[:, here : here + tile])
         recon = jnp.where(kept_ref[...] > 0, total, bias_ref[:, at]).astype(bf16)
         recon_scr[:, at] = recon
         if t == 0:
@@ -606,7 +613,7 @@
         6 * tokens * model + 2 * block.size,
         [VMEM] * 4 + [HBM],
         [HBM, HBM],
-        [scr, scr, scr, pltpu.SemaphoreType.DMA((slots.cuts, 2)), pltpu.SemaphoreType.DMA],
+        [scr, scr, scr, pltpu.SemaphoreType.DMA((TILES, 2)), pltpu.SemaphoreType.DMA],
     )(keys, kept, block, dec_bias, in_hbm(rows))
 
 

time: 197 us -> 197 us (level)
  no operation moved by 1% of the time
where the time goes in v5:
time: 197 us; the launch traced here: 196 us
  waiting for transfers between devices  106 us (54%)
  starting transfers between devices  41 us (21%)
  Pallas kernels  35.2 us (18%)
  local copies, waits for them, and re-layouts  9.82 us (5%)
  other arithmetic  2.32 us (1%)
    all_to_all x3, waiting for transfers between devices, to_all(): lax.all_to_all(block.reshape(devices, 8, block.shape[1]), ('seq', 'exp'),...  49.2 us
    ppermute x7, waiting for transfers between devices, ring_gather(): fw = lax.ppermute(fw, 'exp', ahead)  26.6 us
    ppermute x7, starting transfers between devices, ring_gather(): fw = lax.ppermute(fw, 'exp', ahead)  17.4 us
    ppermute x7, waiting for transfers between devices, ring_gather(): bw = lax.ppermute(bw, 'exp', back)  16.8 us
    all_to_all x3, starting transfers between devices, to_all(): lax.all_to_all(block.reshape(devices, 8, block.shape[1]), ('seq', 'exp'),...  14.2 us
    pallas_call x4, Pallas kernels, attend(): call(functools.partial(attention_kernel, heads, parts, group), jax.ShapeD...  9.81 us
    ppermute x2, waiting for transfers between devices, shards(): lax.ppermute(part, 'seq', over(chips - d))  9.8 us
    pallas_call x1, Pallas kernels, middle(): call(functools.partial(middle_kernel, slots), [pltpu.HBM((n, hidden), bf1...  5.91 us
  transfers between devices with their start and end apart: 38, of which 13 were waited for; matrix products, arithmetic and copies ran while one was open for 3% of the time, Pallas kernels for 14%

profile of v5, /device:TPU:0, one launch (start us, length us, event | category | flops | bytes accessed | tf_op | source)
XLA Modules:
  0.0 195.9 jit_solution(4259175278602032218)
XLA Ops:
  0.6 1.1 fusion.1
  1.7 3.1 %collective-permute-start.19 = (bf16[128,1024]{1,0:T(8,128)(2,1)S(1)}, bf16[128,1024]{1,0:T(8,128)(2,1)S(1)}, u32[]{:S(2)}, u32[]{:S(2)}) collective-permute-start(bf16[128,1024]{1,0:T(8,128)(2,1)S(1)} %get-tuple-element.36.refs_0_), channel_id=1, source_target_pairs={{0,2},{2,4},{4,6},{6,7},{7,5},{5,3},{3,1},{1,0},{8,10},{10,12},{12... | collective-permute-start | bytes 786440 | tf_op jit(solution)/shard_map/ppermute | solution.py:161
  4.8 1.1 dynamic-slice_bitcast_fusion.3
  5.9 5.2 %collective-permute-done.19.refs_1_ = bf16[128,1024]{1,0:T(8,128)(2,1)S(1)} collective-permute-done((bf16[128,1024]{1,0:T(8,128)(2,1)S(1)}, bf16[128,1024]{1,0:T(8,128)(2,1)S(1)}, u32[]{:S(2)}, u32[]{:S(2)}) %collective-permute-start.19) | collective-permute-done | bytes 262176 | tf_op jit(solution)/shard_map/ppermute | solution.py:161
  11.1 1.8 collective-permute-start.21
  12.9 1.6 collective-permute-start
  14.4 2.1 %dynamic-slice_bitcast_fusion = bf16[192,2048]{1,0:T(8,128)(2,1)} fusion(bf16[1,192,4096]{2,1,0:T(8,128)(2,1)} %param.12, s32[]{:T(128)S(6)} %select_n.93), kind=kLoop, calls=%fused_computation | loop fusion | bytes 1572868 | tf_op jit(solution)/shard_map/dynamic_slice | solution.py:657
  16.5 0.5 collective-permute-start.17
  17.1 2.4 %collective-permute-done = bf16[192,512]{1,0:T(8,128)(2,1)S(1)} collective-permute-done((bf16[192,512]{1,0:T(8,128)(2,1)S(1)}, bf16[192,512]{1,0:T(8,128)(2,1)S(1)}, u32[]{:S(2)}, u32[]{:S(2)}) %collective-permute-start) | collective-permute-done | bytes 196640 | tf_op jit(solution)/shard_map/ppermute | solution.py:663
  19.5 0.4 collective-permute-start.22
  19.9 1.7 collective-permute-start.23
  21.6 1.2 add_multiply_fusion.1
  23.0 5.4 %collective-permute-done.22.refs_4_ = bf16[128,1024]{1,0:T(8,128)(2,1)} collective-permute-done((bf16[128,1024]{1,0:T(8,128)(2,1)S(1)}, bf16[128,1024]{1,0:T(8,128)(2,1)}, u32[]{:S(2)}, u32[]{:S(2)}) %collective-permute-start.22) | collective-permute-done | bytes 262176 | tf_op jit(solution)/shard_map/ppermute | solution.py:164
  28.3 0.7 copy-done.10
  29.0 0.4 collective-permute-start.24
  29.4 1.7 collective-permute-start.25
  31.1 0.1 slice.9
  31.2 0.2 copy.22.drow_ref
  31.4 0.1 concatenate.20.scal
  31.5 0.8 pad_add_fusion.1.order
  32.3 0.2 convert_reduce_fusion
  32.6 0.5 collective-permute-start.30
  33.1 5.0 %collective-permute-done.24.refs_6_ = bf16[128,1024]{1,0:T(8,128)(2,1)} collective-permute-done((bf16[128,1024]{1,0:T(8,128)(2,1)}, bf16[128,1024]{1,0:T(8,128)(2,1)}, u32[]{:S(2)}, u32[]{:S(2)}) %collective-permute-start.24) | collective-permute-done | bytes 262176 | tf_op jit(solution)/shard_map/ppermute | solution.py:164
  38.1 0.5 collective-permute-start.32
  38.7 3.0 %shard_map.149.refs_16_ = bf16[192,1024]{1,0:T(8,128)(2,1)S(1)} custom-call(s32[6]{0:T(128)S(1)} %concatenate.25.scal, s32[12]{0:T(128)S(1)} %and_select_fusion.2.first, bf16[192,2048]{1,0:T(8,128)(2,1)S(1)} %collective-permute-done.17.q_ref, bf16[384,512]{1,0:T(8,128)(2,1)S(1)} %pad_maximum_fusion.mine_ref, ...), custom_call_target="tpu_custom_call" | custom-call | flops 301989888 | bytes 1572864 | tf_op jit(solution)/shard_map/pallas_call | solution.py:141
  41.8 3.0 %shard_map.150.refs_17_ = bf16[192,1024]{1,0:T(8,128)(2,1)S(1)} custom-call(s32[6]{0:T(128)S(1)} %concatenate.25.scal, s32[12]{0:T(128)S(1)} %and_select_fusion.2.first, bf16[192,2048]{1,0:T(8,128)(2,1)S(1)} %collective-permute-done.17.q_ref, bf16[384,512]{1,0:T(8,128)(2,1)S(1)} %pad_maximum_fusion.mine_ref, ...), custom_call_target="tpu_custom_call" | custom-call | flops 301989888 | bytes 1572864 | tf_op jit(solution)/shard_map/pallas_call | solution.py:141
  44.8 1.6 collective-permute-start.2
  46.5 0.4 collective-permute-start.3
  47.0 3.0 %shard_map.153 = (bf16[2048,1024]{1,0:T(8,128)(2,1)S(1)}, bf16[192,1024]{1,0:T(8,128)(2,1)S(1)}) custom-call(s32[16]{0:T(128)S(1)} %pad_add_fusion.1.order, bf16[128,1024]{1,0:T(8,128)(2,1)S(1)} %get-tuple-element.36.refs_0_, bf16[128,1024]{1,0:T(8,128)(2,1)S(1)} %collective-permute-done.19.refs_1_, bf16[128,1024]{1,0:T(8,128)(2,1)S(1)} %copy-done.7, ...), custom_call_target="tpu_custom_call" | custom-call | flops 805306368 | bytes 9175040 | tf_op jit(solution)/shard_map/pallas_call | solution.py:200
  50.1 3.7 %collective-permute-done.3.refs_2_ = bf16[128,1024]{1,0:T(8,128)(2,1)} collective-permute-done((bf16[128,1024]{1,0:T(8,128)(2,1)S(1)}, bf16[128,1024]{1,0:T(8,128)(2,1)}, u32[]{:S(2)}, u32[]{:S(2)}) %collective-permute-start.3) | collective-permute-done | bytes 262176 | tf_op jit(solution)/shard_map/ppermute | solution.py:164
  53.7 1.7 collective-permute-start.5
  55.4 2.0 shard_map.147.refs_0_
  57.4 1.8 shard_map.148.refs_1_
  59.1 1.0 shard_map.154.own_ref
  60.2 1.3 collective-permute-done.34.refs_0_
  61.4 1.3 shard_map.155
  62.7 6.4 %all-to-all-start.1 = ((bf16[32,8,1536]{2,1,0:T(8,128)(2,1)}), bf16[32,8,1536]{2,1,0:T(8,128)(2,1)S(1)}, u32[]{:S(2)}, u32[]{:S(2)}) async-start(bf16[32,8,1536]{2,1,0:T(8,128)(2,1)} %bitcast.41), calls=%async_computation.1 | async-start | bytes 1572864 | tf_op jit(solution)/shard_map/all_to_all | solution.py:717
  69.2 1.8 collective-permute-start.4
  71.0 0.3 collective-permute-start.7
  71.3 0.5 collective-permute-start.10
  71.8 16.5 %collective-permute-done.4.refs_3_ = bf16[128,1024]{1,0:T(8,128)(2,1)S(1)} collective-permute-done((bf16[128,1024]{1,0:T(8,128)(2,1)}, bf16[128,1024]{1,0:T(8,128)(2,1)S(1)}, u32[]{:S(2)}, u32[]{:S(2)}) %collective-permute-start.4) | collective-permute-done | bytes 262176 | tf_op jit(solution)/shard_map/ppermute | solution.py:161
  88.3 5.7 %collective-permute-start.6 = (bf16[128,1024]{1,0:T(8,128)(2,1)S(1)}, bf16[128,1024]{1,0:T(8,128)(2,1)S(1)}, u32[]{:S(2)}, u32[]{:S(2)}) collective-permute-start(bf16[128,1024]{1,0:T(8,128)(2,1)S(1)} %collective-permute-done.4.refs_3_), channel_id=1, source_target_pairs={{0,2},{2,4},{4,6},{6,7},{7,5},{5,3},{3,1},{1,0},{8,10},{10,12},{12... | collective-permute-start | bytes 786440 | tf_op jit(solution)/shard_map/ppermute | solution.py:161
  94.0 0.5 collective-permute-start.13
  94.6 4.9 %collective-permute-done.6.refs_5_ = bf16[128,1024]{1,0:T(8,128)(2,1)S(1)} collective-permute-done((bf16[128,1024]{1,0:T(8,128)(2,1)S(1)}, bf16[128,1024]{1,0:T(8,128)(2,1)S(1)}, u32[]{:S(2)}, u32[]{:S(2)}) %collective-permute-start.6) | collective-permute-done | bytes 262176 | tf_op jit(solution)/shard_map/ppermute | solution.py:161
  99.5 2.8 %collective-permute-done.8.refs_7_ = bf16[128,1024]{1,0:T(8,128)(2,1)S(1)} collective-permute-done((bf16[128,1024]{1,0:T(8,128)(2,1)S(1)}, bf16[128,1024]{1,0:T(8,128)(2,1)S(1)}, u32[]{:S(2)}, u32[]{:S(2)}) %collective-permute-start.8) | collective-permute-done | bytes 262176 | tf_op jit(solution)/shard_map/ppermute | solution.py:164
  102.4 1.5 collective-permute-done.16.refs_15_
  103.9 2.6 %shard_map.151 = (bf16[2048,1024]{1,0:T(8,128)(2,1)S(1)}, bf16[192,1024]{1,0:T(8,128)(2,1)S(1)}) custom-call(s32[16]{0:T(128)S(1)} %pad_add_fusion.1.order, bf16[128,1024]{1,0:T(8,128)(2,1)S(1)} %get-tuple-element.37.refs_0_, bf16[128,1024]{1,0:T(8,128)(2,1)} %collective-permute-done.2.refs_1_, bf16[128,1024]{1,0:T(8,128)(2,1)} %collective-permute-done.3.refs_2_, ...), custom_call_target="tpu_custom_call" | custom-call | flops 805306368 | bytes 9175040 | tf_op jit(solution)/shard_map/pallas_call | solution.py:200
  106.5 1.7 collective-permute-start.18
  108.2 1.0 shard_map.152.own_ref
  109.2 8.5 %collective-permute-done.18.refs_0_ = bf16[192,1024]{1,0:T(8,128)(2,1)S(1)} collective-permute-done((bf16[192,1024]{1,0:T(8,128)(2,1)S(1)}, bf16[192,1024]{1,0:T(8,128)(2,1)S(1)}, u32[]{:S(2)}, u32[]{:S(2)}) %collective-permute-start.18) | collective-permute-done | bytes 393248 | tf_op jit(solution)/shard_map/ppermute | solution.py:724
  117.7 1.3 shard_map.156
  119.0 4.7 %all-to-all-start = ((bf16[32,8,1536]{2,1,0:T(8,128)(2,1)}), bf16[32,8,1536]{2,1,0:T(8,128)(2,1)S(1)}, u32[]{:S(2)}, u32[]{:S(2)}) async-start(bf16[32,8,1536]{2,1,0:T(8,128)(2,1)} %bitcast.42), calls=%async_computation | async-start | bytes 1572864 | tf_op jit(solution)/shard_map/all_to_all | solution.py:717
  123.8 2.8 %shard_map.157 = (bf16[384,1024]{1,0:T(8,128)(2,1)S(1)}, bf16[256,1536]{1,0:T(8,128)(2,1)}) custom-call(bf16[256,1536]{1,0:T(8,128)(2,1)S(1)} %bitcast.34, f32[1,2048]{1,0:T(1,128)S(1)} %bitcast.37, bf16[1,2048,1024]{2,1,0:T(8,128)(2,1)} %enc_ref.1), custom_call_target="tpu_custom_call" | custom-call | flops 805306368 | bytes 4456448 | tf_op jit(solution)/shard_map/pallas_call | solution.py:418
  126.6 0.9 copy-done.5
  127.5 18.1 %all-to-all-done = bf16[32,8,1536]{2,1,0:T(8,128)(2,1)S(1)} async-done(((bf16[32,8,1536]{2,1,0:T(8,128)(2,1)}), bf16[32,8,1536]{2,1,0:T(8,128)(2,1)S(1)}, u32[]{:S(2)}, u32[]{:S(2)}) %all-to-all-start) | async-done | bytes 786464 | tf_op jit(solution)/shard_map/all_to_all | solution.py:717
  145.6 5.9 %shard_map.158 = (bf16[384,1024]{1,0:T(8,128)(2,1)}, bf16[256,3072]{1,0:T(8,128)(2,1)}, bf16[256,1536]{1,0:T(8,128)(2,1)}) custom-call(bf16[256,1536]{1,0:T(8,128)(2,1)S(1)} %bitcast.35, f32[1,2048]{1,0:T(1,128)S(1)} %bitcast.38, f32[1,1024]{1,0:T(1,128)S(1)} %copy-done.14, bf16[1,2048,1024]{2,1,0:T(8,128)(2,1)} %enc_ref.1, bf16[384,1024]{1,0:T(8,128)(2,1)} %copy-done.5, ...), custom_call_target="tpu_custom_call" | custom-call | flops 2415919104 | bytes 11010048 | tf_op jit(solution)/shard_map/pallas_call | solution.py:510
  151.5 3.1 %all-to-all-start.2 = ((bf16[32,8,3072]{2,1,0:T(8,128)(2,1)}), bf16[32,8,3072]{2,1,0:T(8,128)(2,1)S(1)}, u32[]{:S(2)}, u32[]{:S(2)}) async-start(bf16[32,8,3072]{2,1,0:T(8,128)(2,1)} %bitcast.33), calls=%async_computation.2 | async-start | bytes 3145728 | tf_op jit(solution)/shard_map/all_to_all | solution.py:717
  154.6 0.1 copy.26.kept_ref
  154.8 1.1 copy-done.2
  155.9 1.1 copy-done.3
  157.0 1.1 copy-done.4
  158.2 4.0 %shard_map.160 = bf16[1,1024,2048]{2,1,0:T(8,128)(2,1)} custom-call(bf16[384,1024]{1,0:T(8,128)(2,1)S(1)} %copy-done.3, bf16[256,3072]{1,0:T(8,128)(2,1)S(1)} %copy-done.1, bf16[256,1536]{1,0:T(8,128)(2,1)S(1)} %copy-done.2, bf16[256,1536]{1,0:T(8,128)(2,1)S(1)} %copy-done.4), custom_call_target="tpu_custom_call" | custom-call | flops 1610612736 | bytes 6553600 | tf_op jit(solution)/shard_map/pallas_call | solution.py:560
  162.1 31.1 %all-to-all-done.2 = bf16[32,8,3072]{2,1,0:T(8,128)(2,1)S(1)} async-done(((bf16[32,8,3072]{2,1,0:T(8,128)(2,1)}), bf16[32,8,3072]{2,1,0:T(8,128)(2,1)S(1)}, u32[]{:S(2)}, u32[]{:S(2)}) %all-to-all-start.2) | async-done | bytes 1572896 | tf_op jit(solution)/shard_map/all_to_all | solution.py:717
  193.2 2.6 %shard_map.159 = (bf16[192,2048]{1,0:T(8,128)(2,1)}, bf16[192,2048]{1,0:T(8,128)(2,1)}) custom-call(s32[3,192]{1,0:T(4,128)S(1)} %pad_add_fusion.keys_ref, s32[192,1]{1,0:T(8,128)S(1)} %copy.26.kept_ref, bf16[256,3072]{1,0:T(8,128)(2,1)S(1)} %bitcast.32, f32[1,2048]{1,0:T(1,128)S(1)} %bitcast.39, bf16[192,2048]{1,0:T(8,128)(2,1)} %get-tuple-element.24.rows_ref), custom_call_target="tpu_custom_call" | custom-call | flops 402653184 | bytes 3932160 | tf_op jit(solution)/shard_map/pallas_call | solution.py:609
  (81 shorter events, 0.8 us)
Async XLA Ops:
  0.6 30.4 %copy-start.12 = (s32[1,768]{1,0:T(1,128)S(1)}, s32[1,768]{1,0:T(1,128)}, u32[]{:S(2)}) copy-start(s32[1,768]{1,0:T(1,128)} %dcol_ref.7) | copy-start | bytes 9220
  1.7 9.4 %collective-permute-start.19 = (bf16[128,1024]{1,0:T(8,128)(2,1)S(1)}, bf16[128,1024]{1,0:T(8,128)(2,1)S(1)}, u32[]{:S(2)}, u32[]{:S(2)}) collective-permute-start(bf16[128,1024]{1,0:T(8,128)(2,1)S(1)} %get-tuple-element.36.refs_0_), channel_id=1, source_target_pairs={{0,2},{2,4},{4,6},{6,7},{7,5},{5,3},{3,1},{1,0},{8,10},{10,12},{12... | collective-permute-start | bytes 786440 | tf_op jit(solution)/shard_map/ppermute | solution.py:161
  4.8 14.7 %collective-permute-start.20 = (bf16[128,1024]{1,0:T(8,128)(2,1)S(1)}, bf16[128,1024]{1,0:T(8,128)(2,1)S(1)}, u32[]{:S(2)}, u32[]{:S(2)}) collective-permute-start(bf16[128,1024]{1,0:T(8,128)(2,1)S(1)} %get-tuple-element.36.refs_0_), channel_id=1, source_target_pairs={{0,1},{2,0},{4,2},{6,4},{7,6},{5,7},{3,5},{1,3},{8,9},{10,8},{12,1... | collective-permute-start | bytes 786440 | tf_op jit(solution)/shard_map/ppermute | solution.py:164
  4.8 18.0 %collective-permute-start.26 = (bf16[128,1024]{1,0:T(8,128)(2,1)S(1)}, bf16[128,1024]{1,0:T(8,128)(2,1)S(1)}, u32[]{:S(2)}, u32[]{:S(2)}) collective-permute-start(bf16[128,1024]{1,0:T(8,128)(2,1)S(1)} %get-tuple-element.36.refs_0_), channel_id=1, source_target_pairs={{0,8},{8,0},{16,24},{24,16},{1,9},{9,1},{17,25},{25,17},{2,10},{10... | collective-permute-start | bytes 786440 | tf_op jit(solution)/shard_map/ppermute | solution.py:166
  11.1 8.8 %collective-permute-start.21 = (bf16[128,1024]{1,0:T(8,128)(2,1)S(1)}, bf16[128,1024]{1,0:T(8,128)(2,1)}, u32[]{:S(2)}, u32[]{:S(2)}) collective-permute-start(bf16[128,1024]{1,0:T(8,128)(2,1)S(1)} %collective-permute-done.19.refs_1_), channel_id=1, source_target_pairs={{0,2},{2,4},{4,6},{6,7},{7,5},{5,3},{3,1},{1,0},{8,10},{10,12},{12... | collective-permute-start | bytes 786440 | tf_op jit(solution)/shard_map/ppermute | solution.py:161
  12.9 6.6 %collective-permute-start = (bf16[192,512]{1,0:T(8,128)(2,1)S(1)}, bf16[192,512]{1,0:T(8,128)(2,1)S(1)}, u32[]{:S(2)}, u32[]{:S(2)}) collective-permute-start(bf16[192,512]{1,0:T(8,128)(2,1)S(1)} %pad_maximum_fusion.1), channel_id=1, source_target_pairs={{0,16},{8,24},{16,0},{24,8},{1,17},{9,25},{17,1},{25,9},{2,18},{10... | collective-permute-start | bytes 589832 | tf_op jit(solution)/shard_map/ppermute | solution.py:663
  16.5 21.5 %collective-permute-start.17 = (bf16[192,2048]{1,0:T(8,128)(2,1)}, bf16[192,2048]{1,0:T(8,128)(2,1)S(1)}, u32[]{:S(2)}, u32[]{:S(2)}) collective-permute-start(bf16[192,2048]{1,0:T(8,128)(2,1)} %dynamic-slice_bitcast_fusion), channel_id=1, source_target_pairs={{0,16},{8,24},{16,0},{24,8},{1,17},{9,25},{17,1},{25,9},{2,18},{10... | collective-permute-start | bytes 2359304 | tf_op jit(solution)/shard_map/ppermute | solution.py:664
  19.5 8.8 %collective-permute-start.27 = (bf16[128,1024]{1,0:T(8,128)(2,1)S(1)}, bf16[128,1024]{1,0:T(8,128)(2,1)S(1)}, u32[]{:S(2)}, u32[]{:S(2)}) collective-permute-start(bf16[128,1024]{1,0:T(8,128)(2,1)S(1)} %collective-permute-done.19.refs_1_), channel_id=1, source_target_pairs={{0,8},{8,0},{16,24},{24,16},{1,9},{9,1},{17,25},{25,17},{2,10},{10... | collective-permute-start | bytes 786440 | tf_op jit(solution)/shard_map/ppermute | solution.py:166
  19.5 19.2 %copy-start.6 = (bf16[128,1024]{1,0:T(8,128)(2,1)}, bf16[128,1024]{1,0:T(8,128)(2,1)S(1)}, u32[]{:S(2)}) copy-start(bf16[128,1024]{1,0:T(8,128)(2,1)S(1)} %collective-permute-done.20.refs_2_) | copy-start | bytes 786436
  19.5 8.8 %collective-permute-start.22 = (bf16[128,1024]{1,0:T(8,128)(2,1)S(1)}, bf16[128,1024]{1,0:T(8,128)(2,1)}, u32[]{:S(2)}, u32[]{:S(2)}) collective-permute-start(bf16[128,1024]{1,0:T(8,128)(2,1)S(1)} %collective-permute-done.20.refs_2_), channel_id=1, source_target_pairs={{0,1},{2,0},{4,2},{6,4},{7,6},{5,7},{3,5},{1,3},{8,9},{10,8},{12,1... | collective-permute-start | bytes 786440 | tf_op jit(solution)/shard_map/ppermute | solution.py:164
  19.9 9.5 %collective-permute-start.23 = (bf16[128,1024]{1,0:T(8,128)(2,1)}, bf16[128,1024]{1,0:T(8,128)(2,1)}, u32[]{:S(2)}, u32[]{:S(2)}) collective-permute-start(bf16[128,1024]{1,0:T(8,128)(2,1)} %collective-permute-done.21.refs_3_), channel_id=1, source_target_pairs={{0,2},{2,4},{4,6},{6,7},{7,5},{5,3},{3,1},{1,0},{8,10},{10,12},{12... | collective-permute-start | bytes 786440 | tf_op jit(solution)/shard_map/ppermute | solution.py:161
  22.9 15.8 %copy-start.8 = (bf16[128,1024]{1,0:T(8,128)(2,1)}, bf16[128,1024]{1,0:T(8,128)(2,1)S(1)}, u32[]{:S(2)}) copy-start(bf16[128,1024]{1,0:T(8,128)(2,1)S(1)} %collective-permute-done.26.refs_8_) | copy-start | bytes 786436
  22.9 9.7 %collective-permute-start.1 = (bf16[384,512]{1,0:T(8,128)(2,1)S(1)}, bf16[384,512]{1,0:T(8,128)(2,1)S(1)}, u32[]{:S(2)}, u32[]{:S(2)}) collective-permute-start(bf16[384,512]{1,0:T(8,128)(2,1)S(1)} %pad_maximum_fusion.mine_ref), channel_id=1, source_target_pairs={{0,8},{8,0},{16,24},{24,16},{1,9},{9,1},{17,25},{25,17},{2,10},{10... | collective-permute-start | bytes 1179656 | tf_op jit(solution)/shard_map/ppermute | solution.py:666
  28.3 4.2 %collective-permute-start.28 = (bf16[128,1024]{1,0:T(8,128)(2,1)S(1)}, bf16[128,1024]{1,0:T(8,128)(2,1)}, u32[]{:S(2)}, u32[]{:S(2)}) collective-permute-start(bf16[128,1024]{1,0:T(8,128)(2,1)S(1)} %collective-permute-done.20.refs_2_), channel_id=1, source_target_pairs={{0,8},{8,0},{16,24},{24,16},{1,9},{9,1},{17,25},{25,17},{2,10},{10... | collective-permute-start | bytes 786440 | tf_op jit(solution)/shard_map/ppermute | solution.py:166
  28.3 0.7 copy-start.10
  29.0 9.0 %collective-permute-start.24 = (bf16[128,1024]{1,0:T(8,128)(2,1)}, bf16[128,1024]{1,0:T(8,128)(2,1)}, u32[]{:S(2)}, u32[]{:S(2)}) collective-permute-start(bf16[128,1024]{1,0:T(8,128)(2,1)} %collective-permute-done.22.refs_4_), channel_id=1, source_target_pairs={{0,1},{2,0},{4,2},{6,4},{7,6},{5,7},{3,5},{1,3},{8,9},{10,8},{12,1... | collective-permute-start | bytes 786440 | tf_op jit(solution)/shard_map/ppermute | solution.py:164
  29.4 9.2 %collective-permute-start.25 = (bf16[128,1024]{1,0:T(8,128)(2,1)}, bf16[128,1024]{1,0:T(8,128)(2,1)}, u32[]{:S(2)}, u32[]{:S(2)}) collective-permute-start(bf16[128,1024]{1,0:T(8,128)(2,1)} %collective-permute-done.23.refs_5_), channel_id=1, source_target_pairs={{0,2},{2,4},{4,6},{6,7},{7,5},{5,3},{3,1},{1,0},{8,10},{10,12},{12... | collective-permute-start | bytes 786440 | tf_op jit(solution)/shard_map/ppermute | solution.py:161
  31.5 15.4 %copy-start.11 = (bf16[128,1024]{1,0:T(8,128)(2,1)S(1)}, bf16[128,1024]{1,0:T(8,128)(2,1)}, u32[]{:S(2)}) copy-start(bf16[128,1024]{1,0:T(8,128)(2,1)} %copy-done.10) | copy-start | bytes 786436
  32.5 12.3 %collective-permute-start.29 = (bf16[128,1024]{1,0:T(8,128)(2,1)}, bf16[128,1024]{1,0:T(8,128)(2,1)S(1)}, u32[]{:S(2)}, u32[]{:S(2)}) collective-permute-start(bf16[128,1024]{1,0:T(8,128)(2,1)} %collective-permute-done.21.refs_3_), channel_id=1, source_target_pairs={{0,8},{8,0},{16,24},{24,16},{1,9},{9,1},{17,25},{25,17},{2,10},{10... | collective-permute-start | bytes 786440 | tf_op jit(solution)/shard_map/ppermute | solution.py:166
  32.6 13.8 %collective-permute-start.30 = (bf16[128,1024]{1,0:T(8,128)(2,1)}, bf16[128,1024]{1,0:T(8,128)(2,1)S(1)}, u32[]{:S(2)}, u32[]{:S(2)}) collective-permute-start(bf16[128,1024]{1,0:T(8,128)(2,1)} %collective-permute-done.22.refs_4_), channel_id=1, source_target_pairs={{0,8},{8,0},{16,24},{24,16},{1,9},{9,1},{17,25},{25,17},{2,10},{10... | collective-permute-start | bytes 786440 | tf_op jit(solution)/shard_map/ppermute | solution.py:166
  38.1 8.9 %collective-permute-start.31 = (bf16[128,1024]{1,0:T(8,128)(2,1)}, bf16[128,1024]{1,0:T(8,128)(2,1)S(1)}, u32[]{:S(2)}, u32[]{:S(2)}) collective-permute-start(bf16[128,1024]{1,0:T(8,128)(2,1)} %collective-permute-done.23.refs_5_), channel_id=1, source_target_pairs={{0,8},{8,0},{16,24},{24,16},{1,9},{9,1},{17,25},{25,17},{2,10},{10... | collective-permute-start | bytes 786440 | tf_op jit(solution)/shard_map/ppermute | solution.py:166
  38.1 8.9 %collective-permute-start.32 = (bf16[128,1024]{1,0:T(8,128)(2,1)}, bf16[128,1024]{1,0:T(8,128)(2,1)S(1)}, u32[]{:S(2)}, u32[]{:S(2)}) collective-permute-start(bf16[128,1024]{1,0:T(8,128)(2,1)} %collective-permute-done.24.refs_6_), channel_id=1, source_target_pairs={{0,8},{8,0},{16,24},{24,16},{1,9},{9,1},{17,25},{25,17},{2,10},{10... | collective-permute-start | bytes 786440 | tf_op jit(solution)/shard_map/ppermute | solution.py:166
  38.6 8.3 %collective-permute-start.33 = (bf16[128,1024]{1,0:T(8,128)(2,1)}, bf16[128,1024]{1,0:T(8,128)(2,1)S(1)}, u32[]{:S(2)}, u32[]{:S(2)}) collective-permute-start(bf16[128,1024]{1,0:T(8,128)(2,1)} %collective-permute-done.25.refs_7_), channel_id=1, source_target_pairs={{0,8},{8,0},{16,24},{24,16},{1,9},{9,1},{17,25},{25,17},{2,10},{10... | collective-permute-start | bytes 786440 | tf_op jit(solution)/shard_map/ppermute | solution.py:166
  38.7 8.3 %copy-start.7 = (bf16[128,1024]{1,0:T(8,128)(2,1)S(1)}, bf16[128,1024]{1,0:T(8,128)(2,1)}, u32[]{:S(2)}) copy-start(bf16[128,1024]{1,0:T(8,128)(2,1)} %copy-done.6) | copy-start | bytes 786436
  38.7 8.3 %copy-start.9 = (bf16[128,1024]{1,0:T(8,128)(2,1)S(1)}, bf16[128,1024]{1,0:T(8,128)(2,1)}, u32[]{:S(2)}) copy-start(bf16[128,1024]{1,0:T(8,128)(2,1)} %copy-done.8) | copy-start | bytes 786436
  41.7 8.3 %copy-start.15 = (s32[1,192]{1,0:T(1,128)S(1)}, s32[1,192]{1,0:T(1,128)}, u32[]{:S(2)}) copy-start(s32[1,192]{1,0:T(1,128)} %param.22) | copy-start | bytes 2308
  41.8 8.3 %copy-start.17 = (s32[1,192]{1,0:T(1,128)S(1)}, s32[1,192]{1,0:T(1,128)}, u32[]{:S(2)}) copy-start(s32[1,192]{1,0:T(1,128)} %param.21) | copy-start | bytes 2308
  41.8 13.6 %copy-start = (bf16[1,192,4096]{2,1,0:T(8,128)(2,1)S(1)}, bf16[1,192,4096]{2,1,0:T(8,128)(2,1)}, u32[]{:S(2)}) copy-start(bf16[1,192,4096]{2,1,0:T(8,128)(2,1)} %param.12) | copy-start | bytes 4718596
  44.8 24.3 %collective-permute-start.2 = (bf16[128,1024]{1,0:T(8,128)(2,1)S(1)}, bf16[128,1024]{1,0:T(8,128)(2,1)}, u32[]{:S(2)}, u32[]{:S(2)}) collective-permute-start(bf16[128,1024]{1,0:T(8,128)(2,1)S(1)} %get-tuple-element.37.refs_0_), channel_id=1, source_target_pairs={{0,2},{2,4},{4,6},{6,7},{7,5},{5,3},{3,1},{1,0},{8,10},{10,12},{12... | collective-permute-start | bytes 786440 | tf_op jit(solution)/shard_map/ppermute | solution.py:161
  46.5 7.3 %collective-permute-start.3 = (bf16[128,1024]{1,0:T(8,128)(2,1)S(1)}, bf16[128,1024]{1,0:T(8,128)(2,1)}, u32[]{:S(2)}, u32[]{:S(2)}) collective-permute-start(bf16[128,1024]{1,0:T(8,128)(2,1)S(1)} %get-tuple-element.37.refs_0_), channel_id=1, source_target_pairs={{0,1},{2,0},{4,2},{6,4},{7,6},{5,7},{3,5},{1,3},{8,9},{10,8},{12,1... | collective-permute-start | bytes 786440 | tf_op jit(solution)/shard_map/ppermute | solution.py:164
  49.9 11.5 %collective-permute-start.34 = (bf16[192,1024]{1,0:T(8,128)(2,1)S(1)}, bf16[192,1024]{1,0:T(8,128)(2,1)S(1)}, u32[]{:S(2)}, u32[]{:S(2)}) collective-permute-start(bf16[192,1024]{1,0:T(8,128)(2,1)S(1)} %get-tuple-element.22), channel_id=1, source_target_pairs={{0,16},{8,24},{16,0},{24,8},{1,17},{9,25},{17,1},{25,9},{2,18},{10... | collective-permute-start | bytes 1179656 | tf_op jit(solution)/shard_map/ppermute | solution.py:724
  53.7 17.3 %collective-permute-start.5 = (bf16[128,1024]{1,0:T(8,128)(2,1)}, bf16[128,1024]{1,0:T(8,128)(2,1)S(1)}, u32[]{:S(2)}, u32[]{:S(2)}) collective-permute-start(bf16[128,1024]{1,0:T(8,128)(2,1)} %collective-permute-done.3.refs_2_), channel_id=1, source_target_pairs={{0,1},{2,0},{4,2},{6,4},{7,6},{5,7},{3,5},{1,3},{8,9},{10,8},{12,1... | collective-permute-start | bytes 786440 | tf_op jit(solution)/shard_map/ppermute | solution.py:164
  62.7 56.3 %all-to-all-start.1 = ((bf16[32,8,1536]{2,1,0:T(8,128)(2,1)}), bf16[32,8,1536]{2,1,0:T(8,128)(2,1)S(1)}, u32[]{:S(2)}, u32[]{:S(2)}) async-start(bf16[32,8,1536]{2,1,0:T(8,128)(2,1)} %bitcast.41), calls=%async_computation.1 | async-start | bytes 1572864 | tf_op jit(solution)/shard_map/all_to_all | solution.py:717
  69.2 19.1 %collective-permute-start.4 = (bf16[128,1024]{1,0:T(8,128)(2,1)}, bf16[128,1024]{1,0:T(8,128)(2,1)S(1)}, u32[]{:S(2)}, u32[]{:S(2)}) collective-permute-start(bf16[128,1024]{1,0:T(8,128)(2,1)} %collective-permute-done.2.refs_1_), channel_id=1, source_target_pairs={{0,2},{2,4},{4,6},{6,7},{7,5},{5,3},{3,1},{1,0},{8,10},{10,12},{12... | collective-permute-start | bytes 786440 | tf_op jit(solution)/shard_map/ppermute | solution.py:161
  71.0 22.9 %collective-permute-start.7 = (bf16[128,1024]{1,0:T(8,128)(2,1)S(1)}, bf16[128,1024]{1,0:T(8,128)(2,1)S(1)}, u32[]{:S(2)}, u32[]{:S(2)}) collective-permute-start(bf16[128,1024]{1,0:T(8,128)(2,1)S(1)} %collective-permute-done.5.refs_4_), channel_id=1, source_target_pairs={{0,1},{2,0},{4,2},{6,4},{7,6},{5,7},{3,5},{1,3},{8,9},{10,8},{12,1... | collective-permute-start | bytes 786440 | tf_op jit(solution)/shard_map/ppermute | solution.py:164
  71.3 22.7 %collective-permute-start.9 = (bf16[128,1024]{1,0:T(8,128)(2,1)S(1)}, bf16[128,1024]{1,0:T(8,128)(2,1)S(1)}, u32[]{:S(2)}, u32[]{:S(2)}) collective-permute-start(bf16[128,1024]{1,0:T(8,128)(2,1)S(1)} %get-tuple-element.37.refs_0_), channel_id=1, source_target_pairs={{0,8},{8,0},{16,24},{24,16},{1,9},{9,1},{17,25},{25,17},{2,10},{10... | collective-permute-start | bytes 786440 | tf_op jit(solution)/shard_map/ppermute | solution.py:166
  71.3 22.8 %collective-permute-start.10 = (bf16[128,1024]{1,0:T(8,128)(2,1)}, bf16[128,1024]{1,0:T(8,128)(2,1)S(1)}, u32[]{:S(2)}, u32[]{:S(2)}) collective-permute-start(bf16[128,1024]{1,0:T(8,128)(2,1)} %collective-permute-done.2.refs_1_), channel_id=1, source_target_pairs={{0,8},{8,0},{16,24},{24,16},{1,9},{9,1},{17,25},{25,17},{2,10},{10... | collective-permute-start | bytes 786440 | tf_op jit(solution)/shard_map/ppermute | solution.py:166
  71.8 22.8 %collective-permute-start.11 = (bf16[128,1024]{1,0:T(8,128)(2,1)}, bf16[128,1024]{1,0:T(8,128)(2,1)S(1)}, u32[]{:S(2)}, u32[]{:S(2)}) collective-permute-start(bf16[128,1024]{1,0:T(8,128)(2,1)} %collective-permute-done.3.refs_2_), channel_id=1, source_target_pairs={{0,8},{8,0},{16,24},{24,16},{1,9},{9,1},{17,25},{25,17},{2,10},{10... | collective-permute-start | bytes 786440 | tf_op jit(solution)/shard_map/ppermute | solution.py:166
  88.3 11.3 %collective-permute-start.6 = (bf16[128,1024]{1,0:T(8,128)(2,1)S(1)}, bf16[128,1024]{1,0:T(8,128)(2,1)S(1)}, u32[]{:S(2)}, u32[]{:S(2)}) collective-permute-start(bf16[128,1024]{1,0:T(8,128)(2,1)S(1)} %collective-permute-done.4.refs_3_), channel_id=1, source_target_pairs={{0,2},{2,4},{4,6},{6,7},{7,5},{5,3},{3,1},{1,0},{8,10},{10,12},{12... | collective-permute-start | bytes 786440 | tf_op jit(solution)/shard_map/ppermute | solution.py:161
  94.0 8.4 %collective-permute-start.8 = (bf16[128,1024]{1,0:T(8,128)(2,1)S(1)}, bf16[128,1024]{1,0:T(8,128)(2,1)S(1)}, u32[]{:S(2)}, u32[]{:S(2)}) collective-permute-start(bf16[128,1024]{1,0:T(8,128)(2,1)S(1)} %collective-permute-done.7.refs_6_), channel_id=1, source_target_pairs={{0,1},{2,0},{4,2},{6,4},{7,6},{5,7},{3,5},{1,3},{8,9},{10,8},{12,1... | collective-permute-start | bytes 786440 | tf_op jit(solution)/shard_map/ppermute | solution.py:164
  94.0 8.4 %collective-permute-start.12 = (bf16[128,1024]{1,0:T(8,128)(2,1)S(1)}, bf16[128,1024]{1,0:T(8,128)(2,1)S(1)}, u32[]{:S(2)}, u32[]{:S(2)}) collective-permute-start(bf16[128,1024]{1,0:T(8,128)(2,1)S(1)} %collective-permute-done.4.refs_3_), channel_id=1, source_target_pairs={{0,8},{8,0},{16,24},{24,16},{1,9},{9,1},{17,25},{25,17},{2,10},{10... | collective-permute-start | bytes 786440 | tf_op jit(solution)/shard_map/ppermute | solution.py:166
  94.0 8.3 %collective-permute-start.13 = (bf16[128,1024]{1,0:T(8,128)(2,1)S(1)}, bf16[128,1024]{1,0:T(8,128)(2,1)S(1)}, u32[]{:S(2)}, u32[]{:S(2)}) collective-permute-start(bf16[128,1024]{1,0:T(8,128)(2,1)S(1)} %collective-permute-done.5.refs_4_), channel_id=1, source_target_pairs={{0,8},{8,0},{16,24},{24,16},{1,9},{9,1},{17,25},{25,17},{2,10},{10... | collective-permute-start | bytes 786440 | tf_op jit(solution)/shard_map/ppermute | solution.py:166
  94.5 7.9 %collective-permute-start.15 = (bf16[128,1024]{1,0:T(8,128)(2,1)S(1)}, bf16[128,1024]{1,0:T(8,128)(2,1)S(1)}, u32[]{:S(2)}, u32[]{:S(2)}) collective-permute-start(bf16[128,1024]{1,0:T(8,128)(2,1)S(1)} %collective-permute-done.7.refs_6_), channel_id=1, source_target_pairs={{0,8},{8,0},{16,24},{24,16},{1,9},{9,1},{17,25},{25,17},{2,10},{10... | collective-permute-start | bytes 786440 | tf_op jit(solution)/shard_map/ppermute | solution.py:166
  99.5 2.9 %collective-permute-start.14 = (bf16[128,1024]{1,0:T(8,128)(2,1)S(1)}, bf16[128,1024]{1,0:T(8,128)(2,1)S(1)}, u32[]{:S(2)}, u32[]{:S(2)}) collective-permute-start(bf16[128,1024]{1,0:T(8,128)(2,1)S(1)} %collective-permute-done.6.refs_5_), channel_id=1, source_target_pairs={{0,8},{8,0},{16,24},{24,16},{1,9},{9,1},{17,25},{25,17},{2,10},{10... | collective-permute-start | bytes 786440 | tf_op jit(solution)/shard_map/ppermute | solution.py:166
  102.4 1.5 collective-permute-start.16
  106.5 11.2 %collective-permute-start.18 = (bf16[192,1024]{1,0:T(8,128)(2,1)S(1)}, bf16[192,1024]{1,0:T(8,128)(2,1)S(1)}, u32[]{:S(2)}, u32[]{:S(2)}) collective-permute-start(bf16[192,1024]{1,0:T(8,128)(2,1)S(1)} %get-tuple-element.20), channel_id=1, source_target_pairs={{0,16},{8,24},{16,0},{24,8},{1,17},{9,25},{17,1},{25,9},{2,18},{10... | collective-permute-start | bytes 1179656 | tf_op jit(solution)/shard_map/ppermute | solution.py:724
  108.2 15.5 %copy-start.13 = (f32[2048]{0:T(1024)S(1)}, f32[2048]{0:T(1024)}, u32[]{:S(2)}) copy-start(f32[2048]{0:T(1024)} %param.20) | copy-start | bytes 24580
  117.7 27.9 %copy-start.14 = (f32[1,1024]{1,0:T(1,128)S(1)}, f32[1,1024]{1,0:T(1,128)}, u32[]{:S(2)}) copy-start(f32[1,1024]{1,0:T(1,128)} %enc_bias_ref.1) | copy-start | bytes 12292
  119.0 26.6 %all-to-all-start = ((bf16[32,8,1536]{2,1,0:T(8,128)(2,1)}), bf16[32,8,1536]{2,1,0:T(8,128)(2,1)S(1)}, u32[]{:S(2)}, u32[]{:S(2)}) async-start(bf16[32,8,1536]{2,1,0:T(8,128)(2,1)} %bitcast.42), calls=%async_computation | async-start | bytes 1572864 | tf_op jit(solution)/shard_map/all_to_all | solution.py:717
  126.6 0.9 copy-start.5
  145.6 9.0 %copy-start.16 = (s32[1,192]{1,0:T(1,128)S(1)}, s32[1,192]{1,0:T(1,128)}, u32[]{:S(2)}) copy-start(s32[1,192]{1,0:T(1,128)} %param.22) | copy-start | bytes 2308
  151.5 3.2 %copy-start.1 = (bf16[256,3072]{1,0:T(8,128)(2,1)S(1)}, bf16[256,3072]{1,0:T(8,128)(2,1)}, u32[]{:S(2)}) copy-start(bf16[256,3072]{1,0:T(8,128)(2,1)} %get-tuple-element.28.built_ref) | copy-start | bytes 4718596
  151.5 41.6 %all-to-all-start.2 = ((bf16[32,8,3072]{2,1,0:T(8,128)(2,1)}), bf16[32,8,3072]{2,1,0:T(8,128)(2,1)S(1)}, u32[]{:S(2)}, u32[]{:S(2)}) async-start(bf16[32,8,3072]{2,1,0:T(8,128)(2,1)} %bitcast.33), calls=%async_computation.2 | async-start | bytes 3145728 | tf_op jit(solution)/shard_map/all_to_all | solution.py:717
  154.8 1.1 copy-start.2
  155.9 1.1 copy-start.3
  157.0 1.1 copy-start.4
